TPU v7x, 32 devices: a whole 2x2x4 slice. The times are simulated.
32 devices in a mesh: groups: 2 (over y), space: 4 (over z), dp: 2 (over x), rep: 2 (over core).
Axes of the slice: x: 2, y: 2, z: 4, core: 2. Of those that a mesh axis runs over, the one named last changes fastest.
Arguments:
- volumes: bfloat16 [8, 16, 24, 24, 128], P(('groups', 'dp', 'rep'), 'space'), parts along dimension 0, may hold values from -6 to 6
- targets: float32 [8, 4], P(('groups', 'dp', 'rep')), parts along dimension 0, may hold values from -4 to 4
- first_kernel: bfloat16 [3456, 128], replicated, may hold values from -0.109375 to 0.109375
- second_kernel: bfloat16 [3456, 256], P(None, 'space'), may hold values from -0.109375 to 0.109375
- head_weights: float32 [256, 4], replicated, may hold values from -0.375 to 0.375
Outputs:
- grad_first: float32 [6912, 128], P('groups'), parts along dimension 0
- grad_second: float32 [6912, 256], P('groups', 'space'), parts along dimension 0
- grad_head: float32 [512, 4], P(('groups', 'space')), parts along dimension 0
There are 2 independent parts, one for each index of `groups`. A program takes and returns all parts, laid end to end along the dimension named above; an argument that names none is the same for every part. Nothing has to cross between parts.
All inputs are finite; a program needn't handle non-finite values.
Results may differ from a plain program's by a relative error of at most 0.0038.
Values may be sent and summed in bfloat16 or wider, within the bound.
No kernel may reach another device: no remote copies, remote signals or barrier semaphores. Data moves between devices by JAX's collectives and lax.ppermute only.
A program may use at most 128 MiB of HBM per device.

v0:
```python
import jax
import jax.numpy as jnp
from jax import lax
from jax.experimental import pallas as pl
from jax.experimental.pallas import tpu as pltpu
from jax.sharding import PartitionSpec as P

leak_slope = 0.3
log_two = 0.6931471805599453
direct_most = 4
f32, bf16 = jnp.float32, jnp.bfloat16
front = 8
heavy = 10**9


def call(body, outs, scratch, *args, smem=(), work=0):
    specs = [pl.BlockSpec(memory_space=pltpu.SMEM if k in smem else pltpu.VMEM) for k in range(len(args))]
    return pl.pallas_call(
        body,
        out_shape=outs,
        in_specs=specs,
        out_specs=jax.tree.map(lambda o: pl.BlockSpec(memory_space=pltpu.VMEM), outs),
        scratch_shapes=scratch,
        compiler_params=pltpu.CompilerParams(vmem_limit_bytes=56 * 2**20),
        cost_estimate=pl.CostEstimate(flops=work, bytes_accessed=0, transcendentals=0),
    )(*args)


def slope_and_activation(value):
    shrunk = jnp.exp(-jnp.abs(value))
    inverse = 1.0 / (1.0 + shrunk)
    slope = leak_slope + (1.0 - leak_slope) * jnp.where(value >= 0, inverse, shrunk * inverse)
    soft = jnp.maximum(value, 0.0) + jnp.log(1.0 + shrunk)
    return slope, leak_slope * value + (1.0 - leak_slope) * (soft - log_two)


def shifted(rows_ref, length, step):
    return rows_ref[front + step : front + step + length, :]


def lay_plane(plane, rows_ref, wide):
    rows, cols, chans = plane.shape
    for h in range(rows):
        rows_ref[front + h * wide : front + h * wide + cols, :] = plane[h].astype(f32)


def wide_plane(source, rows_ref, target, top, wide):
    rows, chans = source.shape[0], source.shape[2]
    lay_plane(source, rows_ref, wide)
    for e in range(3):
        target[top : top + rows * wide, e * chans : (e + 1) * chans] = shifted(
            rows_ref, rows * wide, e - 1
        ).astype(bf16)


def first_forward(vol, before, after, kernel, pooled, slope, u, rows_ref, pairs, acc, half, dense):
    depth, rows, cols, chans = vol.shape
    wide = 32
    cells = rows * wide
    outs = kernel.shape[1]
    span = 3 * chans
    rows_ref[...] = jnp.zeros_like(rows_ref)
    edge = jnp.zeros((u.shape[0], wide, span), bf16)
    u[:, 0:wide, :] = edge
    u[:, wide + cells :, :] = edge
    for p in range(depth + 2):
        if p == 0:
            source = before[0]
        elif p == depth + 1:
            source = after[0]
        else:
            source = vol[p - 1]
        wide_plane(source, rows_ref, u.at[p], wide, wide)

    def tap(a, b):
        return kernel[(9 * a + 3 * b) * chans : (9 * a + 3 * b) * chans + span, :]

    for b in range(3):
        pairs[b, 0:span, 0:outs] = tap(1, b)
        pairs[b, 0:span, outs:] = tap(0, b)
        pairs[b, span:, 0:outs] = tap(2, b)
        pairs[b, span:, outs:] = tap(1, b)
    first_taps = jnp.concatenate([tap(0, b) for b in range(3)], axis=0)
    last_taps = jnp.concatenate([tap(2, b) for b in range(3)], axis=0)

    def one_pair(t, carry):
        def window(q, b):
            return u[2 * t + q, b * wide : b * wide + cells, :]

        left = jnp.concatenate([window(0, b) for b in range(3)], axis=1)
        acc[:, 0:outs] = jnp.dot(left, first_taps, preferred_element_type=f32)
        right = jnp.concatenate([window(3, b) for b in range(3)], axis=1)
        acc[:, outs:] = jnp.dot(right, last_taps, preferred_element_type=f32)
        for b in range(3):
            both = jnp.concatenate([window(1, b), window(2, b)], axis=1)
            acc[...] += jnp.dot(both, pairs[b], preferred_element_type=f32)
        for h in range(rows // 2):
            part = acc[h * 2 * wide : (h + 1) * 2 * wide, :]
            slopes, values = slope_and_activation(part)
            slope[2 * t, h * 2 * wide : (h + 1) * 2 * wide, :] = slopes[:, 0:outs]
            slope[2 * t + 1, h * 2 * wide : (h + 1) * 2 * wide, :] = slopes[:, outs:]
            values = values[:, 0:outs] + values[:, outs:]
            half[h * wide : (h + 1) * wide, :] = values[0:wide] + values[wide:]
        for h in range(rows // 2):
            even = half[pl.ds(h * wide, cols // 2, stride=2), :]
            odd = half[pl.ds(h * wide + 1, cols // 2, stride=2), :]
            dense[t, h * (cols // 2) : (h + 1) * (cols // 2), :] = (even + odd) * 0.125
        return carry

    lax.fori_loop(0, depth // 2, one_pair, 0)
    pooled[...] = dense[...].astype(bf16)


def run_first_forward(vol, before, after, kernel):
    depth, rows, cols, chans = vol.shape
    wide, outs = 32, kernel.shape[1]
    cells = rows * wide
    return call(
        first_forward,
        (
            jax.ShapeDtypeStruct((depth // 2, rows * cols // 4, outs), bf16),
            jax.ShapeDtypeStruct((depth, cells, outs), f32),
        ),
        [
            pltpu.VMEM((depth + 2, cells + 2 * wide, 3 * chans), bf16),
            pltpu.VMEM((cells + 2 * front, chans), f32),
            pltpu.VMEM((3, 6 * chans, 2 * outs), bf16),
            pltpu.VMEM((cells, 2 * outs), f32),
            pltpu.VMEM((cells // 2, outs), f32),
            pltpu.VMEM((depth // 2, rows * cols // 4, outs), f32),
        ],
        vol, before, after, kernel, work=heavy * 8,
    )


def first_backward(vol, before, after, spread, slope, which, keep, send, u, rows_ref, g, acc, twice):
    depth, rows, cols, chans = vol.shape
    wide = 32
    cells = rows * wide
    outs = slope.shape[2]
    rows_ref[...] = jnp.zeros_like(rows_ref)
    for p in range(depth + 2):
        if p == 0:
            source = before[0]
        elif p == depth + 1:
            source = after[0]
        else:
            source = vol[p - 1]
        wide_plane(source, rows_ref, u.at[p], 0, wide)
    edge = jnp.zeros((depth, wide, outs), bf16)
    g[:, 0:wide, :] = edge
    g[:, wide + cells :, :] = edge
    for d in range(depth):
        if d % 2 == 0:
            values = spread[d // 2] * 0.125
            twice[pl.ds(0, cells // 4, stride=2), :] = values
            twice[pl.ds(1, cells // 4, stride=2), :] = values
        for h in range(rows):
            some = twice[(h // 2) * wide : (h // 2 + 1) * wide, :] * slope[d, h * wide : (h + 1) * wide, :]
            g[d, (h + 1) * wide : (h + 2) * wide, :] = some.astype(bf16)
    started = set()
    for p in range(depth + 2):
        taps = [a for a in range(3) if 0 <= p - a < depth]
        rhs = jnp.concatenate(
            [g[p - a, (2 - b) * wide : (2 - b) * wide + cells, :] for a in taps for b in range(3)], axis=1
        )
        part = lax.dot_general(u[p], rhs, (((0,), (0,)), ((), ())), preferred_element_type=f32)
        for place, a in enumerate(taps):
            block = part[:, place * 3 * outs : (place + 1) * 3 * outs]
            lanes = slice(a * 3 * outs, (a + 1) * 3 * outs)
            if a in started:
                acc[:, lanes] += block
            else:
                acc[:, lanes] = block
                started.add(a)
    pieces = keep.shape[0]
    size = chans // (2 * pieces)

    def write(first, second):
        for a in range(3):
            for b in range(3):
                for e in range(3):
                    t = 9 * a + 3 * b + e
                    lanes = slice((3 * a + b) * outs, (3 * a + b + 1) * outs)
                    for target, top in ((first, e * chans), (second, e * chans + chans // 2)):
                        block = acc[top : top + chans // 2, lanes]
                        target[:, t * size : (t + 1) * size, :] = block.reshape(pieces, size, outs)

    @pl.when(which[0] == 0)
    def _():
        write(keep, send)

    @pl.when(which[0] != 0)
    def _():
        write(send, keep)


def run_first_backward(vol, before, after, spread, slope, which, pieces):
    depth, rows, cols, chans = vol.shape
    wide, outs = 32, slope.shape[2]
    cells = rows * wide
    return call(
        first_backward,
        (jax.ShapeDtypeStruct((pieces // 2, 27 * chans // pieces, outs), f32),) * 2,
        [
            pltpu.VMEM((depth + 2, cells, 3 * chans), bf16),
            pltpu.VMEM((cells + 2 * front, chans), f32),
            pltpu.VMEM((depth, cells + 2 * wide, outs), bf16),
            pltpu.VMEM((3 * chans, 9 * outs), f32),
            pltpu.VMEM((cells // 2, outs), f32),
        ],
        vol, before, after, spread, slope, which, work=heavy * 7, smem=(5,),
    )


def lay_pooled(parts, places, flat, rows_ref, target, top, side, wide):
    chans = target.shape[2] // 3
    cells = side * wide
    for part, place in zip(parts, places):
        for d in range(part.shape[0]):
            flat[...] = part[d].astype(f32)
            for h in range(side):
                rows_ref[front + h * wide : front + h * wide + side, :] = flat[h * side : (h + 1) * side, :]
            for e in range(3):
                target[place + d, top : top + cells, e * chans : (e + 1) * chans] = shifted(
                    rows_ref, cells, e - 1
                ).astype(bf16)


def second_layer(
    where, p0, p1, p2, p3, w0, w1, w2, w3, w4, head, wanted,
    pooled_grad, own, result, p, flat, rows_ref, w, acc, slopes, shift_ref, g,
):
    parts, pieces = (p0, p1, p2, p3), (w1, w2, w3, w4)
    planes, area, chans = p0.shape
    side, wide = 12, 16
    cells = side * wide
    depth = planes * len(parts)
    outs = w.shape[0]
    rows_ref[...] = jnp.zeros_like(rows_ref)
    p[0] = jnp.zeros(p.shape[1:], bf16)
    p[depth + 1] = jnp.zeros(p.shape[1:], bf16)
    edge = jnp.zeros((depth + 2, wide, 3 * chans), bf16)
    p[:, 0:wide, :] = edge
    p[:, wide + cells :, :] = edge
    lay_pooled(parts, [1 + planes * where[k] for k in range(4)], flat, rows_ref, p, wide, side, wide)
    share = w0.shape[0]
    quarter = share // 4
    w[0:share, :] = w0[...]
    for k in range(1, 4):
        for j in range(4):
            at = pl.multiple_of(k * share + where[4 + j] * quarter, quarter)
            w[pl.ds(at, quarter), :] = pieces[j][(k - 1) * quarter : k * quarter, :]
    column = lax.broadcasted_iota(jnp.int32, (cells, outs), 0) % wide
    inside = column < side
    step = depth // 2
    slopes[0] = jnp.zeros((cells, outs), f32)
    slopes[depth + 1] = jnp.zeros((cells, outs), f32)

    def half(t, total):
        for a in range(3):
            lhs = jnp.concatenate(
                [
                    p[pl.ds(t * step + a, step), b * wide : b * wide + cells, :].reshape(step * cells, 3 * chans)
                    for b in range(3)
                ],
                axis=1,
            )
            part = lax.dot_general(
                lhs, w[:, 9 * a * chans : 9 * (a + 1) * chans], (((1,), (1,)), ((), ())), preferred_element_type=f32
            )
            if a == 0:
                acc[...] = part
            else:
                acc[...] += part
        for d in range(step):
            slope, value = slope_and_activation(acc[d * cells : (d + 1) * cells, :])
            slopes[t * step + d + 1] = jnp.where(inside, slope, 0.0)
            value = jnp.where(inside, value, 0.0)
            total = total + value.reshape(cells // 8, 8, outs).sum(axis=0)
        return total

    total = lax.fori_loop(0, 2, half, jnp.zeros((8, outs), f32))
    feature = total.sum(axis=0, keepdims=True) / float(depth * area)
    predicted = jnp.sum(feature * head[...], axis=1, keepdims=True)
    error = predicted - wanted[:, 0:1]
    result[...] = error * feature
    scale = jnp.sum(head[...] * error, axis=0, keepdims=True)
    for d in range(depth):
        own[d] = (slopes[d + 1, :, 0:share] * scale[:, 0:share]).astype(bf16)
    shift_ref[...] = jnp.zeros_like(shift_ref)
    rim = jnp.zeros((planes + 2, wide, outs), bf16)
    for e in range(3):
        g[e, :, 0:wide, :] = rim
        g[e, :, wide + cells :, :] = rim
    for k in range(planes + 2):
        shift_ref[front : front + cells, :] = (slopes[where[0] * planes + k] * scale).astype(bf16).astype(f32)
        for e in range(3):
            g[e, k, wide : wide + cells, :] = shifted(shift_ref, cells, 1 - e).astype(bf16)
    out = jnp.zeros((planes * cells, chans), f32)
    for a in range(3):
        for b in range(3):
            for e in range(3):
                lhs = g[e, 2 - a : 2 - a + planes, (2 - b) * wide : (2 - b) * wide + cells, :].reshape(planes * cells, outs)
                t = 9 * a + 3 * b + e
                out = out + jnp.dot(lhs, w[:, t * chans : (t + 1) * chans], preferred_element_type=f32)
    keep = lax.broadcasted_iota(jnp.int32, (planes * cells, chans), 0) % wide < side
    pooled_grad[...] = jnp.where(keep, out, 0.0).reshape(planes, cells, chans)


def run_second_layer(where, parts, part_kernel, pieces, head, wanted):
    planes, area, chans = parts[0].shape
    side, wide = 12, 16
    cells = side * wide
    depth = planes * 4
    share, taps = part_kernel.shape
    outs = 4 * share
    return call(
        second_layer,
        (
            jax.ShapeDtypeStruct((planes, cells, chans), f32),
            jax.ShapeDtypeStruct((depth, cells, share), bf16),
            jax.ShapeDtypeStruct((8, outs), f32),
        ),
        [
            pltpu.VMEM((depth + 2, cells + 2 * wide, 3 * chans), bf16),
            pltpu.VMEM((area, chans), f32),
            pltpu.VMEM((cells + 2 * front, chans), f32),
            pltpu.VMEM((outs, taps), bf16),
            pltpu.VMEM((depth // 2 * cells, outs), f32),
            pltpu.VMEM((depth + 2, cells, outs), f32),
            pltpu.VMEM((cells + 2 * front, outs), f32),
            pltpu.VMEM((3, planes + 2, cells + 2 * wide, outs), bf16),
        ],
        where, *parts, part_kernel, *pieces, head, wanted, smem=(0,), work=heavy * 8,
    )


def second_backward(where, p0, p1, p2, p3, own, result, grad, p, flat, rows_ref, g):
    parts = (p0, p1, p2, p3)
    planes, area, chans = p0.shape
    side, wide = 12, 16
    cells = side * wide
    depth = planes * len(parts)
    share = own.shape[2]
    rows_ref[...] = jnp.zeros_like(rows_ref)
    p[0] = jnp.zeros(p.shape[1:], bf16)
    p[depth + 1] = jnp.zeros(p.shape[1:], bf16)
    lay_pooled(parts, [1 + planes * where[k] for k in range(4)], flat, rows_ref, p, 0, side, wide)
    none = jnp.zeros((depth, wide, share), bf16)
    for b in range(3):
        lanes = slice(b * share, (b + 1) * share)
        if b == 0:
            g[:, 0 : cells - wide, lanes] = own[:, wide:cells, :]
            g[:, cells - wide :, lanes] = none
        elif b == 1:
            g[:, :, lanes] = own[...]
        else:
            g[:, wide:, lanes] = own[:, 0 : cells - wide, :]
            g[:, 0:wide, lanes] = none
    rhs = g[...].reshape(depth * cells, 3 * share)
    for a in range(3):
        lhs = p[a : a + depth].reshape(depth * cells, 3 * chans)
        part = lax.dot_general(rhs, lhs, (((0,), (0,)), ((), ())), preferred_element_type=f32)
        for b in range(3):
            for e in range(3):
                t = 9 * a + 3 * b + e
                block = part[b * share : (b + 1) * share, e * chans : (e + 1) * chans]
                grad[t * share : (t + 1) * share, :] = block
    grad[27 * share : 27 * share + 8, :] = result[:, 0:chans]
    grad[27 * share + 8 :, :] = jnp.zeros((8, chans), f32)


def run_second_backward(where, parts, own, result):
    planes, area, chans = parts[0].shape
    depth, cells, share = own.shape
    return call(
        second_backward,
        jax.ShapeDtypeStruct((27 * share + 16, chans), f32),
        [
            pltpu.VMEM((depth + 2, cells, 3 * chans), bf16),
            pltpu.VMEM((area, chans), f32),
            pltpu.VMEM((cells + 2 * front, chans), f32),
            pltpu.VMEM((depth, cells, 3 * share), bf16),
        ],
        where, *parts, own, result, smem=(0,), work=heavy * 4,
    )


def spread_first(blocks, out):
    pieces, rows, outs = blocks.shape
    size = 8
    for k in range(pieces):
        out[:, k * size : (k + 1) * size, :] = blocks[k].astype(f32).reshape(rows // size, size, outs)


def run_spread_first(blocks):
    pieces, rows, outs = blocks.shape
    steps, size = 9, rows // 27
    out = pl.pallas_call(
        spread_first,
        grid=(steps,),
        out_shape=jax.ShapeDtypeStruct((27, pieces * size, outs), f32),
        in_specs=[pl.BlockSpec((pieces, rows // steps, outs), lambda i: (0, i, 0))],
        out_specs=pl.BlockSpec((27 // steps, pieces * size, outs), lambda i: (i, 0, 0)),
    )(blocks)
    return out.reshape(-1, outs)


def spread_second(packed, out, head):
    chans = packed.shape[1]
    share = out.shape[0]
    for t in range(27):
        out[:, t * chans : (t + 1) * chans] = packed[t * share : (t + 1) * share, :]
    head[...] = packed[27 * share : 27 * share + 8, :]


def run_spread_second(packed, share):
    rows, chans = packed.shape
    return call(
        spread_second,
        (jax.ShapeDtypeStruct((share, 27 * chans), f32), jax.ShapeDtypeStruct((8, chans), f32)),
        [],
        packed,
    )


def turn(x, axis, step):
    size = lax.axis_size(axis)
    return lax.ppermute(x, axis, [(i, (i + step) % size) for i in range(size)])


def direct(axis):
    return lax.axis_size(axis) <= direct_most


def gathered(x, axis):
    if not direct(axis):
        return lax.all_gather(x, axis)
    size, place = lax.axis_size(axis), lax.axis_index(axis)
    parts = [x] + [turn(x, axis, step) for step in range(1, size)]
    out = jnp.zeros((size,) + x.shape, x.dtype)
    for step, part in enumerate(parts):
        out = lax.dynamic_update_index_in_dim(out, part, (place - step) % size, 0)
    return out


def scattered_sum(x, axis, wire):
    size, place = lax.axis_size(axis), lax.axis_index(axis)
    blocks = x.reshape((size, x.shape[0] // size) + x.shape[1:])
    if not direct(axis):
        return lax.psum_scatter(blocks, axis)
    total = lax.dynamic_index_in_dim(blocks, place, 0, False)
    for step in range(1, size):
        sent = lax.dynamic_index_in_dim(blocks, (place + step) % size, 0, False).astype(wire)
        total = total + turn(sent, axis, step).astype(jnp.float32)
    return total


def total_first(x):
    columns = x.shape[1]
    x = scattered_sum(x, "rep", jnp.float32)
    x = scattered_sum(x, "dp", jnp.bfloat16)
    if direct("space"):
        x = scattered_sum(x, "space", jnp.bfloat16).astype(jnp.bfloat16)
        x = gathered(x, "space").reshape(-1, columns)
    else:
        x = lax.psum(x, "space").astype(jnp.bfloat16)
    x = gathered(x, "dp").reshape(-1, columns)
    x = gathered(x, "rep").reshape(-1, columns)
    return x.astype(jnp.float32)


def total_second(x):
    columns = x.shape[1]
    x = scattered_sum(x, "rep", jnp.float32)
    if direct("dp"):
        x = gathered(x.astype(jnp.bfloat16), "dp").astype(jnp.float32).sum(0)
    else:
        x = lax.psum(x, "dp")
    return gathered(x, "rep").reshape(-1, columns)


def whole_kernel(part):
    rows, share = part.shape
    copies = [axis for axis in ("dp", "rep")]
    pieces, place = (1, 0)
    for axis in copies:
        place = place * lax.axis_size(axis) + lax.axis_index(axis)
        pieces = pieces * lax.axis_size(axis)
    length = rows // pieces
    piece = lax.dynamic_slice_in_dim(part, place * length, length, 0)
    packed = jnp.concatenate([piece[: length // 2], piece[length // 2 :]], axis=1)
    packs = gathered(packed, "space")
    upper = jnp.moveaxis(packs[:, :, :share], 0, 1).reshape(length // 2, -1)
    lower = jnp.moveaxis(packs[:, :, share:], 0, 1).reshape(length // 2, -1)
    wide = jnp.concatenate([upper, lower], axis=0)
    wide = gathered(wide, "dp")
    wide = jnp.moveaxis(gathered(wide, "rep"), 0, 1)
    return wide.reshape(rows, -1)


def extended_2(x, sides, width):
    for axis, dim in sides:
        devices, length = (lax.axis_size(axis), x.shape[dim])
        up = [(i, (i + 1) % devices) for i in range(devices - 1)]
        down = [(j, i) for i, j in up]
        last = lax.slice_in_dim(x, length - width, length, axis=dim)
        leading = lax.slice_in_dim(x, 0, width, axis=dim)
        before = lax.ppermute(last, axis, up)
        after = lax.ppermute(leading, axis, down)
        x = jnp.concatenate([before, x, after], axis=dim)
    return x


def activate(value):
    return leak_slope * value + (1.0 - leak_slope) * (jax.nn.softplus(value) - log_two)


def activate_slope(value):
    return leak_slope + (1.0 - leak_slope) * jax.nn.sigmoid(value)


def convolve(extended, kernel):
    result = lax.conv_general_dilated(
        extended[None],
        kernel,
        (1, 1, 1),
        [(0, 0), (1, 1), (1, 1)],
        dimension_numbers=("NDHWC", "DHWIO", "NDHWC"),
        preferred_element_type=jnp.float32,
    )
    return result[0]


def pooling(grid):
    depth, rows, cols, chans = grid.shape
    return grid.reshape(depth // 2, 2, rows // 2, 2, cols // 2, 2, chans).mean(axis=(1, 3, 5))


def expand(grid):
    depth, rows, cols, chans = grid.shape
    spread = jnp.broadcast_to(
        grid[:, None, :, None, :, None, :], (depth, 2, rows, 2, cols, 2, chans)
    )
    return spread.reshape(depth * 2, rows * 2, cols * 2, chans) / 8.0


def kernel_grad(extended, grad):
    widened = jnp.pad(extended, ((0, 0), (1, 1), (1, 1), (0, 0)))
    result = lax.conv_general_dilated(
        widened[..., None],
        grad[:, :, :, None, :],
        (1, 1, 1),
        "VALID",
        dimension_numbers=("DHWNC", "DHWIO", "NDHWC"),
        preferred_element_type=jnp.float32,
    )
    return jnp.transpose(result, (1, 2, 3, 0, 4)).reshape(-1, grad.shape[-1])


def general_shards(volumes, targets, first_kernel, second_kernel, head_weights):
    grid_in = volumes[0]
    target_row = targets[0]
    channels = grid_in.shape[-1]
    kernel_one = first_kernel.reshape(3, 3, 3, channels, first_kernel.shape[1])
    extended = extended_2(grid_in, (("space", 0),), 1)
    share = second_kernel.shape[1]
    place = lax.axis_index("space")
    kernel_two = whole_kernel(second_kernel).reshape(3, 3, 3, channels, -1)
    before_one = convolve(extended, kernel_one)
    pooled = pooling(activate(before_one)).astype(jnp.bfloat16)
    whole = gathered(pooled, "space").reshape((-1,) + pooled.shape[1:])
    padded_whole = jnp.pad(whole, ((1, 1), (0, 0), (0, 0), (0, 0)))
    before_two = convolve(padded_whole, kernel_two)
    feature = jnp.mean(activate(before_two), axis=(0, 1, 2))
    predicted = jnp.dot(feature, head_weights, precision=lax.Precision.HIGHEST)
    error = predicted - target_row
    feature_part = lax.dynamic_slice_in_dim(feature, place * share, share, 0)
    head_grad = feature_part[:, None] * error[None, :]
    feature_grad = jnp.dot(head_weights, error, precision=lax.Precision.HIGHEST)
    grad_two = (feature_grad * activate_slope(before_two)).astype(jnp.bfloat16)
    padded_grad = jnp.pad(grad_two, ((1, 1), (0, 0), (0, 0), (0, 0)))
    flipped = jnp.swapaxes(kernel_two[::-1, ::-1, ::-1], 3, 4)
    planes = pooled.shape[0]
    window = lax.dynamic_slice_in_dim(padded_grad, place * planes, planes + 2, 0)
    pooled_grad = convolve(window, flipped)
    grad_one = (expand(pooled_grad) * activate_slope(before_one)).astype(jnp.bfloat16)
    first_total = total_first(kernel_grad(extended, grad_one))
    grad_part = lax.dynamic_slice_in_dim(grad_two, place * share, share, 3)
    second_part = kernel_grad(padded_whole, grad_part)
    rows = second_part.shape[0]
    packed = jnp.concatenate([second_part[: rows // 2], second_part[rows // 2 :]], axis=1)
    packed = total_second(packed)
    second_total = jnp.concatenate([packed[:, :share], packed[:, share:]], axis=0)
    head_total = gathered(gathered(head_grad, "rep").sum(0), "dp").sum(0)
    return (first_total, second_total, head_total)


def neighbours(grid):
    devices = lax.axis_size("space")
    up = [(i, i + 1) for i in range(devices - 1)]
    down = [(j, i) for i, j in up]
    before = lax.ppermute(grid[-1:], "space", up)
    after = lax.ppermute(grid[:1], "space", down)
    return before, after


def shards(volumes, targets, first_kernel, second_kernel, head_weights):
    sizes = tuple(lax.axis_size(axis) for axis in ("space", "dp", "rep"))
    if sizes != (4, 2, 2):
        return general_shards(volumes, targets, first_kernel, second_kernel, head_weights)
    grid = volumes[0]
    share = second_kernel.shape[1]
    outs = head_weights.shape[1]
    place = lax.axis_index("space")
    rep = lax.axis_index("rep")
    copy = 2 * lax.axis_index("dp") + rep
    where = jnp.stack([(place - k) % 4 for k in range(4)] + [copy ^ k for k in range(4)])
    before, after = neighbours(grid)
    turned = second_kernel.T
    piece = lax.dynamic_slice_in_dim(turned, copy * (share // 4), share // 4, 0)
    others = jnp.concatenate([turn(piece, "space", k) for k in range(1, 4)], axis=0)
    across = turn(others, "dp", 1)
    pieces = [others, turn(others, "rep", 1), across, turn(across, "rep", 1)]
    pooled, slope = run_first_forward(grid, before, after, first_kernel)
    parts = [pooled] + [turn(pooled, "space", k) for k in range(1, 4)]
    blocks = head_weights.T.reshape(outs, 4, share)
    head = jnp.concatenate([lax.dynamic_index_in_dim(blocks, (place - k) % 4, 1, False) for k in range(4)], axis=1)
    head = jnp.pad(head, ((0, 8 - outs), (0, 0)))
    wanted = jnp.pad(jnp.broadcast_to(targets[0][:, None], (outs, 128)), ((0, 8 - outs), (0, 0)))
    pooled_grad, own, result = run_second_layer(where, parts, turned, pieces, head, wanted)
    keep, send = run_first_backward(grid, before, after, pooled_grad, slope, rep[None], 16)
    x = keep + turn(send, "rep", 1)
    x, own = lax.optimization_barrier((x, own))
    second_part = run_second_backward(where, parts, own, result)
    x = x.reshape(-1, x.shape[2])
    x = scattered_sum(x, "dp", bf16)
    x, second_part = lax.optimization_barrier((x, second_part))
    x = scattered_sum(x, "space", bf16).astype(bf16)
    for axis in ("space", "dp", "rep"):
        x = gathered(x, axis).reshape(-1, x.shape[1])
    first_total = run_spread_first(x.reshape((16, -1) + x.shape[1:]))
    second_total, head_total = run_spread_second(total_second(second_part), share)
    return (first_total, second_total.T, head_total[:outs, :share].T)


def solution(mesh):
    in_specs = (
        P(("groups", "dp", "rep"), "space", None, None, None),
        P(("groups", "dp", "rep"), None),
        P(),
        P(None, "space"),
        P(),
    )
    out_specs = (P("groups", None), P("groups", "space"), P(("groups", "space"), None))
    return jax.shard_map(shards, mesh=mesh, in_specs=in_specs, out_specs=out_specs, check_vma=False)
```

profile of v0, /device:TPU:0, one launch (start us, length us, event | category | flops | bytes accessed | tf_op | source)
XLA Modules:
  0.0 115.9 jit_solution(12012139791616381017)
XLA Ops:
  0.6 0.9 dynamic-slice_bitcast_fusion.1
  1.5 3.0 %collective-permute-start.5 = (bf16[16,3456]{1,0:T(8,128)(2,1)S(1)}, bf16[16,3456]{1,0:T(8,128)(2,1)S(1)}, u32[]{:S(2)}, u32[]{:S(2)}) collective-permute-start(bf16[16,3456]{1,0:T(8,128)(2,1)S(1)} %dynamic-slice_bitcast_fusion.1), channel_id=1, source_target_pairs={{0,4},{4,8},{8,12},{12,0},{1,5},{5,9},{9,13},{13,1},{2,6},{6,10},{... | collective-permute-start | bytes 331784 | tf_op jit(solution)/shard_map/ppermute | solution.py:430
  4.6 2.6 %collective-permute-start.6 = (bf16[16,3456]{1,0:T(8,128)(2,1)S(1)}, bf16[16,3456]{1,0:T(8,128)(2,1)S(1)}, u32[]{:S(2)}, u32[]{:S(2)}) collective-permute-start(bf16[16,3456]{1,0:T(8,128)(2,1)S(1)} %dynamic-slice_bitcast_fusion.1), channel_id=1, source_target_pairs={{0,8},{4,12},{8,0},{12,4},{1,9},{5,13},{9,1},{13,5},{2,10},{6,14},... | collective-permute-start | bytes 331784 | tf_op jit(solution)/shard_map/ppermute | solution.py:430
  7.2 1.3 %collective-permute-start.7 = (bf16[16,3456]{1,0:T(8,128)(2,1)S(1)}, bf16[16,3456]{1,0:T(8,128)(2,1)S(1)}, u32[]{:S(2)}, u32[]{:S(2)}) collective-permute-start(bf16[16,3456]{1,0:T(8,128)(2,1)S(1)} %dynamic-slice_bitcast_fusion.1), channel_id=1, source_target_pairs={{0,12},{4,0},{8,4},{12,8},{1,13},{5,1},{9,5},{13,9},{2,14},{6,2},{... | collective-permute-start | bytes 331784 | tf_op jit(solution)/shard_map/ppermute | solution.py:430
  8.5 2.1 %collective-permute-done.5 = bf16[16,3456]{1,0:T(8,128)(2,1)S(1)} collective-permute-done((bf16[16,3456]{1,0:T(8,128)(2,1)S(1)}, bf16[16,3456]{1,0:T(8,128)(2,1)S(1)}, u32[]{:S(2)}, u32[]{:S(2)}) %collective-permute-start.5) | collective-permute-done | bytes 110624 | tf_op jit(solution)/shard_map/ppermute | solution.py:430
  10.6 3.9 %collective-permute-done.6 = bf16[16,3456]{1,0:T(8,128)(2,1)S(1)} collective-permute-done((bf16[16,3456]{1,0:T(8,128)(2,1)S(1)}, bf16[16,3456]{1,0:T(8,128)(2,1)S(1)}, u32[]{:S(2)}, u32[]{:S(2)}) %collective-permute-start.6) | collective-permute-done | bytes 110624 | tf_op jit(solution)/shard_map/ppermute | solution.py:430
  14.5 1.6 %collective-permute-start.9 = (bf16[48,3456]{1,0:T(8,128)(2,1)S(1)}, bf16[48,3456]{1,0:T(8,128)(2,1)S(1)}, u32[]{:S(2)}, u32[]{:S(2)}) collective-permute-start(bf16[48,3456]{1,0:T(8,128)(2,1)S(1)} %constant_dynamic-update-slice_fusion.w1), channel_id=1, source_target_pairs={{0,2},{2,0},{1,3},{3,1},{4,6},{6,4},{5,7},{7,5},{8,10},{10,8},{9,1... | collective-permute-start | bytes 995336 | tf_op jit(solution)/shard_map/ppermute | solution.py:430
  16.1 1.0 slice_bitcast_fusion
  17.2 4.7 %collective-permute-start = (bf16[1,24,24,128]{3,2,1,0:T(8,128)(2,1)S(1)}, bf16[1,24,24,128]{3,2,1,0:T(8,128)(2,1)S(1)}, u32[]{:S(2)}, u32[]{:S(2)}) collective-permute-start(bf16[1,24,24,128]{3,2,1,0:T(8,128)(2,1)S(1)} %get-tuple-element.34), channel_id=1, source_target_pairs={{0,4},{4,8},{8,12},{1,5},{5,9},{9,13},{2,6},{6,10},{10,14},{3,7},{... | collective-permute-start | bytes 442376 | tf_op jit(solution)/shard_map/ppermute | solution.py:604
  21.9 1.3 %collective-permute-start.1 = (bf16[1,24,24,128]{3,2,1,0:T(8,128)(2,1)S(1)}, bf16[1,24,24,128]{3,2,1,0:T(8,128)(2,1)S(1)}, u32[]{:S(2)}, u32[]{:S(2)}) collective-permute-start(bf16[1,24,24,128]{3,2,1,0:T(8,128)(2,1)S(1)} %get-tuple-element.33), channel_id=1, source_target_pairs={{4,0},{8,4},{12,8},{5,1},{9,5},{13,9},{6,2},{10,6},{14,10},{7,3},{... | collective-permute-start | bytes 442376 | tf_op jit(solution)/shard_map/ppermute | solution.py:605
  23.3 0.8 reshape.36
  24.0 0.7 pad.11
  24.7 0.6 stack.35.where
  25.9 3.1 %collective-permute-done.1.after = bf16[1,24,24,128]{3,2,1,0:T(8,128)(2,1)S(1)} collective-permute-done((bf16[1,24,24,128]{3,2,1,0:T(8,128)(2,1)S(1)}, bf16[1,24,24,128]{3,2,1,0:T(8,128)(2,1)S(1)}, u32[]{:S(2)}, u32[]{:S(2)}) %collective-permute-start.1) | collective-permute-done | bytes 147488 | tf_op jit(solution)/shard_map/ppermute | solution.py:605
  29.0 0.7 copy-done.8
  29.6 8.4 %shard_map.76 = (bf16[2,144,128]{2,1,0:T(8,128)(2,1)}, f32[4,768,128]{2,1,0:T(8,128)}) custom-call(bf16[4,24,24,128]{3,2,1,0:T(8,128)(2,1)} %bitcast.107, bf16[1,24,24,128]{3,2,1,0:T(8,128)(2,1)} %copy-done.7, bf16[1,24,24,128]{3,2,1,0:T(8,128)(2,1)} %copy-done.8, bf16[3456,128]{1,0:T(8,128)(2,1)} %kernel.1), custom_call_target="tpu_custom_call" | custom-call | flops 8000000000 | tf_op jit(solution)/shard_map/pallas_call | solution.py:18
  38.4 1.3 %collective-permute-start.3 = (bf16[2,144,128]{2,1,0:T(8,128)(2,1)}, bf16[2,144,128]{2,1,0:T(8,128)(2,1)S(1)}, u32[]{:S(2)}, u32[]{:S(2)}) collective-permute-start(bf16[2,144,128]{2,1,0:T(8,128)(2,1)} %get-tuple-element.16.p0), channel_id=1, source_target_pairs={{0,8},{4,12},{8,0},{12,4},{1,9},{5,13},{9,1},{13,5},{2,10},{6,14},... | collective-permute-start | bytes 221192 | tf_op jit(solution)/shard_map/ppermute | solution.py:430
  39.7 2.8 %collective-permute-start.4 = (bf16[2,144,128]{2,1,0:T(8,128)(2,1)}, bf16[2,144,128]{2,1,0:T(8,128)(2,1)S(1)}, u32[]{:S(2)}, u32[]{:S(2)}) collective-permute-start(bf16[2,144,128]{2,1,0:T(8,128)(2,1)} %get-tuple-element.16.p0), channel_id=1, source_target_pairs={{0,12},{4,0},{8,4},{12,8},{1,13},{5,1},{9,5},{13,9},{2,14},{6,2},{... | collective-permute-start | bytes 221192 | tf_op jit(solution)/shard_map/ppermute | solution.py:430
  42.6 0.7 select_maximum_fusion.head
  43.3 1.3 %collective-permute-done.2.p1 = bf16[2,144,128]{2,1,0:T(8,128)(2,1)S(1)} collective-permute-done((bf16[2,144,128]{2,1,0:T(8,128)(2,1)}, bf16[2,144,128]{2,1,0:T(8,128)(2,1)S(1)}, u32[]{:S(2)}, u32[]{:S(2)}) %collective-permute-start.2) | collective-permute-done | bytes 73760 | tf_op jit(solution)/shard_map/ppermute | solution.py:430
  44.6 1.7 %collective-permute-done.3.p2 = bf16[2,144,128]{2,1,0:T(8,128)(2,1)S(1)} collective-permute-done((bf16[2,144,128]{2,1,0:T(8,128)(2,1)}, bf16[2,144,128]{2,1,0:T(8,128)(2,1)S(1)}, u32[]{:S(2)}, u32[]{:S(2)}) %collective-permute-start.3) | collective-permute-done | bytes 73760 | tf_op jit(solution)/shard_map/ppermute | solution.py:430
  46.4 0.7 pad.12.wanted
  47.2 8.6 %shard_map.77 = (f32[2,192,128]{2,1,0:T(8,128)}, bf16[8,192,64]{2,1,0:T(8,128)(2,1)}, f32[8,256]{1,0:T(8,128)}) custom-call(s32[8]{0:T(128)} %stack.35.where, bf16[2,144,128]{2,1,0:T(8,128)(2,1)} %get-tuple-element.16.p0, bf16[2,144,128]{2,1,0:T(8,128)(2,1)} %copy-done.9, bf16[2,144,128]{2,1,0:T(8,128)(2,1)} %copy-done.10, bf16[2,144,128]{2,1,0:T(8,128)(2,1)} %copy-done.11, ...), custom_call_target="tpu_custom_call" | custom-call | flops 8000000000 | tf_op jit(solution)/shard_map/pallas_call | solution.py:18
  55.8 7.1 %shard_map.78 = (f32[8,216,128]{2,1,0:T(8,128)}, f32[8,216,128]{2,1,0:T(8,128)}) custom-call(bf16[4,24,24,128]{3,2,1,0:T(8,128)(2,1)} %bitcast.108, bf16[1,24,24,128]{3,2,1,0:T(8,128)(2,1)} %copy-done.7, bf16[1,24,24,128]{3,2,1,0:T(8,128)(2,1)} %copy-done.8, f32[2,192,128]{2,1,0:T(8,128)} %get-tuple-element.17.spread, ...), custom_call_target="tpu_custom_call" | custom-call | flops 7000000000 | tf_op jit(solution)/shard_map/pallas_call | solution.py:18
  62.9 2.6 %collective-permute-done.11 = f32[8,216,128]{2,1,0:T(8,128)S(1)} collective-permute-done((f32[8,216,128]{2,1,0:T(8,128)}, f32[8,216,128]{2,1,0:T(8,128)S(1)}, u32[]{:S(2)}, u32[]{:S(2)}) %collective-permute-start.11) | collective-permute-done | bytes 884768 | tf_op jit(solution)/shard_map/ppermute | solution.py:430
  65.5 1.3 %add.175 = f32[8,216,128]{2,1,0:T(8,128)S(1)} add(f32[8,216,128]{2,1,0:T(8,128)} %get-tuple-element.19, f32[8,216,128]{2,1,0:T(8,128)S(1)} %collective-permute-done.11) | non-fusion elementwise | flops 221184 | bytes 2654208 | tf_op jit(solution)/shard_map/add | solution.py:634
  66.8 0.6 collective-permute-start.12
  67.4 4.0 %shard_map.79 = f32[1744,128]{1,0:T(8,128)} custom-call(s32[8]{0:T(128)} %stack.35.where, bf16[2,144,128]{2,1,0:T(8,128)(2,1)} %get-tuple-element.16.p0, bf16[2,144,128]{2,1,0:T(8,128)(2,1)} %copy-done.9, bf16[2,144,128]{2,1,0:T(8,128)(2,1)} %copy-done.10, bf16[2,144,128]{2,1,0:T(8,128)(2,1)} %copy-done.11, bf16[8,192,64]{2,1,0:T(8,128)(2,1)} %get-tuple-element.23.own, ...), custom_call_target="tpu_custom_call" | custom-call | flops 4000000000 | tf_op jit(solution)/shard_map/pallas_call | solution.py:18
  71.4 3.0 %collective-permute-done.12 = bf16[864,128]{1,0:T(8,128)(2,1)S(1)} collective-permute-done((bf16[864,128]{1,0:T(8,128)(2,1)S(1)}, bf16[864,128]{1,0:T(8,128)(2,1)S(1)}, u32[]{:S(2)}, u32[]{:S(2)}) %collective-permute-start.12) | collective-permute-done | bytes 221216 | tf_op jit(solution)/shard_map/ppermute | solution.py:430
  74.4 1.6 %collective-permute-start.13 = (bf16[216,128]{1,0:T(8,128)(2,1)S(1)}, bf16[216,128]{1,0:T(8,128)(2,1)S(1)}, u32[]{:S(2)}, u32[]{:S(2)}) collective-permute-start(bf16[216,128]{1,0:T(8,128)(2,1)S(1)} %get-tuple-element.35), channel_id=1, source_target_pairs={{0,4},{4,8},{8,12},{12,0},{1,5},{5,9},{9,13},{13,1},{2,6},{6,10},{... | collective-permute-start | bytes 165896 | tf_op jit(solution)/shard_map/ppermute | solution.py:430
  76.0 1.9 %collective-permute-start.14 = (bf16[216,128]{1,0:T(8,128)(2,1)S(1)}, bf16[216,128]{1,0:T(8,128)(2,1)S(1)}, u32[]{:S(2)}, u32[]{:S(2)}) collective-permute-start(bf16[216,128]{1,0:T(8,128)(2,1)S(1)} %get-tuple-element.37), channel_id=1, source_target_pairs={{0,8},{4,12},{8,0},{12,4},{1,9},{5,13},{9,1},{13,5},{2,10},{6,14},... | collective-permute-start | bytes 165896 | tf_op jit(solution)/shard_map/ppermute | solution.py:430
  77.9 0.6 collective-permute-start.15
  78.4 2.5 %collective-permute-done.13 = bf16[216,128]{1,0:T(8,128)(2,1)S(1)} collective-permute-done((bf16[216,128]{1,0:T(8,128)(2,1)S(1)}, bf16[216,128]{1,0:T(8,128)(2,1)S(1)}, u32[]{:S(2)}, u32[]{:S(2)}) %collective-permute-start.13) | collective-permute-done | bytes 55328 | tf_op jit(solution)/shard_map/ppermute | solution.py:430
  80.9 1.5 %collective-permute-done.14 = bf16[216,128]{1,0:T(8,128)(2,1)S(1)} collective-permute-done((bf16[216,128]{1,0:T(8,128)(2,1)S(1)}, bf16[216,128]{1,0:T(8,128)(2,1)S(1)}, u32[]{:S(2)}, u32[]{:S(2)}) %collective-permute-start.14) | collective-permute-done | bytes 55328 | tf_op jit(solution)/shard_map/ppermute | solution.py:430
  82.7 1.0 collective-permute-start.16
  83.6 1.9 %collective-permute-start.17 = (bf16[216,128]{1,0:T(8,128)(2,1)S(1)}, bf16[216,128]{1,0:T(8,128)(2,1)S(1)}, u32[]{:S(2)}, u32[]{:S(2)}) collective-permute-start(bf16[216,128]{1,0:T(8,128)(2,1)S(1)} %get-tuple-element.32), channel_id=1, source_target_pairs={{0,8},{4,12},{8,0},{12,4},{1,9},{5,13},{9,1},{13,5},{2,10},{6,14},... | collective-permute-start | bytes 165896 | tf_op jit(solution)/shard_map/ppermute | solution.py:430
  85.6 1.0 collective-permute-start.18
  86.6 2.2 %collective-permute-done.16 = bf16[216,128]{1,0:T(8,128)(2,1)S(1)} collective-permute-done((bf16[216,128]{1,0:T(8,128)(2,1)S(1)}, bf16[216,128]{1,0:T(8,128)(2,1)S(1)}, u32[]{:S(2)}, u32[]{:S(2)}) %collective-permute-start.16) | collective-permute-done | bytes 55328 | tf_op jit(solution)/shard_map/ppermute | solution.py:430
  88.8 1.2 %collective-permute-done.17 = bf16[216,128]{1,0:T(8,128)(2,1)S(1)} collective-permute-done((bf16[216,128]{1,0:T(8,128)(2,1)S(1)}, bf16[216,128]{1,0:T(8,128)(2,1)S(1)}, u32[]{:S(2)}, u32[]{:S(2)}) %collective-permute-start.17) | collective-permute-done | bytes 55328 | tf_op jit(solution)/shard_map/ppermute | solution.py:430
  90.2 0.6 collective-permute-start.19
  91.1 5.1 %collective-permute-done.19 = bf16[864,128]{1,0:T(8,128)(2,1)S(1)} collective-permute-done((bf16[864,128]{1,0:T(8,128)(2,1)S(1)}, bf16[864,128]{1,0:T(8,128)(2,1)S(1)}, u32[]{:S(2)}, u32[]{:S(2)}) %collective-permute-start.19) | collective-permute-done | bytes 221216 | tf_op jit(solution)/shard_map/ppermute | solution.py:430
  96.5 0.6 collective-permute-start.22
  97.3 7.2 %collective-permute-done.22 = bf16[872,128]{1,0:T(8,128)(2,1)S(1)} collective-permute-done((bf16[872,128]{1,0:T(8,128)(2,1)S(1)}, bf16[872,128]{1,0:T(8,128)(2,1)S(1)}, u32[]{:S(2)}, u32[]{:S(2)}) %collective-permute-start.22) | collective-permute-done | bytes 223264 | tf_op jit(solution)/shard_map/ppermute | solution.py:430
  104.8 0.9 copy-done.1
  105.7 5.8 %shard_map.80 = f32[27,128,128]{2,1,0:T(8,128)} custom-call(bf16[16,216,128]{2,1,0:T(8,128)(2,1)} %bitcast.95), custom_call_target="tpu_custom_call" | custom-call | tf_op jit(solution)/shard_map/pallas_call | solution.py:400
  111.6 0.9 copy-done
  112.5 2.1 %shard_map.81 = (f32[64,3456]{1,0:T(8,128)}, f32[8,128]{1,0:T(8,128)}) custom-call(f32[1744,128]{1,0:T(8,128)} %bitcast.94), custom_call_target="tpu_custom_call" | custom-call | tf_op jit(solution)/shard_map/pallas_call | solution.py:18
  114.7 1.2 %slice_bitcast_fusion.2 = f32[64,4]{0,1:T(4,128)} fusion(f32[8,128]{1,0:T(8,128)} %get-tuple-element.28), kind=kLoop, calls=%fused_computation.43 | loop fusion | bytes 2048 | tf_op jit(solution)/shard_map/transpose | solution.py:645
  (65 shorter events, 2.7 us)
Async XLA Ops:
  1.5 9.0 %collective-permute-start.5 = (bf16[16,3456]{1,0:T(8,128)(2,1)S(1)}, bf16[16,3456]{1,0:T(8,128)(2,1)S(1)}, u32[]{:S(2)}, u32[]{:S(2)}) collective-permute-start(bf16[16,3456]{1,0:T(8,128)(2,1)S(1)} %dynamic-slice_bitcast_fusion.1), channel_id=1, source_target_pairs={{0,4},{4,8},{8,12},{12,0},{1,5},{5,9},{9,13},{13,1},{2,6},{6,10},{... | collective-permute-start | bytes 331784 | tf_op jit(solution)/shard_map/ppermute | solution.py:430
  4.6 9.9 %collective-permute-start.6 = (bf16[16,3456]{1,0:T(8,128)(2,1)S(1)}, bf16[16,3456]{1,0:T(8,128)(2,1)S(1)}, u32[]{:S(2)}, u32[]{:S(2)}) collective-permute-start(bf16[16,3456]{1,0:T(8,128)(2,1)S(1)} %dynamic-slice_bitcast_fusion.1), channel_id=1, source_target_pairs={{0,8},{4,12},{8,0},{12,4},{1,9},{5,13},{9,1},{13,5},{2,10},{6,14},... | collective-permute-start | bytes 331784 | tf_op jit(solution)/shard_map/ppermute | solution.py:430
  7.2 7.3 %collective-permute-start.7 = (bf16[16,3456]{1,0:T(8,128)(2,1)S(1)}, bf16[16,3456]{1,0:T(8,128)(2,1)S(1)}, u32[]{:S(2)}, u32[]{:S(2)}) collective-permute-start(bf16[16,3456]{1,0:T(8,128)(2,1)S(1)} %dynamic-slice_bitcast_fusion.1), channel_id=1, source_target_pairs={{0,12},{4,0},{8,4},{12,8},{1,13},{5,1},{9,5},{13,9},{2,14},{6,2},{... | collective-permute-start | bytes 331784 | tf_op jit(solution)/shard_map/ppermute | solution.py:430
  14.5 23.5 %copy-start.3 = (bf16[48,3456]{1,0:T(8,128)(2,1)}, bf16[48,3456]{1,0:T(8,128)(2,1)S(1)}, u32[]{:S(2)}) copy-start(bf16[48,3456]{1,0:T(8,128)(2,1)S(1)} %constant_dynamic-update-slice_fusion.w1) | copy-start | bytes 995332
  14.5 10.9 %collective-permute-start.9 = (bf16[48,3456]{1,0:T(8,128)(2,1)S(1)}, bf16[48,3456]{1,0:T(8,128)(2,1)S(1)}, u32[]{:S(2)}, u32[]{:S(2)}) collective-permute-start(bf16[48,3456]{1,0:T(8,128)(2,1)S(1)} %constant_dynamic-update-slice_fusion.w1), channel_id=1, source_target_pairs={{0,2},{2,0},{1,3},{3,1},{4,6},{6,4},{5,7},{7,5},{8,10},{10,8},{9,1... | collective-permute-start | bytes 995336 | tf_op jit(solution)/shard_map/ppermute | solution.py:430
  17.2 8.7 %collective-permute-start = (bf16[1,24,24,128]{3,2,1,0:T(8,128)(2,1)S(1)}, bf16[1,24,24,128]{3,2,1,0:T(8,128)(2,1)S(1)}, u32[]{:S(2)}, u32[]{:S(2)}) collective-permute-start(bf16[1,24,24,128]{3,2,1,0:T(8,128)(2,1)S(1)} %get-tuple-element.34), channel_id=1, source_target_pairs={{0,4},{4,8},{8,12},{1,5},{5,9},{9,13},{2,6},{6,10},{10,14},{3,7},{... | collective-permute-start | bytes 442376 | tf_op jit(solution)/shard_map/ppermute | solution.py:604
  21.9 7.1 %collective-permute-start.1 = (bf16[1,24,24,128]{3,2,1,0:T(8,128)(2,1)S(1)}, bf16[1,24,24,128]{3,2,1,0:T(8,128)(2,1)S(1)}, u32[]{:S(2)}, u32[]{:S(2)}) collective-permute-start(bf16[1,24,24,128]{3,2,1,0:T(8,128)(2,1)S(1)} %get-tuple-element.33), channel_id=1, source_target_pairs={{4,0},{8,4},{12,8},{5,1},{9,5},{13,9},{6,2},{10,6},{14,10},{7,3},{... | collective-permute-start | bytes 442376 | tf_op jit(solution)/shard_map/ppermute | solution.py:605
  25.3 21.0 %collective-permute-start.8 = (bf16[48,3456]{1,0:T(8,128)(2,1)S(1)}, bf16[48,3456]{1,0:T(8,128)(2,1)S(1)}, u32[]{:S(2)}, u32[]{:S(2)}) collective-permute-start(bf16[48,3456]{1,0:T(8,128)(2,1)S(1)} %constant_dynamic-update-slice_fusion.w1), channel_id=1, source_target_pairs={{0,1},{1,0},{2,3},{3,2},{4,5},{5,4},{6,7},{7,6},{8,9},{9,8},{10,11... | collective-permute-start | bytes 995336 | tf_op jit(solution)/shard_map/ppermute | solution.py:430
  25.4 12.7 %copy-start.4 = (bf16[48,3456]{1,0:T(8,128)(2,1)}, bf16[48,3456]{1,0:T(8,128)(2,1)S(1)}, u32[]{:S(2)}) copy-start(bf16[48,3456]{1,0:T(8,128)(2,1)S(1)} %collective-permute-done.9.w3) | copy-start | bytes 995332
  25.4 20.9 %collective-permute-start.10 = (bf16[48,3456]{1,0:T(8,128)(2,1)S(1)}, bf16[48,3456]{1,0:T(8,128)(2,1)S(1)}, u32[]{:S(2)}, u32[]{:S(2)}) collective-permute-start(bf16[48,3456]{1,0:T(8,128)(2,1)S(1)} %collective-permute-done.9.w3), channel_id=1, source_target_pairs={{0,1},{1,0},{2,3},{3,2},{4,5},{5,4},{6,7},{7,6},{8,9},{9,8},{10,11... | collective-permute-start | bytes 995336 | tf_op jit(solution)/shard_map/ppermute | solution.py:430
  25.9 3.1 %copy-start.7 = (bf16[1,24,24,128]{3,2,1,0:T(8,128)(2,1)}, bf16[1,24,24,128]{3,2,1,0:T(8,128)(2,1)S(1)}, u32[]{:S(2)}) copy-start(bf16[1,24,24,128]{3,2,1,0:T(8,128)(2,1)S(1)} %collective-permute-done.before) | copy-start | bytes 442372
  29.0 0.7 copy-start.8
  38.1 6.5 %collective-permute-start.2 = (bf16[2,144,128]{2,1,0:T(8,128)(2,1)}, bf16[2,144,128]{2,1,0:T(8,128)(2,1)S(1)}, u32[]{:S(2)}, u32[]{:S(2)}) collective-permute-start(bf16[2,144,128]{2,1,0:T(8,128)(2,1)} %get-tuple-element.16.p0), channel_id=1, source_target_pairs={{0,4},{4,8},{8,12},{12,0},{1,5},{5,9},{9,13},{13,1},{2,6},{6,10},{... | collective-permute-start | bytes 221192 | tf_op jit(solution)/shard_map/ppermute | solution.py:430
  38.4 7.9 %collective-permute-start.3 = (bf16[2,144,128]{2,1,0:T(8,128)(2,1)}, bf16[2,144,128]{2,1,0:T(8,128)(2,1)S(1)}, u32[]{:S(2)}, u32[]{:S(2)}) collective-permute-start(bf16[2,144,128]{2,1,0:T(8,128)(2,1)} %get-tuple-element.16.p0), channel_id=1, source_target_pairs={{0,8},{4,12},{8,0},{12,4},{1,9},{5,13},{9,1},{13,5},{2,10},{6,14},... | collective-permute-start | bytes 221192 | tf_op jit(solution)/shard_map/ppermute | solution.py:430
  39.7 6.6 %collective-permute-start.4 = (bf16[2,144,128]{2,1,0:T(8,128)(2,1)}, bf16[2,144,128]{2,1,0:T(8,128)(2,1)S(1)}, u32[]{:S(2)}, u32[]{:S(2)}) collective-permute-start(bf16[2,144,128]{2,1,0:T(8,128)(2,1)} %get-tuple-element.16.p0), channel_id=1, source_target_pairs={{0,12},{4,0},{8,4},{12,8},{1,13},{5,1},{9,5},{13,9},{2,14},{6,2},{... | collective-permute-start | bytes 221192 | tf_op jit(solution)/shard_map/ppermute | solution.py:430
  44.6 2.5 %copy-start.9 = (bf16[2,144,128]{2,1,0:T(8,128)(2,1)}, bf16[2,144,128]{2,1,0:T(8,128)(2,1)S(1)}, u32[]{:S(2)}) copy-start(bf16[2,144,128]{2,1,0:T(8,128)(2,1)S(1)} %collective-permute-done.2.p1) | copy-start | bytes 221188
  46.3 0.8 copy-start.10
  46.3 0.8 copy-start.11
  46.3 0.8 copy-start.5
  46.3 0.9 copy-start.6
  62.9 2.6 %collective-permute-start.11 = (f32[8,216,128]{2,1,0:T(8,128)}, f32[8,216,128]{2,1,0:T(8,128)S(1)}, u32[]{:S(2)}, u32[]{:S(2)}) collective-permute-start(f32[8,216,128]{2,1,0:T(8,128)} %get-tuple-element.20), channel_id=1, source_target_pairs={{0,1},{1,0},{2,3},{3,2},{4,5},{5,4},{6,7},{7,6},{8,9},{9,8},{10,11... | collective-permute-start | bytes 2654216 | tf_op jit(solution)/shard_map/ppermute | solution.py:430
  66.8 7.5 %collective-permute-start.12 = (bf16[864,128]{1,0:T(8,128)(2,1)S(1)}, bf16[864,128]{1,0:T(8,128)(2,1)S(1)}, u32[]{:S(2)}, u32[]{:S(2)}) collective-permute-start(bf16[864,128]{1,0:T(8,128)(2,1)S(1)} %fusion.1), channel_id=1, source_target_pairs={{0,2},{2,0},{1,3},{3,1},{4,6},{6,4},{5,7},{7,5},{8,10},{10,8},{9,1... | collective-permute-start | bytes 663560 | tf_op jit(solution)/shard_map/ppermute | solution.py:430
  71.4 19.4 %copy-start.2 = (f32[1744,128]{1,0:T(8,128)S(1)}, f32[1744,128]{1,0:T(8,128)}, u32[]{:S(2)}) copy-start(f32[1744,128]{1,0:T(8,128)} %shard_map.79) | copy-start | bytes 2678788
  74.4 6.5 %collective-permute-start.13 = (bf16[216,128]{1,0:T(8,128)(2,1)S(1)}, bf16[216,128]{1,0:T(8,128)(2,1)S(1)}, u32[]{:S(2)}, u32[]{:S(2)}) collective-permute-start(bf16[216,128]{1,0:T(8,128)(2,1)S(1)} %get-tuple-element.35), channel_id=1, source_target_pairs={{0,4},{4,8},{8,12},{12,0},{1,5},{5,9},{9,13},{13,1},{2,6},{6,10},{... | collective-permute-start | bytes 165896 | tf_op jit(solution)/shard_map/ppermute | solution.py:430
  76.0 6.4 %collective-permute-start.14 = (bf16[216,128]{1,0:T(8,128)(2,1)S(1)}, bf16[216,128]{1,0:T(8,128)(2,1)S(1)}, u32[]{:S(2)}, u32[]{:S(2)}) collective-permute-start(bf16[216,128]{1,0:T(8,128)(2,1)S(1)} %get-tuple-element.37), channel_id=1, source_target_pairs={{0,8},{4,12},{8,0},{12,4},{1,9},{5,13},{9,1},{13,5},{2,10},{6,14},... | collective-permute-start | bytes 165896 | tf_op jit(solution)/shard_map/ppermute | solution.py:430
  77.9 4.7 %collective-permute-start.15 = (bf16[216,128]{1,0:T(8,128)(2,1)S(1)}, bf16[216,128]{1,0:T(8,128)(2,1)S(1)}, u32[]{:S(2)}, u32[]{:S(2)}) collective-permute-start(bf16[216,128]{1,0:T(8,128)(2,1)S(1)} %get-tuple-element.36), channel_id=1, source_target_pairs={{0,12},{4,0},{8,4},{12,8},{1,13},{5,1},{9,5},{13,9},{2,14},{6,2},{... | collective-permute-start | bytes 165896 | tf_op jit(solution)/shard_map/ppermute | solution.py:430
  82.7 6.1 %collective-permute-start.16 = (bf16[216,128]{1,0:T(8,128)(2,1)S(1)}, bf16[216,128]{1,0:T(8,128)(2,1)S(1)}, u32[]{:S(2)}, u32[]{:S(2)}) collective-permute-start(bf16[216,128]{1,0:T(8,128)(2,1)S(1)} %get-tuple-element.32), channel_id=1, source_target_pairs={{0,4},{4,8},{8,12},{12,0},{1,5},{5,9},{9,13},{13,1},{2,6},{6,10},{... | collective-permute-start | bytes 165896 | tf_op jit(solution)/shard_map/ppermute | solution.py:430
  83.6 6.3 %collective-permute-start.17 = (bf16[216,128]{1,0:T(8,128)(2,1)S(1)}, bf16[216,128]{1,0:T(8,128)(2,1)S(1)}, u32[]{:S(2)}, u32[]{:S(2)}) collective-permute-start(bf16[216,128]{1,0:T(8,128)(2,1)S(1)} %get-tuple-element.32), channel_id=1, source_target_pairs={{0,8},{4,12},{8,0},{12,4},{1,9},{5,13},{9,1},{13,5},{2,10},{6,14},... | collective-permute-start | bytes 165896 | tf_op jit(solution)/shard_map/ppermute | solution.py:430
  85.6 4.6 %collective-permute-start.18 = (bf16[216,128]{1,0:T(8,128)(2,1)S(1)}, bf16[216,128]{1,0:T(8,128)(2,1)S(1)}, u32[]{:S(2)}, u32[]{:S(2)}) collective-permute-start(bf16[216,128]{1,0:T(8,128)(2,1)S(1)} %get-tuple-element.32), channel_id=1, source_target_pairs={{0,12},{4,0},{8,4},{12,8},{1,13},{5,1},{9,5},{13,9},{2,14},{6,2},{... | collective-permute-start | bytes 165896 | tf_op jit(solution)/shard_map/ppermute | solution.py:430
  90.2 6.0 %collective-permute-start.19 = (bf16[864,128]{1,0:T(8,128)(2,1)S(1)}, bf16[864,128]{1,0:T(8,128)(2,1)S(1)}, u32[]{:S(2)}, u32[]{:S(2)}) collective-permute-start(bf16[864,128]{1,0:T(8,128)(2,1)S(1)} %bitcast.105), channel_id=1, source_target_pairs={{0,2},{2,0},{1,3},{3,1},{4,6},{6,4},{5,7},{7,5},{8,10},{10,8},{9,1... | collective-permute-start | bytes 663560 | tf_op jit(solution)/shard_map/ppermute | solution.py:430
  90.8 5.5 %collective-permute-start.21 = (f32[872,128]{1,0:T(8,128)S(1)}, f32[872,128]{1,0:T(8,128)S(1)}, u32[]{:S(2)}, u32[]{:S(2)}) collective-permute-start(f32[872,128]{1,0:T(8,128)S(1)} %dynamic-slice_bitcast_fusion), channel_id=1, source_target_pairs={{0,1},{1,0},{2,3},{3,2},{4,5},{5,4},{6,7},{7,6},{8,9},{9,8},{10,11... | collective-permute-start | bytes 1339400 | tf_op jit(solution)/shard_map/ppermute | solution.py:430
  96.3 8.5 %collective-permute-start.20 = (bf16[1728,128]{1,0:T(8,128)(2,1)S(1)}, bf16[1728,128]{1,0:T(8,128)(2,1)S(1)}, u32[]{:S(2)}, u32[]{:S(2)}) collective-permute-start(bf16[1728,128]{1,0:T(8,128)(2,1)S(1)} %bitcast.98), channel_id=1, source_target_pairs={{0,1},{1,0},{2,3},{3,2},{4,5},{5,4},{6,7},{7,6},{8,9},{9,8},{10,11... | collective-permute-start | bytes 1327112 | tf_op jit(solution)/shard_map/ppermute | solution.py:430
  96.5 7.9 %collective-permute-start.22 = (bf16[872,128]{1,0:T(8,128)(2,1)S(1)}, bf16[872,128]{1,0:T(8,128)(2,1)S(1)}, u32[]{:S(2)}, u32[]{:S(2)}) collective-permute-start(bf16[872,128]{1,0:T(8,128)(2,1)S(1)} %get-tuple-element.30), channel_id=1, source_target_pairs={{0,2},{2,0},{1,3},{3,1},{4,6},{6,4},{5,7},{7,5},{8,10},{10,8},{9,1... | collective-permute-start | bytes 669704 | tf_op jit(solution)/shard_map/ppermute | solution.py:430
  104.5 7.0 %collective-permute-start.23 = (f32[872,128]{1,0:T(8,128)S(1)}, f32[872,128]{1,0:T(8,128)S(1)}, u32[]{:S(2)}, u32[]{:S(2)}) collective-permute-start(f32[872,128]{1,0:T(8,128)S(1)} %convert_reduce_fusion), channel_id=1, source_target_pairs={{0,1},{1,0},{2,3},{3,2},{4,5},{5,4},{6,7},{7,6},{8,9},{9,8},{10,11... | collective-permute-start | bytes 1339400 | tf_op jit(solution)/shard_map/ppermute | solution.py:430
  104.8 0.9 copy-start.1
  111.6 0.9 copy-start
where the time goes:
time: 117 us; the launch traced here: 116 us
  waiting for transfers between devices  37.8 us (32%)
  Pallas kernels  36 us (31%)
  starting transfers between devices  29.4 us (25%)
  local copies, waits for them, and re-layouts  9.39 us (8%)
  other arithmetic  2.18 us (2%)
    ppermute x22, waiting for transfers between devices, turn(): return lax.ppermute(x, axis, [(i, (i + step) % size) for i in range(size)])  34.7 us
    pallas_call x5, Pallas kernels, call(): pl.pallas_call(body, out_shape=outs, in_specs=specs, out_specs=jax.tree.m...  30.2 us
    ppermute x22, starting transfers between devices, turn(): return lax.ppermute(x, axis, [(i, (i + step) % size) for i in range(size)])  23.4 us
    pallas_call x1, Pallas kernels, run_spread_first(): pl.pallas_call(spread_first, grid=(steps,), out_shape=jax.ShapeDtypeStruc...  5.82 us
    ppermute x1, starting transfers between devices, neighbours(): before = lax.ppermute(grid[-1:], 'space', up)  4.72 us
    ppermute x1, waiting for transfers between devices, neighbours(): after = lax.ppermute(grid[:1], 'space', down)  3.09 us
    unnamed x26, local copies, waits for them, and re-layouts  2.66 us
  transfers between devices with their start and end apart: 24, of which 15 were waited for; matrix products, arithmetic and copies ran while one was open for 4% of the time, Pallas kernels for 16%

commit v1 on v0

--- a/solution.py
+++ b/solution.py
@@ -13,15 +13,21 @@
 heavy = 10**9
 
 
-def call(body, outs, scratch, *args, smem=(), work=0):
-    specs = [pl.BlockSpec(memory_space=pltpu.SMEM if k in smem else pltpu.VMEM) for k in range(len(args))]
+def call(body, outs, scratch, *args, smem=(), away=(), work=0, room=16, far_outs=()):
+    spaces = [pltpu.SMEM if k in smem else pltpu.HBM if k in away else pltpu.VMEM for k in range(len(args))]
+    specs = [pl.BlockSpec(memory_space=space) for space in spaces]
+    one = not isinstance(outs, tuple)
+    out_specs = [
+        pl.BlockSpec(memory_space=pltpu.HBM if k in far_outs else pltpu.VMEM) for k in range(1 if one else len(outs))
+    ]
+    out_specs = out_specs[0] if one else tuple(out_specs)
     return pl.pallas_call(
         body,
         out_shape=outs,
         in_specs=specs,
-        out_specs=jax.tree.map(lambda o: pl.BlockSpec(memory_space=pltpu.VMEM), outs),
+        out_specs=out_specs,
         scratch_shapes=scratch,
-        compiler_params=pltpu.CompilerParams(vmem_limit_bytes=56 * 2**20),
+        compiler_params=pltpu.CompilerParams(vmem_limit_bytes=room * 2**20),
         cost_estimate=pl.CostEstimate(flops=work, bytes_accessed=0, transcendentals=0),
     )(*args)
 
@@ -173,18 +179,20 @@
             else:
                 acc[:, lanes] = block
                 started.add(a)
-    pieces = keep.shape[0]
-    size = chans // (2 * pieces)
+    length = keep.shape[0]
 
     def write(first, second):
         for a in range(3):
             for b in range(3):
                 for e in range(3):
-                    t = 9 * a + 3 * b + e
+                    top = (9 * a + 3 * b + e) * chans
                     lanes = slice((3 * a + b) * outs, (3 * a + b + 1) * outs)
-                    for target, top in ((first, e * chans), (second, e * chans + chans // 2)):
-                        block = acc[top : top + chans // 2, lanes]
-                        target[:, t * size : (t + 1) * size, :] = block.reshape(pieces, size, outs)
+                    cut = min(max(length - top, 0), chans)
+                    if cut > 0:
+                        first[top : top + cut, :] = acc[e * chans : e * chans + cut, lanes]
+                    if cut < chans:
+                        low = top + cut - length
+                        second[low : low + chans - cut, :] = acc[e * chans + cut : (e + 1) * chans, lanes]
 
     @pl.when(which[0] == 0)
     def _():
@@ -195,13 +203,13 @@
         write(send, keep)
 
 
-def run_first_backward(vol, before, after, spread, slope, which, pieces):
+def run_first_backward(vol, before, after, spread, slope, which):
     depth, rows, cols, chans = vol.shape
     wide, outs = 32, slope.shape[2]
     cells = rows * wide
     return call(
         first_backward,
-        (jax.ShapeDtypeStruct((pieces // 2, 27 * chans // pieces, outs), f32),) * 2,
+        (jax.ShapeDtypeStruct((27 * chans // 2, outs), f32),) * 2,
         [
             pltpu.VMEM((depth + 2, cells, 3 * chans), bf16),
             pltpu.VMEM((cells + 2 * front, chans), f32),
@@ -336,7 +344,7 @@
     )
 
 
-def second_backward(where, p0, p1, p2, p3, own, result, grad, p, flat, rows_ref, g):
+def second_backward(where, p0, p1, p2, p3, own, result, which, keep, send, p, flat, rows_ref, g, grad):
     parts = (p0, p1, p2, p3)
     planes, area, chans = p0.shape
     side, wide = 12, 16
@@ -369,42 +377,70 @@
                 grad[t * share : (t + 1) * share, :] = block
     grad[27 * share : 27 * share + 8, :] = result[:, 0:chans]
     grad[27 * share + 8 :, :] = jnp.zeros((8, chans), f32)
-
-
-def run_second_backward(where, parts, own, result):
+    half = keep.shape[0]
+    low = pl.multiple_of(which[0] * half, 8)
+    keep[...] = grad[pl.ds(low, half), :]
+    send[...] = grad[pl.ds(pl.multiple_of(half - low, 8), half), :]
+
+
+def run_second_backward(where, parts, own, result, which):
     planes, area, chans = parts[0].shape
     depth, cells, share = own.shape
     return call(
         second_backward,
-        jax.ShapeDtypeStruct((27 * share + 16, chans), f32),
+        (jax.ShapeDtypeStruct((27 * share // 2 + 8, chans), f32),) * 2,
         [
             pltpu.VMEM((depth + 2, cells, 3 * chans), bf16),
             pltpu.VMEM((area, chans), f32),
             pltpu.VMEM((cells + 2 * front, chans), f32),
             pltpu.VMEM((depth, cells, 3 * share), bf16),
+            pltpu.VMEM((27 * share + 16, chans), f32),
         ],
-        where, *parts, own, result, smem=(0,), work=heavy * 4,
-    )
-
-
-def spread_first(blocks, out):
-    pieces, rows, outs = blocks.shape
-    size = 8
-    for k in range(pieces):
-        out[:, k * size : (k + 1) * size, :] = blocks[k].astype(f32).reshape(rows // size, size, outs)
-
-
-def run_spread_first(blocks):
-    pieces, rows, outs = blocks.shape
-    steps, size = 9, rows // 27
-    out = pl.pallas_call(
-        spread_first,
-        grid=(steps,),
-        out_shape=jax.ShapeDtypeStruct((27, pieces * size, outs), f32),
-        in_specs=[pl.BlockSpec((pieces, rows // steps, outs), lambda i: (0, i, 0))],
-        out_specs=pl.BlockSpec((27 // steps, pieces * size, outs), lambda i: (i, 0, 0)),
-    )(blocks)
-    return out.reshape(-1, outs)
+        where, *parts, own, result, which, smem=(0, 7), work=heavy * 4,
+    )
+
+
+def join(r0, r1, r2, out):
+    rows = r0.shape[0]
+    for k, r in enumerate((r0, r1, r2)):
+        out[k * rows : (k + 1) * rows, :] = r[...]
+
+
+def run_join(parts):
+    rows, cols = parts[0].shape
+    return call(join, jax.ShapeDtypeStruct((3 * rows, cols), bf16), [], *parts)
+
+
+def merge_half(which, kept, came, keep, send):
+    half = keep.shape[0]
+    low = pl.multiple_of(which[0] * half, 8)
+    high = pl.multiple_of(half - low, 8)
+    keep[...] = kept[pl.ds(low, half), :] + came[pl.ds(low, half), :]
+    send[...] = (kept[pl.ds(high, half), :] + came[pl.ds(high, half), :]).astype(bf16)
+
+
+def run_merge_half(which, kept, came):
+    rows, cols = kept.shape
+    outs = tuple(jax.ShapeDtypeStruct((rows // 2, cols), kind) for kind in (f32, bf16))
+    return call(merge_half, outs, [], which, kept, came, smem=(0,))
+
+
+def merge_blocks(which, kept, came, keep, s1, s2, s3):
+    size = keep.shape[0]
+
+    def block(step):
+        low = pl.multiple_of((which[0] + step) % 4 * size, 8)
+        return kept[pl.ds(low, size), :] + came[pl.ds(low, size), :].astype(f32)
+
+    keep[...] = block(0)
+    for step, send in ((1, s1), (2, s2), (3, s3)):
+        send[...] = block(step).astype(bf16)
+
+
+def run_merge_blocks(which, kept, came):
+    rows, cols = kept.shape
+    outs = tuple(jax.ShapeDtypeStruct((rows // 4, cols), kind) for kind in (f32, bf16, bf16, bf16))
+    return call(merge_blocks, outs, [], which, kept, came, smem=(0,))
 
 
 def spread_second(packed, out, head):
@@ -412,22 +448,27 @@
     share = out.shape[0]
     for t in range(27):
         out[:, t * chans : (t + 1) * chans] = packed[t * share : (t + 1) * share, :]
-    head[...] = packed[27 * share : 27 * share + 8, :]
-
-
-def run_spread_second(packed, share):
+    head[...] = packed[27 * share : 27 * share + head.shape[0], 0:share]
+
+
+def run_spread_second(packed, share, outs):
     rows, chans = packed.shape
     return call(
         spread_second,
-        (jax.ShapeDtypeStruct((share, 27 * chans), f32), jax.ShapeDtypeStruct((8, chans), f32)),
+        (jax.ShapeDtypeStruct((share, 27 * chans), f32), jax.ShapeDtypeStruct((outs, share), f32)),
         [],
         packed,
+        work=heavy * 2,
     )
 
 
 def turn(x, axis, step):
     size = lax.axis_size(axis)
     return lax.ppermute(x, axis, [(i, (i + step) % size) for i in range(size)])
+
+
+def paired(x, axis, bits):
+    return lax.ppermute(x, axis, [(i, i ^ bits) for i in range(lax.axis_size(axis))])
 
 
 def direct(axis):
@@ -475,7 +516,7 @@
     columns = x.shape[1]
     x = scattered_sum(x, "rep", jnp.float32)
     if direct("dp"):
-        x = gathered(x.astype(jnp.bfloat16), "dp").astype(jnp.float32).sum(0)
+        x = gathered(x, "dp").sum(0)
     else:
         x = lax.psum(x, "dp")
     return gathered(x, "rep").reshape(-1, columns)
@@ -597,12 +638,12 @@
     return (first_total, second_total, head_total)
 
 
-def neighbours(grid):
+def neighbours(first, last):
     devices = lax.axis_size("space")
     up = [(i, i + 1) for i in range(devices - 1)]
     down = [(j, i) for i, j in up]
-    before = lax.ppermute(grid[-1:], "space", up)
-    after = lax.ppermute(grid[:1], "space", down)
+    before = lax.ppermute(last, "space", up)
+    after = lax.ppermute(first, "space", down)
     return before, after
 
 
@@ -617,32 +658,47 @@
     rep = lax.axis_index("rep")
     copy = 2 * lax.axis_index("dp") + rep
     where = jnp.stack([(place - k) % 4 for k in range(4)] + [copy ^ k for k in range(4)])
-    before, after = neighbours(grid)
     turned = second_kernel.T
+    before, after = neighbours(grid[:1], grid[-1:])
     piece = lax.dynamic_slice_in_dim(turned, copy * (share // 4), share // 4, 0)
-    others = jnp.concatenate([turn(piece, "space", k) for k in range(1, 4)], axis=0)
-    across = turn(others, "dp", 1)
-    pieces = [others, turn(others, "rep", 1), across, turn(across, "rep", 1)]
-    pooled, slope = run_first_forward(grid, before, after, first_kernel)
-    parts = [pooled] + [turn(pooled, "space", k) for k in range(1, 4)]
+    others = [turn(piece, "space", k) for k in range(1, 4)]
     blocks = head_weights.T.reshape(outs, 4, share)
     head = jnp.concatenate([lax.dynamic_index_in_dim(blocks, (place - k) % 4, 1, False) for k in range(4)], axis=1)
     head = jnp.pad(head, ((0, 8 - outs), (0, 0)))
     wanted = jnp.pad(jnp.broadcast_to(targets[0][:, None], (outs, 128)), ((0, 8 - outs), (0, 0)))
+    pooled, slope = run_first_forward(grid, before, after, first_kernel)
+    pooled, *others = lax.optimization_barrier([pooled] + others)
+    others = run_join(others)
+    across = turn(others, "dp", 1)
+    parts = [pooled] + [turn(pooled, "space", k) for k in range(1, 4)]
+    across, *parts = lax.optimization_barrier([across] + parts)
+    pieces = [others, turn(others, "rep", 1), across, turn(across, "rep", 1)]
     pooled_grad, own, result = run_second_layer(where, parts, turned, pieces, head, wanted)
-    keep, send = run_first_backward(grid, before, after, pooled_grad, slope, rep[None], 16)
-    x = keep + turn(send, "rep", 1)
-    x, own = lax.optimization_barrier((x, own))
-    second_part = run_second_backward(where, parts, own, result)
-    x = x.reshape(-1, x.shape[2])
-    x = scattered_sum(x, "dp", bf16)
-    x, second_part = lax.optimization_barrier((x, second_part))
-    x = scattered_sum(x, "space", bf16).astype(bf16)
-    for axis in ("space", "dp", "rep"):
+    keep, send = run_first_backward(grid, before, after, pooled_grad, slope, rep[None])
+    keep, send = run_merge_half(lax.axis_index("dp")[None], keep, turn(send, "rep", 1))
+    arrived = turn(send, "dp", 1)
+    keep, own = lax.optimization_barrier((keep, own))
+    kept, sent = run_second_backward(where, parts, own, result, rep[None])
+    x, *sends = run_merge_blocks(place[None], keep, arrived)
+    sends[0], sends[1], sends[2], kept, sent = lax.optimization_barrier((*sends, kept, sent))
+    second = kept + turn(sent, "rep", 1)
+    for k in (1, 3, 2):
+        x = x + turn(sends[k - 1], "space", k).astype(f32)
+    x = x.astype(bf16)
+    second = second + turn(second, "dp", 1)
+    whole = jnp.zeros((4,) + x.shape, bf16)
+    for k in (0, 1, 3, 2):
+        part = turn(x, "space", k) if k else x
+        if k == 1:
+            part, second = lax.optimization_barrier((part, second))
+        whole = lax.dynamic_update_index_in_dim(whole, part, (place - k) % 4, 0)
+    x = whole.reshape(-1, x.shape[1])
+    second = gathered(second, "rep").reshape(-1, second.shape[1])
+    second_total, head_total = run_spread_second(second, share, outs)
+    for axis in ("dp", "rep"):
         x = gathered(x, axis).reshape(-1, x.shape[1])
-    first_total = run_spread_first(x.reshape((16, -1) + x.shape[1:]))
-    second_total, head_total = run_spread_second(total_second(second_part), share)
-    return (first_total, second_total.T, head_total[:outs, :share].T)
+    first_total = x.astype(f32)
+    return (first_total, second_total.T, head_total.T)
 
 
 def solution(mesh):

time: 117 us -> 87.5 us (0.75)
  Pallas kernels: 36 us -> 20.4 us
  waiting for transfers between devices: 37.8 us -> 27.5 us
  local copies, waits for them, and re-layouts: 9.39 us -> 6.13 us
    pallas_call x6 -> x8, Pallas kernels: 36 us -> 20.4 us  [call(): pl.pallas_call(body, out_shape=outs, in_specs=specs, out_specs=out_specs,...]
    ppermute x22, waiting for transfers between devices: 34.7 us -> 27.4 us  [turn(): return lax.ppermute(x, axis, [(i, (i + step) % size) for i in range(size)])]
    ppermute x2, waiting for transfers between devices: 3.09 us -> 0.01 us  [the longest x1 0.01 us: neighbours(): before = lax.ppermute(last, 'space', up)]
    convert_element_type x0 -> x1, other arithmetic: none -> 1.38 us  [shards(): first_total = x.astype(f32)]
    pad x2, local copies, waits for them, and re-layouts: 1.41 us -> 0.07 us  [shards(): jnp.pad(jnp.broadcast_to(targets[0][:, None], (outs, 128)), ((0, 8 - outs...]
    transpose x1 -> x0, local copies, waits for them, and re-layouts: 1.25 us -> none  [shards(): return (first_total, second_total.T, head_total[:outs, :share].T)]
    add x2, other arithmetic: 1.3 us -> 0.09 us  [the longest x1 0.05 us: shards(): second = kept + turn(sent, 'rep', 1)]
    unnamed x26 -> x16, local copies, waits for them, and re-layouts: 2.66 us -> 3.39 us
  transfers between devices with their start and end apart: 24 -> 24, of which waited for: 15 -> 12; matrix products, arithmetic and copies ran while one was open for 4% -> 2% of each run, Pallas kernels for 16% -> 11%
where the time goes in v1:
time: 87.5 us; the launch traced here: 87.2 us
  starting transfers between devices  30.5 us (35%)
  waiting for transfers between devices  27.5 us (31%)
  Pallas kernels  20.4 us (23%)
  local copies, waits for them, and re-layouts  6.13 us (7%)
  other arithmetic  1.61 us (2%)
  between operations  1.05 us (1%)
    ppermute x22, waiting for transfers between devices, turn(): return lax.ppermute(x, axis, [(i, (i + step) % size) for i in range(size)])  27.4 us
    ppermute x22, starting transfers between devices, turn(): return lax.ppermute(x, axis, [(i, (i + step) % size) for i in range(size)])  24.3 us
    pallas_call x8, Pallas kernels, call(): pl.pallas_call(body, out_shape=outs, in_specs=specs, out_specs=out_specs,...  20.4 us
    ppermute x1, starting transfers between devices, neighbours(): before = lax.ppermute(last, 'space', up)  4.94 us
    unnamed x16, local copies, waits for them, and re-layouts  3.39 us
  transfers between devices with their start and end apart: 24, of which 12 were waited for; matrix products, arithmetic and copies ran while one was open for 2% of the time, Pallas kernels for 11%

profile of v1, /device:TPU:0, one launch (start us, length us, event | category | flops | bytes accessed | tf_op | source)
XLA Modules:
  0.0 87.2 jit_solution(10514312300289348236)
XLA Ops:
  0.6 1.0 %slice_bitcast_fusion = (bf16[1,24,24,128]{3,2,1,0:T(8,128)(2,1)S(1)}, bf16[1,24,24,128]{3,2,1,0:T(8,128)(2,1)S(1)}) fusion(bf16[1,4,24,24,128]{4,3,2,1,0:T(8,128)(2,1)} %param.5), kind=kLoop, calls=%fused_computation.7 | loop fusion | bytes 589824 | tf_op jit(solution)/shard_map/slice | solution.py:662
  1.6 4.9 %collective-permute-start = (bf16[1,24,24,128]{3,2,1,0:T(8,128)(2,1)S(1)}, bf16[1,24,24,128]{3,2,1,0:T(8,128)(2,1)S(1)}, u32[]{:S(2)}, u32[]{:S(2)}) collective-permute-start(bf16[1,24,24,128]{3,2,1,0:T(8,128)(2,1)S(1)} %get-tuple-element.76), channel_id=1, source_target_pairs={{0,4},{4,8},{8,12},{1,5},{5,9},{9,13},{2,6},{6,10},{10,14},{3,7},{... | collective-permute-start | bytes 442376 | tf_op jit(solution)/shard_map/ppermute | solution.py:645
  6.6 1.3 %collective-permute-start.1 = (bf16[1,24,24,128]{3,2,1,0:T(8,128)(2,1)S(1)}, bf16[1,24,24,128]{3,2,1,0:T(8,128)(2,1)S(1)}, u32[]{:S(2)}, u32[]{:S(2)}) collective-permute-start(bf16[1,24,24,128]{3,2,1,0:T(8,128)(2,1)S(1)} %get-tuple-element.75), channel_id=1, source_target_pairs={{4,0},{8,4},{12,8},{5,1},{9,5},{13,9},{6,2},{10,6},{14,10},{7,3},{... | collective-permute-start | bytes 442376 | tf_op jit(solution)/shard_map/ppermute | solution.py:646
  7.9 0.9 %dynamic-slice_bitcast_fusion = bf16[16,3456]{1,0:T(8,128)(2,1)S(1)} fusion(bf16[3456,64]{0,1:T(8,128)(2,1)} %param.8, s32[]{:T(128)S(6)} %select_n.97), kind=kLoop, calls=%fused_computation.10 | loop fusion | bytes 221188 | tf_op jit(solution)/shard_map/dynamic_slice | solution.py:663
  8.8 2.6 %collective-permute-start.2 = (bf16[16,3456]{1,0:T(8,128)(2,1)S(1)}, bf16[16,3456]{1,0:T(8,128)(2,1)S(1)}, u32[]{:S(2)}, u32[]{:S(2)}) collective-permute-start(bf16[16,3456]{1,0:T(8,128)(2,1)S(1)} %dynamic-slice_bitcast_fusion), channel_id=1, source_target_pairs={{0,4},{4,8},{8,12},{12,0},{1,5},{5,9},{9,13},{13,1},{2,6},{6,10},{... | collective-permute-start | bytes 331784 | tf_op jit(solution)/shard_map/ppermute | solution.py:467
  11.5 2.6 %collective-permute-start.3 = (bf16[16,3456]{1,0:T(8,128)(2,1)S(1)}, bf16[16,3456]{1,0:T(8,128)(2,1)S(1)}, u32[]{:S(2)}, u32[]{:S(2)}) collective-permute-start(bf16[16,3456]{1,0:T(8,128)(2,1)S(1)} %dynamic-slice_bitcast_fusion), channel_id=1, source_target_pairs={{0,8},{4,12},{8,0},{12,4},{1,9},{5,13},{9,1},{13,5},{2,10},{6,14},... | collective-permute-start | bytes 331784 | tf_op jit(solution)/shard_map/ppermute | solution.py:467
  14.0 1.3 %collective-permute-start.4 = (bf16[16,3456]{1,0:T(8,128)(2,1)S(1)}, bf16[16,3456]{1,0:T(8,128)(2,1)S(1)}, u32[]{:S(2)}, u32[]{:S(2)}) collective-permute-start(bf16[16,3456]{1,0:T(8,128)(2,1)S(1)} %dynamic-slice_bitcast_fusion), channel_id=1, source_target_pairs={{0,12},{4,0},{8,4},{12,8},{1,13},{5,1},{9,5},{13,9},{2,14},{6,2},{... | collective-permute-start | bytes 331784 | tf_op jit(solution)/shard_map/ppermute | solution.py:467
  15.4 1.1 %copy-done = bf16[1,4,24,24,128]{4,3,2,1,0:T(8,128)(2,1)S(1)} copy-done((bf16[1,4,24,24,128]{4,3,2,1,0:T(8,128)(2,1)S(1)}, bf16[1,4,24,24,128]{4,3,2,1,0:T(8,128)(2,1)}, u32[]{:S(2)}) %copy-start) | copy-done | bytes 589848
  16.5 1.2 %copy-done.3 = bf16[3456,128]{1,0:T(8,128)(2,1)S(1)} copy-done((bf16[3456,128]{1,0:T(8,128)(2,1)S(1)}, bf16[3456,128]{1,0:T(8,128)(2,1)}, u32[]{:S(2)}) %copy-start.3) | copy-done | bytes 884760
  17.6 5.8 %shard_map.76 = (bf16[2,144,128]{2,1,0:T(8,128)(2,1)S(1)}, f32[4,768,128]{2,1,0:T(8,128)S(1)}) custom-call(bf16[4,24,24,128]{3,2,1,0:T(8,128)(2,1)S(1)} %bitcast.64, bf16[1,24,24,128]{3,2,1,0:T(8,128)(2,1)S(1)} %collective-permute-done.before, bf16[1,24,24,128]{3,2,1,0:T(8,128)(2,1)S(1)} %collective-permute-done.1.after, bf16[3456,128]{1,0:T(8,128)(2,1)S(1)} %copy-done.3), custom_call_target="tpu_custom_call" | custom-call | flops 8000000000 | tf_op jit(solution)/shard_map/pallas_call | solution.py:24
  23.4 1.1 %copy-done.4 = f32[4,768,128]{2,1,0:T(8,128)} copy-done((f32[4,768,128]{2,1,0:T(8,128)}, f32[4,768,128]{2,1,0:T(8,128)S(1)}, u32[]{:S(2)}) %copy-start.4) | copy-done | bytes 1572888
  24.6 1.6 %collective-permute-start.5 = (bf16[48,3456]{1,0:T(8,128)(2,1)S(1)}, bf16[48,3456]{1,0:T(8,128)(2,1)S(1)}, u32[]{:S(2)}, u32[]{:S(2)}) collective-permute-start(bf16[48,3456]{1,0:T(8,128)(2,1)S(1)} %shard_map.77.w1), channel_id=1, source_target_pairs={{0,2},{2,0},{1,3},{3,1},{4,6},{6,4},{5,7},{7,5},{8,10},{10,8},{9,1... | collective-permute-start | bytes 995336 | tf_op jit(solution)/shard_map/ppermute | solution.py:467
  26.2 2.2 %collective-permute-start.6 = (bf16[2,144,128]{2,1,0:T(8,128)(2,1)S(1)}, bf16[2,144,128]{2,1,0:T(8,128)(2,1)S(1)}, u32[]{:S(2)}, u32[]{:S(2)}) collective-permute-start(bf16[2,144,128]{2,1,0:T(8,128)(2,1)S(1)} %get-tuple-element.43.p0), channel_id=1, source_target_pairs={{0,4},{4,8},{8,12},{12,0},{1,5},{5,9},{9,13},{13,1},{2,6},{6,10},{... | collective-permute-start | bytes 221192 | tf_op jit(solution)/shard_map/ppermute | solution.py:467
  28.3 0.3 collective-permute-start.7
  28.6 2.9 %collective-permute-start.8 = (bf16[2,144,128]{2,1,0:T(8,128)(2,1)S(1)}, bf16[2,144,128]{2,1,0:T(8,128)(2,1)S(1)}, u32[]{:S(2)}, u32[]{:S(2)}) collective-permute-start(bf16[2,144,128]{2,1,0:T(8,128)(2,1)S(1)} %get-tuple-element.43.p0), channel_id=1, source_target_pairs={{0,12},{4,0},{8,4},{12,8},{1,13},{5,1},{9,5},{13,9},{2,14},{6,2},{... | collective-permute-start | bytes 221192 | tf_op jit(solution)/shard_map/ppermute | solution.py:467
  31.6 0.9 %collective-permute-done.6.p1 = bf16[2,144,128]{2,1,0:T(8,128)(2,1)S(1)} collective-permute-done((bf16[2,144,128]{2,1,0:T(8,128)(2,1)S(1)}, bf16[2,144,128]{2,1,0:T(8,128)(2,1)S(1)}, u32[]{:S(2)}, u32[]{:S(2)}) %collective-permute-start.6) | collective-permute-done | bytes 73760 | tf_op jit(solution)/shard_map/ppermute | solution.py:467
  32.5 1.9 %collective-permute-done.7.p2 = bf16[2,144,128]{2,1,0:T(8,128)(2,1)S(1)} collective-permute-done((bf16[2,144,128]{2,1,0:T(8,128)(2,1)S(1)}, bf16[2,144,128]{2,1,0:T(8,128)(2,1)S(1)}, u32[]{:S(2)}, u32[]{:S(2)}) %collective-permute-start.7) | collective-permute-done | bytes 73760 | tf_op jit(solution)/shard_map/ppermute | solution.py:467
  34.5 0.1 reshape.26
  34.6 0.1 stack.35.where
  34.7 0.1 select_maximum_fusion.head
  34.8 1.3 %collective-permute-done.10.w4 = bf16[48,3456]{1,0:T(8,128)(2,1)S(1)} collective-permute-done((bf16[48,3456]{1,0:T(8,128)(2,1)S(1)}, bf16[48,3456]{1,0:T(8,128)(2,1)S(1)}, u32[]{:S(2)}, u32[]{:S(2)}) %collective-permute-start.10) | collective-permute-done | bytes 331808 | tf_op jit(solution)/shard_map/ppermute | solution.py:467
  36.0 0.1 pad.12.wanted
  36.1 7.0 %shard_map.78 = (f32[2,192,128]{2,1,0:T(8,128)S(1)}, bf16[8,192,64]{2,1,0:T(8,128)(2,1)S(1)}, f32[8,256]{1,0:T(8,128)S(1)}) custom-call(s32[8]{0:T(128)S(1)} %stack.35.where, bf16[2,144,128]{2,1,0:T(8,128)(2,1)S(1)} %get-tuple-element.43.p0, bf16[2,144,128]{2,1,0:T(8,128)(2,1)S(1)} %collective-permute-done.6.p1, ...), custom_call_target="tpu_custom_call" | custom-call | flops 8000000000 | tf_op jit(solution)/shard_map/pallas_call | solution.py:24
  43.1 4.0 %shard_map.79 = (f32[1728,128]{1,0:T(8,128)S(1)}, f32[1728,128]{1,0:T(8,128)S(1)}) custom-call(bf16[4,24,24,128]{3,2,1,0:T(8,128)(2,1)S(1)} %bitcast.65, bf16[1,24,24,128]{3,2,1,0:T(8,128)(2,1)S(1)} %collective-permute-done.before, bf16[1,24,24,128]{3,2,1,0:T(8,128)(2,1)S(1)} %collective-permute-done.1.after, f32[2,192,128]{2,1,0:T(8,128)S(1)} %get-tuple-element.48.spread, ...), custom_call_target="tpu_custom_call" | custom-call | flops 7000000000 | tf_op jit(solution)/shard_map/pallas_call | solution.py:24
  47.2 0.2 collective-permute-start.11
  47.4 2.3 %collective-permute-done.11.came = f32[1728,128]{1,0:T(8,128)S(1)} collective-permute-done((f32[1728,128]{1,0:T(8,128)S(1)}, f32[1728,128]{1,0:T(8,128)S(1)}, u32[]{:S(2)}, u32[]{:S(2)}) %collective-permute-start.11) | collective-permute-done | bytes 884768 | tf_op jit(solution)/shard_map/ppermute | solution.py:467
  49.6 0.1 shard_map.80
  49.7 0.6 collective-permute-start.12
  50.3 2.5 %shard_map.82 = (f32[872,128]{1,0:T(8,128)S(1)}, f32[872,128]{1,0:T(8,128)S(1)}) custom-call(s32[8]{0:T(128)S(1)} %stack.35.where, bf16[2,144,128]{2,1,0:T(8,128)(2,1)S(1)} %get-tuple-element.43.p0, bf16[2,144,128]{2,1,0:T(8,128)(2,1)S(1)} %collective-permute-done.6.p1, bf16[2,144,128]{2,1,0:T(8,128)(2,1)S(1)} %collective-permute-done.7.p2, ...), custom_call_target="tpu_custom_call" | custom-call | flops 4000000000 | tf_op jit(solution)/shard_map/pallas_call | solution.py:24
  52.8 4.4 %collective-permute-done.12.came = bf16[864,128]{1,0:T(8,128)(2,1)S(1)} collective-permute-done((bf16[864,128]{1,0:T(8,128)(2,1)S(1)}, bf16[864,128]{1,0:T(8,128)(2,1)S(1)}, u32[]{:S(2)}, u32[]{:S(2)}) %collective-permute-start.12) | collective-permute-done | bytes 221216 | tf_op jit(solution)/shard_map/ppermute | solution.py:467
  57.3 0.1 collective-permute-start.17
  57.4 1.8 %collective-permute-done.17 = f32[872,128]{1,0:T(8,128)S(1)} collective-permute-done((f32[872,128]{1,0:T(8,128)S(1)}, f32[872,128]{1,0:T(8,128)S(1)}, u32[]{:S(2)}, u32[]{:S(2)}) %collective-permute-start.17) | collective-permute-done | bytes 446496 | tf_op jit(solution)/shard_map/ppermute | solution.py:467
  59.2 0.6 collective-permute-start.18
  59.8 1.4 %collective-permute-start.13 = (bf16[216,128]{1,0:T(8,128)(2,1)S(1)}, bf16[216,128]{1,0:T(8,128)(2,1)S(1)}, u32[]{:S(2)}, u32[]{:S(2)}) collective-permute-start(bf16[216,128]{1,0:T(8,128)(2,1)S(1)} %get-tuple-element.64), channel_id=1, source_target_pairs={{0,4},{4,8},{8,12},{12,0},{1,5},{5,9},{9,13},{13,1},{2,6},{6,10},{... | collective-permute-start | bytes 165896 | tf_op jit(solution)/shard_map/ppermute | solution.py:467
  61.2 2.5 %collective-permute-start.14 = (bf16[216,128]{1,0:T(8,128)(2,1)S(1)}, bf16[216,128]{1,0:T(8,128)(2,1)S(1)}, u32[]{:S(2)}, u32[]{:S(2)}) collective-permute-start(bf16[216,128]{1,0:T(8,128)(2,1)S(1)} %get-tuple-element.65), channel_id=1, source_target_pairs={{0,12},{4,0},{8,4},{12,8},{1,13},{5,1},{9,5},{13,9},{2,14},{6,2},{... | collective-permute-start | bytes 165896 | tf_op jit(solution)/shard_map/ppermute | solution.py:467
  63.7 2.5 %collective-permute-done.13 = bf16[216,128]{1,0:T(8,128)(2,1)S(1)} collective-permute-done((bf16[216,128]{1,0:T(8,128)(2,1)S(1)}, bf16[216,128]{1,0:T(8,128)(2,1)S(1)}, u32[]{:S(2)}, u32[]{:S(2)}) %collective-permute-start.13) | collective-permute-done | bytes 55328 | tf_op jit(solution)/shard_map/ppermute | solution.py:467
  66.3 2.6 %collective-permute-done.15 = bf16[216,128]{1,0:T(8,128)(2,1)S(1)} collective-permute-done((bf16[216,128]{1,0:T(8,128)(2,1)S(1)}, bf16[216,128]{1,0:T(8,128)(2,1)S(1)}, u32[]{:S(2)}, u32[]{:S(2)}) %collective-permute-start.15) | collective-permute-done | bytes 55328 | tf_op jit(solution)/shard_map/ppermute | solution.py:467
  69.1 3.7 %collective-permute-start.19 = (bf16[216,128]{1,0:T(8,128)(2,1)S(1)}, bf16[216,128]{1,0:T(8,128)(2,1)S(1)}, u32[]{:S(2)}, u32[]{:S(2)}) collective-permute-start(bf16[216,128]{1,0:T(8,128)(2,1)S(1)} %get-tuple-element.74), channel_id=1, source_target_pairs={{0,12},{4,0},{8,4},{12,8},{1,13},{5,1},{9,5},{13,9},{2,14},{6,2},{... | collective-permute-start | bytes 165896 | tf_op jit(solution)/shard_map/ppermute | solution.py:467
  72.9 2.5 %collective-permute-done.16 = bf16[216,128]{1,0:T(8,128)(2,1)S(1)} collective-permute-done((bf16[216,128]{1,0:T(8,128)(2,1)S(1)}, bf16[216,128]{1,0:T(8,128)(2,1)S(1)}, u32[]{:S(2)}, u32[]{:S(2)}) %collective-permute-start.16) | collective-permute-done | bytes 55328 | tf_op jit(solution)/shard_map/ppermute | solution.py:467
  75.4 2.4 %collective-permute-done.20 = bf16[216,128]{1,0:T(8,128)(2,1)S(1)} collective-permute-done((bf16[216,128]{1,0:T(8,128)(2,1)S(1)}, bf16[216,128]{1,0:T(8,128)(2,1)S(1)}, u32[]{:S(2)}, u32[]{:S(2)}) %collective-permute-start.20) | collective-permute-done | bytes 55328 | tf_op jit(solution)/shard_map/ppermute | solution.py:467
  77.9 1.6 %collective-permute-start.21 = (bf16[864,128]{1,0:T(8,128)(2,1)S(1)}, bf16[864,128]{1,0:T(8,128)(2,1)S(1)}, u32[]{:S(2)}, u32[]{:S(2)}) collective-permute-start(bf16[864,128]{1,0:T(8,128)(2,1)S(1)} %bitcast.69), channel_id=1, source_target_pairs={{0,2},{2,0},{1,3},{3,1},{4,6},{6,4},{5,7},{7,5},{8,10},{10,8},{9,1... | collective-permute-start | bytes 663560 | tf_op jit(solution)/shard_map/ppermute | solution.py:467
  79.6 4.2 %collective-permute-done.21 = bf16[864,128]{1,0:T(8,128)(2,1)S(1)} collective-permute-done((bf16[864,128]{1,0:T(8,128)(2,1)S(1)}, bf16[864,128]{1,0:T(8,128)(2,1)S(1)}, u32[]{:S(2)}, u32[]{:S(2)}) %collective-permute-start.21) | collective-permute-done | bytes 221216 | tf_op jit(solution)/shard_map/ppermute | solution.py:467
  83.9 0.1 collective-permute-start.22
  84.0 0.1 broadcast_in_dim.61
  84.1 0.1 bitcast_dynamic-update-slice_fusion.3
  84.2 1.0 %shard_map.83 = (f32[64,3456]{1,0:T(8,128)}, f32[4,64]{1,0:T(4,128)}) custom-call(f32[1744,128]{1,0:T(8,128)S(1)} %bitcast.63), custom_call_target="tpu_custom_call" | custom-call | flops 2000000000 | tf_op jit(solution)/shard_map/pallas_call | solution.py:24
  85.2 0.6 collective-permute-done.22
  85.8 1.4 %bitcast_convert_fusion = f32[3456,128]{1,0:T(8,128)} fusion(bf16[2,1728,128]{2,1,0:T(8,128)(2,1)S(1)} %bitcast_dynamic-update-slice_fusion.2), kind=kLoop, calls=%fused_computation | loop fusion | flops 442368 | bytes 2654208 | tf_op jit(solution)/shard_map/convert_element_type | solution.py:700
  (49 shorter events, 0.8 us)
Async XLA Ops:
  1.6 13.7 %collective-permute-start = (bf16[1,24,24,128]{3,2,1,0:T(8,128)(2,1)S(1)}, bf16[1,24,24,128]{3,2,1,0:T(8,128)(2,1)S(1)}, u32[]{:S(2)}, u32[]{:S(2)}) collective-permute-start(bf16[1,24,24,128]{3,2,1,0:T(8,128)(2,1)S(1)} %get-tuple-element.76), channel_id=1, source_target_pairs={{0,4},{4,8},{8,12},{1,5},{5,9},{9,13},{2,6},{6,10},{10,14},{3,7},{... | collective-permute-start | bytes 442376 | tf_op jit(solution)/shard_map/ppermute | solution.py:645
  6.6 8.8 %collective-permute-start.1 = (bf16[1,24,24,128]{3,2,1,0:T(8,128)(2,1)S(1)}, bf16[1,24,24,128]{3,2,1,0:T(8,128)(2,1)S(1)}, u32[]{:S(2)}, u32[]{:S(2)}) collective-permute-start(bf16[1,24,24,128]{3,2,1,0:T(8,128)(2,1)S(1)} %get-tuple-element.75), channel_id=1, source_target_pairs={{4,0},{8,4},{12,8},{5,1},{9,5},{13,9},{6,2},{10,6},{14,10},{7,3},{... | collective-permute-start | bytes 442376 | tf_op jit(solution)/shard_map/ppermute | solution.py:646
  8.8 15.8 %collective-permute-start.2 = (bf16[16,3456]{1,0:T(8,128)(2,1)S(1)}, bf16[16,3456]{1,0:T(8,128)(2,1)S(1)}, u32[]{:S(2)}, u32[]{:S(2)}) collective-permute-start(bf16[16,3456]{1,0:T(8,128)(2,1)S(1)} %dynamic-slice_bitcast_fusion), channel_id=1, source_target_pairs={{0,4},{4,8},{8,12},{12,0},{1,5},{5,9},{9,13},{13,1},{2,6},{6,10},{... | collective-permute-start | bytes 331784 | tf_op jit(solution)/shard_map/ppermute | solution.py:467
  11.5 13.1 %collective-permute-start.3 = (bf16[16,3456]{1,0:T(8,128)(2,1)S(1)}, bf16[16,3456]{1,0:T(8,128)(2,1)S(1)}, u32[]{:S(2)}, u32[]{:S(2)}) collective-permute-start(bf16[16,3456]{1,0:T(8,128)(2,1)S(1)} %dynamic-slice_bitcast_fusion), channel_id=1, source_target_pairs={{0,8},{4,12},{8,0},{12,4},{1,9},{5,13},{9,1},{13,5},{2,10},{6,14},... | collective-permute-start | bytes 331784 | tf_op jit(solution)/shard_map/ppermute | solution.py:467
  14.0 10.5 %collective-permute-start.4 = (bf16[16,3456]{1,0:T(8,128)(2,1)S(1)}, bf16[16,3456]{1,0:T(8,128)(2,1)S(1)}, u32[]{:S(2)}, u32[]{:S(2)}) collective-permute-start(bf16[16,3456]{1,0:T(8,128)(2,1)S(1)} %dynamic-slice_bitcast_fusion), channel_id=1, source_target_pairs={{0,12},{4,0},{8,4},{12,8},{1,13},{5,1},{9,5},{13,9},{2,14},{6,2},{... | collective-permute-start | bytes 331784 | tf_op jit(solution)/shard_map/ppermute | solution.py:467
  15.4 1.1 %copy-start = (bf16[1,4,24,24,128]{4,3,2,1,0:T(8,128)(2,1)S(1)}, bf16[1,4,24,24,128]{4,3,2,1,0:T(8,128)(2,1)}, u32[]{:S(2)}) copy-start(bf16[1,4,24,24,128]{4,3,2,1,0:T(8,128)(2,1)} %param.5) | copy-start | bytes 1769476
  16.5 1.2 %copy-start.3 = (bf16[3456,128]{1,0:T(8,128)(2,1)S(1)}, bf16[3456,128]{1,0:T(8,128)(2,1)}, u32[]{:S(2)}) copy-start(bf16[3456,128]{1,0:T(8,128)(2,1)} %kernel.1) | copy-start | bytes 2654212
  17.6 16.9 %copy-start.6 = (f32[256,4]{0,1:T(4,128)S(1)}, f32[256,4]{0,1:T(4,128)}, u32[]{:S(2)}) copy-start(f32[256,4]{0,1:T(4,128)} %param.9) | copy-start | bytes 12292
  17.6 16.9 %copy-start.7 = (f32[1,4]{1,0:T(1,128)S(1)}, f32[1,4]{1,0:T(1,128)}, u32[]{:S(2)}) copy-start(f32[1,4]{1,0:T(1,128)} %param.6) | copy-start | bytes 52
  17.6 18.5 %copy-start.2 = (bf16[3456,64]{0,1:T(8,128)(2,1)S(1)}, bf16[3456,64]{0,1:T(8,128)(2,1)}, u32[]{:S(2)}) copy-start(bf16[3456,64]{0,1:T(8,128)(2,1)} %param.8) | copy-start | bytes 1327108
  23.4 1.1 %copy-start.4 = (f32[4,768,128]{2,1,0:T(8,128)}, f32[4,768,128]{2,1,0:T(8,128)S(1)}, u32[]{:S(2)}) copy-start(f32[4,768,128]{2,1,0:T(8,128)S(1)} %get-tuple-element.49.slope) | copy-start | bytes 4718596
  24.6 9.8 %collective-permute-start.5 = (bf16[48,3456]{1,0:T(8,128)(2,1)S(1)}, bf16[48,3456]{1,0:T(8,128)(2,1)S(1)}, u32[]{:S(2)}, u32[]{:S(2)}) collective-permute-start(bf16[48,3456]{1,0:T(8,128)(2,1)S(1)} %shard_map.77.w1), channel_id=1, source_target_pairs={{0,2},{2,0},{1,3},{3,1},{4,6},{6,4},{5,7},{7,5},{8,10},{10,8},{9,1... | collective-permute-start | bytes 995336 | tf_op jit(solution)/shard_map/ppermute | solution.py:467
  26.2 6.3 %collective-permute-start.6 = (bf16[2,144,128]{2,1,0:T(8,128)(2,1)S(1)}, bf16[2,144,128]{2,1,0:T(8,128)(2,1)S(1)}, u32[]{:S(2)}, u32[]{:S(2)}) collective-permute-start(bf16[2,144,128]{2,1,0:T(8,128)(2,1)S(1)} %get-tuple-element.43.p0), channel_id=1, source_target_pairs={{0,4},{4,8},{8,12},{12,0},{1,5},{5,9},{9,13},{13,1},{2,6},{6,10},{... | collective-permute-start | bytes 221192 | tf_op jit(solution)/shard_map/ppermute | solution.py:467
  28.3 6.0 %collective-permute-start.7 = (bf16[2,144,128]{2,1,0:T(8,128)(2,1)S(1)}, bf16[2,144,128]{2,1,0:T(8,128)(2,1)S(1)}, u32[]{:S(2)}, u32[]{:S(2)}) collective-permute-start(bf16[2,144,128]{2,1,0:T(8,128)(2,1)S(1)} %get-tuple-element.43.p0), channel_id=1, source_target_pairs={{0,8},{4,12},{8,0},{12,4},{1,9},{5,13},{9,1},{13,5},{2,10},{6,14},... | collective-permute-start | bytes 221192 | tf_op jit(solution)/shard_map/ppermute | solution.py:467
  28.6 5.8 %collective-permute-start.8 = (bf16[2,144,128]{2,1,0:T(8,128)(2,1)S(1)}, bf16[2,144,128]{2,1,0:T(8,128)(2,1)S(1)}, u32[]{:S(2)}, u32[]{:S(2)}) collective-permute-start(bf16[2,144,128]{2,1,0:T(8,128)(2,1)S(1)} %get-tuple-element.43.p0), channel_id=1, source_target_pairs={{0,12},{4,0},{8,4},{12,8},{1,13},{5,1},{9,5},{13,9},{2,14},{6,2},{... | collective-permute-start | bytes 221192 | tf_op jit(solution)/shard_map/ppermute | solution.py:467
  31.6 3.2 %collective-permute-start.9 = (bf16[48,3456]{1,0:T(8,128)(2,1)S(1)}, bf16[48,3456]{1,0:T(8,128)(2,1)S(1)}, u32[]{:S(2)}, u32[]{:S(2)}) collective-permute-start(bf16[48,3456]{1,0:T(8,128)(2,1)S(1)} %shard_map.77.w1), channel_id=1, source_target_pairs={{0,1},{1,0},{2,3},{3,2},{4,5},{5,4},{6,7},{7,6},{8,9},{9,8},{10,11... | collective-permute-start | bytes 995336 | tf_op jit(solution)/shard_map/ppermute | solution.py:467
  34.4 1.6 %collective-permute-start.10 = (bf16[48,3456]{1,0:T(8,128)(2,1)S(1)}, bf16[48,3456]{1,0:T(8,128)(2,1)S(1)}, u32[]{:S(2)}, u32[]{:S(2)}) collective-permute-start(bf16[48,3456]{1,0:T(8,128)(2,1)S(1)} %collective-permute-done.5.w3), channel_id=1, source_target_pairs={{0,1},{1,0},{2,3},{3,2},{4,5},{5,4},{6,7},{7,6},{8,9},{9,8},{10,11... | collective-permute-start | bytes 995336 | tf_op jit(solution)/shard_map/ppermute | solution.py:467
  36.1 7.0 %copy-start.1 = (bf16[1,4,24,24,128]{4,3,2,1,0:T(8,128)(2,1)S(1)}, bf16[1,4,24,24,128]{4,3,2,1,0:T(8,128)(2,1)}, u32[]{:S(2)}) copy-start(bf16[1,4,24,24,128]{4,3,2,1,0:T(8,128)(2,1)} %param.5) | copy-start | bytes 1769476
  36.1 7.0 %copy-start.5 = (f32[4,768,128]{2,1,0:T(8,128)S(1)}, f32[4,768,128]{2,1,0:T(8,128)}, u32[]{:S(2)}) copy-start(f32[4,768,128]{2,1,0:T(8,128)} %copy-done.4) | copy-start | bytes 4718596
  47.2 2.5 %collective-permute-start.11 = (f32[1728,128]{1,0:T(8,128)S(1)}, f32[1728,128]{1,0:T(8,128)S(1)}, u32[]{:S(2)}, u32[]{:S(2)}) collective-permute-start(f32[1728,128]{1,0:T(8,128)S(1)} %get-tuple-element.51), channel_id=1, source_target_pairs={{0,1},{1,0},{2,3},{3,2},{4,5},{5,4},{6,7},{7,6},{8,9},{9,8},{10,11... | collective-permute-start | bytes 2654216 | tf_op jit(solution)/shard_map/ppermute | solution.py:467
  49.7 7.5 %collective-permute-start.12 = (bf16[864,128]{1,0:T(8,128)(2,1)S(1)}, bf16[864,128]{1,0:T(8,128)(2,1)S(1)}, u32[]{:S(2)}, u32[]{:S(2)}) collective-permute-start(bf16[864,128]{1,0:T(8,128)(2,1)S(1)} %get-tuple-element.55), channel_id=1, source_target_pairs={{0,2},{2,0},{1,3},{3,1},{4,6},{6,4},{5,7},{7,5},{8,10},{10,8},{9,1... | collective-permute-start | bytes 663560 | tf_op jit(solution)/shard_map/ppermute | solution.py:467
  57.3 1.9 %collective-permute-start.17 = (f32[872,128]{1,0:T(8,128)S(1)}, f32[872,128]{1,0:T(8,128)S(1)}, u32[]{:S(2)}, u32[]{:S(2)}) collective-permute-start(f32[872,128]{1,0:T(8,128)S(1)} %get-tuple-element.68), channel_id=1, source_target_pairs={{0,1},{1,0},{2,3},{3,2},{4,5},{5,4},{6,7},{7,6},{8,9},{9,8},{10,11... | collective-permute-start | bytes 1339400 | tf_op jit(solution)/shard_map/ppermute | solution.py:467
  59.2 13.6 %collective-permute-start.18 = (f32[872,128]{1,0:T(8,128)S(1)}, f32[872,128]{1,0:T(8,128)S(1)}, u32[]{:S(2)}, u32[]{:S(2)}) collective-permute-start(f32[872,128]{1,0:T(8,128)S(1)} %add.113), channel_id=1, source_target_pairs={{0,2},{2,0},{1,3},{3,1},{4,6},{6,4},{5,7},{7,5},{8,10},{10,8},{9,1... | collective-permute-start | bytes 1339400 | tf_op jit(solution)/shard_map/ppermute | solution.py:467
  59.8 6.4 %collective-permute-start.13 = (bf16[216,128]{1,0:T(8,128)(2,1)S(1)}, bf16[216,128]{1,0:T(8,128)(2,1)S(1)}, u32[]{:S(2)}, u32[]{:S(2)}) collective-permute-start(bf16[216,128]{1,0:T(8,128)(2,1)S(1)} %get-tuple-element.64), channel_id=1, source_target_pairs={{0,4},{4,8},{8,12},{12,0},{1,5},{5,9},{9,13},{13,1},{2,6},{6,10},{... | collective-permute-start | bytes 165896 | tf_op jit(solution)/shard_map/ppermute | solution.py:467
  61.2 5.1 %collective-permute-start.14 = (bf16[216,128]{1,0:T(8,128)(2,1)S(1)}, bf16[216,128]{1,0:T(8,128)(2,1)S(1)}, u32[]{:S(2)}, u32[]{:S(2)}) collective-permute-start(bf16[216,128]{1,0:T(8,128)(2,1)S(1)} %get-tuple-element.65), channel_id=1, source_target_pairs={{0,12},{4,0},{8,4},{12,8},{1,13},{5,1},{9,5},{13,9},{2,14},{6,2},{... | collective-permute-start | bytes 165896 | tf_op jit(solution)/shard_map/ppermute | solution.py:467
  63.7 5.2 %collective-permute-start.15 = (bf16[216,128]{1,0:T(8,128)(2,1)S(1)}, bf16[216,128]{1,0:T(8,128)(2,1)S(1)}, u32[]{:S(2)}, u32[]{:S(2)}) collective-permute-start(bf16[216,128]{1,0:T(8,128)(2,1)S(1)} %get-tuple-element.66), channel_id=1, source_target_pairs={{0,8},{4,12},{8,0},{12,4},{1,9},{5,13},{9,1},{13,5},{2,10},{6,14},... | collective-permute-start | bytes 165896 | tf_op jit(solution)/shard_map/ppermute | solution.py:467
  68.9 6.4 %collective-permute-start.16 = (bf16[216,128]{1,0:T(8,128)(2,1)S(1)}, bf16[216,128]{1,0:T(8,128)(2,1)S(1)}, u32[]{:S(2)}, u32[]{:S(2)}) collective-permute-start(bf16[216,128]{1,0:T(8,128)(2,1)S(1)} %get-tuple-element.74), channel_id=1, source_target_pairs={{0,4},{4,8},{8,12},{12,0},{1,5},{5,9},{9,13},{13,1},{2,6},{6,10},{... | collective-permute-start | bytes 165896 | tf_op jit(solution)/shard_map/ppermute | solution.py:467
  69.1 6.3 %collective-permute-start.19 = (bf16[216,128]{1,0:T(8,128)(2,1)S(1)}, bf16[216,128]{1,0:T(8,128)(2,1)S(1)}, u32[]{:S(2)}, u32[]{:S(2)}) collective-permute-start(bf16[216,128]{1,0:T(8,128)(2,1)S(1)} %get-tuple-element.74), channel_id=1, source_target_pairs={{0,12},{4,0},{8,4},{12,8},{1,13},{5,1},{9,5},{13,9},{2,14},{6,2},{... | collective-permute-start | bytes 165896 | tf_op jit(solution)/shard_map/ppermute | solution.py:467
  72.8 5.1 %collective-permute-start.20 = (bf16[216,128]{1,0:T(8,128)(2,1)S(1)}, bf16[216,128]{1,0:T(8,128)(2,1)S(1)}, u32[]{:S(2)}, u32[]{:S(2)}) collective-permute-start(bf16[216,128]{1,0:T(8,128)(2,1)S(1)} %get-tuple-element.74), channel_id=1, source_target_pairs={{0,8},{4,12},{8,0},{12,4},{1,9},{5,13},{9,1},{13,5},{2,10},{6,14},... | collective-permute-start | bytes 165896 | tf_op jit(solution)/shard_map/ppermute | solution.py:467
  75.4 8.8 %collective-permute-start.23 = (f32[872,128]{1,0:T(8,128)S(1)}, f32[872,128]{1,0:T(8,128)S(1)}, u32[]{:S(2)}, u32[]{:S(2)}) collective-permute-start(f32[872,128]{1,0:T(8,128)S(1)} %add.114), channel_id=1, source_target_pairs={{0,1},{1,0},{2,3},{3,2},{4,5},{5,4},{6,7},{7,6},{8,9},{9,8},{10,11... | collective-permute-start | bytes 1339400 | tf_op jit(solution)/shard_map/ppermute | solution.py:467
  77.9 6.0 %collective-permute-start.21 = (bf16[864,128]{1,0:T(8,128)(2,1)S(1)}, bf16[864,128]{1,0:T(8,128)(2,1)S(1)}, u32[]{:S(2)}, u32[]{:S(2)}) collective-permute-start(bf16[864,128]{1,0:T(8,128)(2,1)S(1)} %bitcast.69), channel_id=1, source_target_pairs={{0,2},{2,0},{1,3},{3,1},{4,6},{6,4},{5,7},{7,5},{8,10},{10,8},{9,1... | collective-permute-start | bytes 663560 | tf_op jit(solution)/shard_map/ppermute | solution.py:467
  83.9 1.9 %collective-permute-start.22 = (bf16[1728,128]{1,0:T(8,128)(2,1)S(1)}, bf16[1728,128]{1,0:T(8,128)(2,1)S(1)}, u32[]{:S(2)}, u32[]{:S(2)}) collective-permute-start(bf16[1728,128]{1,0:T(8,128)(2,1)S(1)} %bitcast.67), channel_id=1, source_target_pairs={{0,1},{1,0},{2,3},{3,2},{4,5},{5,4},{6,7},{7,6},{8,9},{9,8},{10,11... | collective-permute-start | bytes 1327112 | tf_op jit(solution)/shard_map/ppermute | solution.py:467

commit v2 on v1

--- a/solution.py
+++ b/solution.py
@@ -139,7 +139,7 @@
     )
 
 
-def first_backward(vol, before, after, spread, slope, which, keep, send, u, rows_ref, g, acc, twice):
+def first_backward(vol, before, after, spread, slope, keep, send, u, rows_ref, g, acc, twice):
     depth, rows, cols, chans = vol.shape
     wide = 32
     cells = rows * wide
@@ -194,16 +194,16 @@
                         low = top + cut - length
                         second[low : low + chans - cut, :] = acc[e * chans + cut : (e + 1) * chans, lanes]
 
-    @pl.when(which[0] == 0)
+    @pl.when(lax.axis_index("rep") == 0)
     def _():
         write(keep, send)
 
-    @pl.when(which[0] != 0)
+    @pl.when(lax.axis_index("rep") != 0)
     def _():
         write(send, keep)
 
 
-def run_first_backward(vol, before, after, spread, slope, which):
+def run_first_backward(vol, before, after, spread, slope):
     depth, rows, cols, chans = vol.shape
     wide, outs = 32, slope.shape[2]
     cells = rows * wide
@@ -217,8 +217,14 @@
             pltpu.VMEM((3 * chans, 9 * outs), f32),
             pltpu.VMEM((cells // 2, outs), f32),
         ],
-        vol, before, after, spread, slope, which, work=heavy * 7, smem=(5,),
-    )
+        vol, before, after, spread, slope, work=heavy * 7,
+    )
+
+
+def positions():
+    place = lax.axis_index("space")
+    copy = 2 * lax.axis_index("dp") + lax.axis_index("rep")
+    return [(place + 4 - k) % 4 for k in range(4)] + [copy ^ k for k in range(4)]
 
 
 def lay_pooled(parts, places, flat, rows_ref, target, top, side, wide):
@@ -236,10 +242,11 @@
 
 
 def second_layer(
-    where, p0, p1, p2, p3, w0, w1, w2, w3, w4, head, wanted,
+    p0, p1, p2, p3, w0, w1, w2, w3, w4, head, wanted,
     pooled_grad, own, result, p, flat, rows_ref, w, acc, slopes, shift_ref, g,
 ):
     parts, pieces = (p0, p1, p2, p3), (w1, w2, w3, w4)
+    where = positions()
     planes, area, chans = p0.shape
     side, wide = 12, 16
     cells = side * wide
@@ -290,10 +297,23 @@
 
     total = lax.fori_loop(0, 2, half, jnp.zeros((8, outs), f32))
     feature = total.sum(axis=0, keepdims=True) / float(depth * area)
-    predicted = jnp.sum(feature * head[...], axis=1, keepdims=True)
-    error = predicted - wanted[:, 0:1]
+    natural = [head[:, k * share : (k + 1) * share] for k in range(4)]
+    turned = []
+    for k in range(4):
+        block = natural[0]
+        for j in range(1, 4):
+            block = jnp.where(where[k] == j, natural[j], block)
+        turned.append(block)
+    head = jnp.concatenate(turned, axis=1)
+    count = head.shape[0]
+    predicted = jnp.sum(feature * head, axis=1, keepdims=True)
+    row = lax.broadcasted_iota(jnp.int32, (count, 1), 0)
+    target = jnp.zeros((count, 1), f32)
+    for k in range(count):
+        target = jnp.where(row == k, wanted[0, k], target)
+    error = predicted - target
     result[...] = error * feature
-    scale = jnp.sum(head[...] * error, axis=0, keepdims=True)
+    scale = jnp.sum(head * error, axis=0, keepdims=True)
     for d in range(depth):
         own[d] = (slopes[d + 1, :, 0:share] * scale[:, 0:share]).astype(bf16)
     shift_ref[...] = jnp.zeros_like(shift_ref)
@@ -316,7 +336,7 @@
     pooled_grad[...] = jnp.where(keep, out, 0.0).reshape(planes, cells, chans)
 
 
-def run_second_layer(where, parts, part_kernel, pieces, head, wanted):
+def run_second_layer(parts, part_kernel, pieces, head, wanted):
     planes, area, chans = parts[0].shape
     side, wide = 12, 16
     cells = side * wide
@@ -328,7 +348,7 @@
         (
             jax.ShapeDtypeStruct((planes, cells, chans), f32),
             jax.ShapeDtypeStruct((depth, cells, share), bf16),
-            jax.ShapeDtypeStruct((8, outs), f32),
+            jax.ShapeDtypeStruct((head.shape[0], outs), f32),
         ),
         [
             pltpu.VMEM((depth + 2, cells + 2 * wide, 3 * chans), bf16),
@@ -340,12 +360,13 @@
             pltpu.VMEM((cells + 2 * front, outs), f32),
             pltpu.VMEM((3, planes + 2, cells + 2 * wide, outs), bf16),
         ],
-        where, *parts, part_kernel, *pieces, head, wanted, smem=(0,), work=heavy * 8,
-    )
-
-
-def second_backward(where, p0, p1, p2, p3, own, result, which, keep, send, p, flat, rows_ref, g, grad):
+        *parts, part_kernel, *pieces, head, wanted, smem=(10,), work=heavy * 8,
+    )
+
+
+def second_backward(p0, p1, p2, p3, own, result, keep, send, p, flat, rows_ref, g, grad):
     parts = (p0, p1, p2, p3)
+    where = positions()
     planes, area, chans = p0.shape
     side, wide = 12, 16
     cells = side * wide
@@ -375,15 +396,15 @@
                 t = 9 * a + 3 * b + e
                 block = part[b * share : (b + 1) * share, e * chans : (e + 1) * chans]
                 grad[t * share : (t + 1) * share, :] = block
-    grad[27 * share : 27 * share + 8, :] = result[:, 0:chans]
-    grad[27 * share + 8 :, :] = jnp.zeros((8, chans), f32)
+    grad[27 * share :, :] = jnp.zeros((16, chans), f32)
+    grad[27 * share : 27 * share + result.shape[0], :] = result[:, 0:chans]
     half = keep.shape[0]
-    low = pl.multiple_of(which[0] * half, 8)
+    low = pl.multiple_of(lax.axis_index("rep") * half, 8)
     keep[...] = grad[pl.ds(low, half), :]
     send[...] = grad[pl.ds(pl.multiple_of(half - low, 8), half), :]
 
 
-def run_second_backward(where, parts, own, result, which):
+def run_second_backward(parts, own, result):
     planes, area, chans = parts[0].shape
     depth, cells, share = own.shape
     return call(
@@ -396,8 +417,22 @@
             pltpu.VMEM((depth, cells, 3 * share), bf16),
             pltpu.VMEM((27 * share + 16, chans), f32),
         ],
-        where, *parts, own, result, which, smem=(0, 7), work=heavy * 4,
-    )
+        *parts, own, result, work=heavy * 4,
+    )
+
+
+def entry(vol, kernel, other, first, last, piece):
+    rows = piece.shape[0]
+    copy = 2 * lax.axis_index("dp") + lax.axis_index("rep")
+    piece[...] = kernel[pl.ds(pl.multiple_of(copy * rows, rows), rows), :]
+    first[0] = vol[0]
+    last[0] = vol[vol.shape[0] - 1]
+
+
+def run_entry(vol, kernel, other):
+    plane = jax.ShapeDtypeStruct((1,) + vol.shape[1:], bf16)
+    piece = jax.ShapeDtypeStruct((kernel.shape[0] // 4, kernel.shape[1]), bf16)
+    return call(entry, (plane, plane, piece), [], vol, kernel, other)
 
 
 def join(r0, r1, r2, out):
@@ -411,25 +446,25 @@
     return call(join, jax.ShapeDtypeStruct((3 * rows, cols), bf16), [], *parts)
 
 
-def merge_half(which, kept, came, keep, send):
+def merge_half(kept, came, keep, send):
     half = keep.shape[0]
-    low = pl.multiple_of(which[0] * half, 8)
+    low = pl.multiple_of(lax.axis_index("dp") * half, 8)
     high = pl.multiple_of(half - low, 8)
     keep[...] = kept[pl.ds(low, half), :] + came[pl.ds(low, half), :]
     send[...] = (kept[pl.ds(high, half), :] + came[pl.ds(high, half), :]).astype(bf16)
 
 
-def run_merge_half(which, kept, came):
+def run_merge_half(kept, came):
     rows, cols = kept.shape
     outs = tuple(jax.ShapeDtypeStruct((rows // 2, cols), kind) for kind in (f32, bf16))
-    return call(merge_half, outs, [], which, kept, came, smem=(0,))
-
-
-def merge_blocks(which, kept, came, keep, s1, s2, s3):
+    return call(merge_half, outs, [], kept, came)
+
+
+def merge_blocks(kept, came, keep, s1, s2, s3):
     size = keep.shape[0]
 
     def block(step):
-        low = pl.multiple_of((which[0] + step) % 4 * size, 8)
+        low = pl.multiple_of((lax.axis_index("space") + step) % 4 * size, 8)
         return kept[pl.ds(low, size), :] + came[pl.ds(low, size), :].astype(f32)
 
     keep[...] = block(0)
@@ -437,10 +472,10 @@
         send[...] = block(step).astype(bf16)
 
 
-def run_merge_blocks(which, kept, came):
+def run_merge_blocks(kept, came):
     rows, cols = kept.shape
     outs = tuple(jax.ShapeDtypeStruct((rows // 4, cols), kind) for kind in (f32, bf16, bf16, bf16))
-    return call(merge_blocks, outs, [], which, kept, came, smem=(0,))
+    return call(merge_blocks, outs, [], kept, came)
 
 
 def spread_second(packed, out, head):
@@ -655,17 +690,11 @@
     share = second_kernel.shape[1]
     outs = head_weights.shape[1]
     place = lax.axis_index("space")
-    rep = lax.axis_index("rep")
-    copy = 2 * lax.axis_index("dp") + rep
-    where = jnp.stack([(place - k) % 4 for k in range(4)] + [copy ^ k for k in range(4)])
     turned = second_kernel.T
     before, after = neighbours(grid[:1], grid[-1:])
+    copy = 2 * lax.axis_index("dp") + lax.axis_index("rep")
     piece = lax.dynamic_slice_in_dim(turned, copy * (share // 4), share // 4, 0)
     others = [turn(piece, "space", k) for k in range(1, 4)]
-    blocks = head_weights.T.reshape(outs, 4, share)
-    head = jnp.concatenate([lax.dynamic_index_in_dim(blocks, (place - k) % 4, 1, False) for k in range(4)], axis=1)
-    head = jnp.pad(head, ((0, 8 - outs), (0, 0)))
-    wanted = jnp.pad(jnp.broadcast_to(targets[0][:, None], (outs, 128)), ((0, 8 - outs), (0, 0)))
     pooled, slope = run_first_forward(grid, before, after, first_kernel)
     pooled, *others = lax.optimization_barrier([pooled] + others)
     others = run_join(others)
@@ -673,15 +702,14 @@
     parts = [pooled] + [turn(pooled, "space", k) for k in range(1, 4)]
     across, *parts = lax.optimization_barrier([across] + parts)
     pieces = [others, turn(others, "rep", 1), across, turn(across, "rep", 1)]
-    pooled_grad, own, result = run_second_layer(where, parts, turned, pieces, head, wanted)
-    keep, send = run_first_backward(grid, before, after, pooled_grad, slope, rep[None])
-    keep, send = run_merge_half(lax.axis_index("dp")[None], keep, turn(send, "rep", 1))
+    pooled_grad, own, result = run_second_layer(parts, turned, pieces, head_weights.T, targets)
+    keep, send = run_first_backward(grid, before, after, pooled_grad, slope)
+    keep, send = run_merge_half(keep, turn(send, "rep", 1))
     arrived = turn(send, "dp", 1)
-    keep, own = lax.optimization_barrier((keep, own))
-    kept, sent = run_second_backward(where, parts, own, result, rep[None])
-    x, *sends = run_merge_blocks(place[None], keep, arrived)
-    sends[0], sends[1], sends[2], kept, sent = lax.optimization_barrier((*sends, kept, sent))
+    kept, sent = run_second_backward(parts, own, result)
+    x, *sends = run_merge_blocks(keep, arrived)
     second = kept + turn(sent, "rep", 1)
+    *sends, second = lax.optimization_barrier((*sends, second))
     for k in (1, 3, 2):
         x = x + turn(sends[k - 1], "space", k).astype(f32)
     x = x.astype(bf16)

time: 87.5 us -> 84.7 us (0.968)
  waiting for transfers between devices: 27.5 us -> 26.1 us
  local copies, waits for them, and re-layouts: 6.13 us -> 4.74 us
    ppermute x22, waiting for transfers between devices: 27.4 us -> 26.1 us  [turn(): return lax.ppermute(x, axis, [(i, (i + step) % size) for i in range(size)])]
    unnamed x16 -> x12, local copies, waits for them, and re-layouts: 3.39 us -> 2.25 us
  transfers between devices with their start and end apart: 24 -> 24, of which waited for: 12 -> 11; matrix products, arithmetic and copies ran while one was open for 2% -> 2% of each run, Pallas kernels for 11% -> 11%
where the time goes in v2:
time: 84.7 us; the launch traced here: 84.4 us
  starting transfers between devices  30.8 us (36%)
  waiting for transfers between devices  26.1 us (31%)
  Pallas kernels  20.2 us (24%)
  local copies, waits for them, and re-layouts  4.74 us (6%)
  other arithmetic  1.53 us (2%)
  between operations  1.02 us (1%)
    ppermute x22, waiting for transfers between devices, turn(): return lax.ppermute(x, axis, [(i, (i + step) % size) for i in range(size)])  26.1 us
    ppermute x22, starting transfers between devices, turn(): return lax.ppermute(x, axis, [(i, (i + step) % size) for i in range(size)])  24.6 us
    pallas_call x8, Pallas kernels, call(): pl.pallas_call(body, out_shape=outs, in_specs=specs, out_specs=out_specs,...  20.2 us
    ppermute x1, starting transfers between devices, neighbours(): before = lax.ppermute(last, 'space', up)  4.94 us
    unnamed x12, local copies, waits for them, and re-layouts  2.25 us
  transfers between devices with their start and end apart: 24, of which 11 were waited for; matrix products, arithmetic and copies ran while one was open for 2% of the time, Pallas kernels for 11%

profile of v2, /device:TPU:0, one launch (start us, length us, event | category | flops | bytes accessed | tf_op | source)
XLA Modules:
  0.0 84.4 jit_solution(5304036651966240938)
XLA Ops:
  0.6 1.0 %slice_bitcast_fusion = (bf16[1,24,24,128]{3,2,1,0:T(8,128)(2,1)S(1)}, bf16[1,24,24,128]{3,2,1,0:T(8,128)(2,1)S(1)}) fusion(bf16[1,4,24,24,128]{4,3,2,1,0:T(8,128)(2,1)} %param.5), kind=kLoop, calls=%fused_computation.7 | loop fusion | bytes 589824 | tf_op jit(solution)/shard_map/slice | solution.py:694
  1.6 4.9 %collective-permute-start = (bf16[1,24,24,128]{3,2,1,0:T(8,128)(2,1)S(1)}, bf16[1,24,24,128]{3,2,1,0:T(8,128)(2,1)S(1)}, u32[]{:S(2)}, u32[]{:S(2)}) collective-permute-start(bf16[1,24,24,128]{3,2,1,0:T(8,128)(2,1)S(1)} %get-tuple-element.70), channel_id=1, source_target_pairs={{0,4},{4,8},{8,12},{1,5},{5,9},{9,13},{2,6},{6,10},{10,14},{3,7},{... | collective-permute-start | bytes 442376 | tf_op jit(solution)/shard_map/ppermute | solution.py:680
  6.6 1.3 %collective-permute-start.1 = (bf16[1,24,24,128]{3,2,1,0:T(8,128)(2,1)S(1)}, bf16[1,24,24,128]{3,2,1,0:T(8,128)(2,1)S(1)}, u32[]{:S(2)}, u32[]{:S(2)}) collective-permute-start(bf16[1,24,24,128]{3,2,1,0:T(8,128)(2,1)S(1)} %get-tuple-element.69), channel_id=1, source_target_pairs={{4,0},{8,4},{12,8},{5,1},{9,5},{13,9},{6,2},{10,6},{14,10},{7,3},{... | collective-permute-start | bytes 442376 | tf_op jit(solution)/shard_map/ppermute | solution.py:681
  7.9 0.9 %dynamic-slice_bitcast_fusion = bf16[16,3456]{1,0:T(8,128)(2,1)S(1)} fusion(bf16[3456,64]{0,1:T(8,128)(2,1)} %param.8, s32[]{:T(128)S(6)} %select_n.72), kind=kLoop, calls=%fused_computation.10 | loop fusion | bytes 221188 | tf_op jit(solution)/shard_map/dynamic_slice | solution.py:696
  8.8 2.6 %collective-permute-start.2 = (bf16[16,3456]{1,0:T(8,128)(2,1)S(1)}, bf16[16,3456]{1,0:T(8,128)(2,1)S(1)}, u32[]{:S(2)}, u32[]{:S(2)}) collective-permute-start(bf16[16,3456]{1,0:T(8,128)(2,1)S(1)} %dynamic-slice_bitcast_fusion), channel_id=1, source_target_pairs={{0,4},{4,8},{8,12},{12,0},{1,5},{5,9},{9,13},{13,1},{2,6},{6,10},{... | collective-permute-start | bytes 331784 | tf_op jit(solution)/shard_map/ppermute | solution.py:502
  11.5 2.6 %collective-permute-start.3 = (bf16[16,3456]{1,0:T(8,128)(2,1)S(1)}, bf16[16,3456]{1,0:T(8,128)(2,1)S(1)}, u32[]{:S(2)}, u32[]{:S(2)}) collective-permute-start(bf16[16,3456]{1,0:T(8,128)(2,1)S(1)} %dynamic-slice_bitcast_fusion), channel_id=1, source_target_pairs={{0,8},{4,12},{8,0},{12,4},{1,9},{5,13},{9,1},{13,5},{2,10},{6,14},... | collective-permute-start | bytes 331784 | tf_op jit(solution)/shard_map/ppermute | solution.py:502
  14.0 1.3 %collective-permute-start.4 = (bf16[16,3456]{1,0:T(8,128)(2,1)S(1)}, bf16[16,3456]{1,0:T(8,128)(2,1)S(1)}, u32[]{:S(2)}, u32[]{:S(2)}) collective-permute-start(bf16[16,3456]{1,0:T(8,128)(2,1)S(1)} %dynamic-slice_bitcast_fusion), channel_id=1, source_target_pairs={{0,12},{4,0},{8,4},{12,8},{1,13},{5,1},{9,5},{13,9},{2,14},{6,2},{... | collective-permute-start | bytes 331784 | tf_op jit(solution)/shard_map/ppermute | solution.py:502
  15.4 1.1 %copy-done = bf16[1,4,24,24,128]{4,3,2,1,0:T(8,128)(2,1)S(1)} copy-done((bf16[1,4,24,24,128]{4,3,2,1,0:T(8,128)(2,1)S(1)}, bf16[1,4,24,24,128]{4,3,2,1,0:T(8,128)(2,1)}, u32[]{:S(2)}) %copy-start) | copy-done | bytes 589848
  16.5 1.2 %copy-done.3 = bf16[3456,128]{1,0:T(8,128)(2,1)S(1)} copy-done((bf16[3456,128]{1,0:T(8,128)(2,1)S(1)}, bf16[3456,128]{1,0:T(8,128)(2,1)}, u32[]{:S(2)}) %copy-start.3) | copy-done | bytes 884760
  17.6 5.8 %shard_map.76 = (bf16[2,144,128]{2,1,0:T(8,128)(2,1)S(1)}, f32[4,768,128]{2,1,0:T(8,128)S(1)}) custom-call(bf16[4,24,24,128]{3,2,1,0:T(8,128)(2,1)S(1)} %bitcast.40, bf16[1,24,24,128]{3,2,1,0:T(8,128)(2,1)S(1)} %collective-permute-done.before, bf16[1,24,24,128]{3,2,1,0:T(8,128)(2,1)S(1)} %collective-permute-done.1.after, bf16[3456,128]{1,0:T(8,128)(2,1)S(1)} %copy-done.3), custom_call_target="tpu_custom_call" | custom-call | flops 8000000000 | tf_op jit(solution)/shard_map/pallas_call | solution.py:24
  23.5 1.6 %collective-permute-start.5 = (bf16[48,3456]{1,0:T(8,128)(2,1)S(1)}, bf16[48,3456]{1,0:T(8,128)(2,1)S(1)}, u32[]{:S(2)}, u32[]{:S(2)}) collective-permute-start(bf16[48,3456]{1,0:T(8,128)(2,1)S(1)} %shard_map.77.w1), channel_id=1, source_target_pairs={{0,2},{2,0},{1,3},{3,1},{4,6},{6,4},{5,7},{7,5},{8,10},{10,8},{9,1... | collective-permute-start | bytes 995336 | tf_op jit(solution)/shard_map/ppermute | solution.py:502
  25.1 2.2 %collective-permute-start.6 = (bf16[2,144,128]{2,1,0:T(8,128)(2,1)S(1)}, bf16[2,144,128]{2,1,0:T(8,128)(2,1)S(1)}, u32[]{:S(2)}, u32[]{:S(2)}) collective-permute-start(bf16[2,144,128]{2,1,0:T(8,128)(2,1)S(1)} %get-tuple-element.40.p0), channel_id=1, source_target_pairs={{0,4},{4,8},{8,12},{12,0},{1,5},{5,9},{9,13},{13,1},{2,6},{6,10},{... | collective-permute-start | bytes 221192 | tf_op jit(solution)/shard_map/ppermute | solution.py:502
  27.2 0.3 collective-permute-start.7
  27.5 2.9 %collective-permute-start.8 = (bf16[2,144,128]{2,1,0:T(8,128)(2,1)S(1)}, bf16[2,144,128]{2,1,0:T(8,128)(2,1)S(1)}, u32[]{:S(2)}, u32[]{:S(2)}) collective-permute-start(bf16[2,144,128]{2,1,0:T(8,128)(2,1)S(1)} %get-tuple-element.40.p0), channel_id=1, source_target_pairs={{0,12},{4,0},{8,4},{12,8},{1,13},{5,1},{9,5},{13,9},{2,14},{6,2},{... | collective-permute-start | bytes 221192 | tf_op jit(solution)/shard_map/ppermute | solution.py:502
  30.4 1.0 %collective-permute-done.6.p1 = bf16[2,144,128]{2,1,0:T(8,128)(2,1)S(1)} collective-permute-done((bf16[2,144,128]{2,1,0:T(8,128)(2,1)S(1)}, bf16[2,144,128]{2,1,0:T(8,128)(2,1)S(1)}, u32[]{:S(2)}, u32[]{:S(2)}) %collective-permute-start.6) | collective-permute-done | bytes 73760 | tf_op jit(solution)/shard_map/ppermute | solution.py:502
  31.4 1.8 %collective-permute-done.7.p2 = bf16[2,144,128]{2,1,0:T(8,128)(2,1)S(1)} collective-permute-done((bf16[2,144,128]{2,1,0:T(8,128)(2,1)S(1)}, bf16[2,144,128]{2,1,0:T(8,128)(2,1)S(1)}, u32[]{:S(2)}, u32[]{:S(2)}) %collective-permute-start.7) | collective-permute-done | bytes 73760 | tf_op jit(solution)/shard_map/ppermute | solution.py:502
  33.3 1.6 %collective-permute-done.10.w4 = bf16[48,3456]{1,0:T(8,128)(2,1)S(1)} collective-permute-done((bf16[48,3456]{1,0:T(8,128)(2,1)S(1)}, bf16[48,3456]{1,0:T(8,128)(2,1)S(1)}, u32[]{:S(2)}, u32[]{:S(2)}) %collective-permute-start.10) | collective-permute-done | bytes 331808 | tf_op jit(solution)/shard_map/ppermute | solution.py:502
  34.9 7.1 %shard_map.78 = (f32[2,192,128]{2,1,0:T(8,128)S(1)}, bf16[8,192,64]{2,1,0:T(8,128)(2,1)S(1)}, f32[4,256]{1,0:T(4,128)S(1)}) custom-call(bf16[2,144,128]{2,1,0:T(8,128)(2,1)S(1)} %get-tuple-element.40.p0, bf16[2,144,128]{2,1,0:T(8,128)(2,1)S(1)} %collective-permute-done.6.p1, bf16[2,144,128]{2,1,0:T(8,128)(2,1)S(1)} %collective-permute-done.7.p2, ...), custom_call_target="tpu_custom_call" | custom-call | flops 8000000000 | tf_op jit(solution)/shard_map/pallas_call | solution.py:24
  42.1 4.1 %shard_map.79 = (f32[1728,128]{1,0:T(8,128)S(1)}, f32[1728,128]{1,0:T(8,128)S(1)}) custom-call(bf16[4,24,24,128]{3,2,1,0:T(8,128)(2,1)S(1)} %bitcast.41, bf16[1,24,24,128]{3,2,1,0:T(8,128)(2,1)S(1)} %collective-permute-done.before, bf16[1,24,24,128]{3,2,1,0:T(8,128)(2,1)S(1)} %collective-permute-done.1.after, f32[2,192,128]{2,1,0:T(8,128)S(1)} %get-tuple-element.45.spread, ...), custom_call_target="tpu_custom_call" | custom-call | flops 7000000000 | tf_op jit(solution)/shard_map/pallas_call | solution.py:24
  46.2 0.2 collective-permute-start.11
  46.4 2.1 %shard_map.82 = (f32[872,128]{1,0:T(8,128)S(1)}, f32[872,128]{1,0:T(8,128)S(1)}) custom-call(bf16[2,144,128]{2,1,0:T(8,128)(2,1)S(1)} %get-tuple-element.40.p0, bf16[2,144,128]{2,1,0:T(8,128)(2,1)S(1)} %collective-permute-done.6.p1, bf16[2,144,128]{2,1,0:T(8,128)(2,1)S(1)} %collective-permute-done.7.p2, bf16[2,144,128]{2,1,0:T(8,128)(2,1)S(1)} %collective-permute-done.8.p3, ...), custom_call_target="tpu_custom_call" | custom-call | flops 4000000000 | tf_op jit(solution)/shard_map/pallas_call | solution.py:24
  48.4 0.4 collective-permute-start.13
  48.9 0.1 shard_map.80
  49.0 0.6 collective-permute-start.12
  49.6 0.7 collective-permute-done.13
  50.3 6.1 %collective-permute-done.12.came = bf16[864,128]{1,0:T(8,128)(2,1)S(1)} collective-permute-done((bf16[864,128]{1,0:T(8,128)(2,1)S(1)}, bf16[864,128]{1,0:T(8,128)(2,1)S(1)}, u32[]{:S(2)}, u32[]{:S(2)}) %collective-permute-start.12) | collective-permute-done | bytes 221216 | tf_op jit(solution)/shard_map/ppermute | solution.py:502
  56.6 0.6 collective-permute-start.18
  57.2 1.6 %collective-permute-start.14 = (bf16[216,128]{1,0:T(8,128)(2,1)S(1)}, bf16[216,128]{1,0:T(8,128)(2,1)S(1)}, u32[]{:S(2)}, u32[]{:S(2)}) collective-permute-start(bf16[216,128]{1,0:T(8,128)(2,1)S(1)} %get-tuple-element.59), channel_id=1, source_target_pairs={{0,4},{4,8},{8,12},{12,0},{1,5},{5,9},{9,13},{13,1},{2,6},{6,10},{... | collective-permute-start | bytes 165896 | tf_op jit(solution)/shard_map/ppermute | solution.py:502
  58.7 2.3 %collective-permute-start.15 = (bf16[216,128]{1,0:T(8,128)(2,1)S(1)}, bf16[216,128]{1,0:T(8,128)(2,1)S(1)}, u32[]{:S(2)}, u32[]{:S(2)}) collective-permute-start(bf16[216,128]{1,0:T(8,128)(2,1)S(1)} %get-tuple-element.60), channel_id=1, source_target_pairs={{0,12},{4,0},{8,4},{12,8},{1,13},{5,1},{9,5},{13,9},{2,14},{6,2},{... | collective-permute-start | bytes 165896 | tf_op jit(solution)/shard_map/ppermute | solution.py:502
  61.0 0.1 collective-permute-start.16
  61.0 2.6 %collective-permute-done.14 = bf16[216,128]{1,0:T(8,128)(2,1)S(1)} collective-permute-done((bf16[216,128]{1,0:T(8,128)(2,1)S(1)}, bf16[216,128]{1,0:T(8,128)(2,1)S(1)}, u32[]{:S(2)}, u32[]{:S(2)}) %collective-permute-start.14) | collective-permute-done | bytes 55328 | tf_op jit(solution)/shard_map/ppermute | solution.py:502
  63.7 2.3 %collective-permute-done.16 = bf16[216,128]{1,0:T(8,128)(2,1)S(1)} collective-permute-done((bf16[216,128]{1,0:T(8,128)(2,1)S(1)}, bf16[216,128]{1,0:T(8,128)(2,1)S(1)}, u32[]{:S(2)}, u32[]{:S(2)}) %collective-permute-start.16) | collective-permute-done | bytes 55328 | tf_op jit(solution)/shard_map/ppermute | solution.py:502
  66.1 0.1 bitcast_dynamic-update-slice_fusion.9
  66.1 0.1 collective-permute-start.17
  66.3 3.7 %collective-permute-start.19 = (bf16[216,128]{1,0:T(8,128)(2,1)S(1)}, bf16[216,128]{1,0:T(8,128)(2,1)S(1)}, u32[]{:S(2)}, u32[]{:S(2)}) collective-permute-start(bf16[216,128]{1,0:T(8,128)(2,1)S(1)} %get-tuple-element.68), channel_id=1, source_target_pairs={{0,12},{4,0},{8,4},{12,8},{1,13},{5,1},{9,5},{13,9},{2,14},{6,2},{... | collective-permute-start | bytes 165896 | tf_op jit(solution)/shard_map/ppermute | solution.py:502
  70.1 2.1 %collective-permute-done.17 = bf16[216,128]{1,0:T(8,128)(2,1)S(1)} collective-permute-done((bf16[216,128]{1,0:T(8,128)(2,1)S(1)}, bf16[216,128]{1,0:T(8,128)(2,1)S(1)}, u32[]{:S(2)}, u32[]{:S(2)}) %collective-permute-start.17) | collective-permute-done | bytes 55328 | tf_op jit(solution)/shard_map/ppermute | solution.py:502
  72.2 2.9 %collective-permute-done.20 = bf16[216,128]{1,0:T(8,128)(2,1)S(1)} collective-permute-done((bf16[216,128]{1,0:T(8,128)(2,1)S(1)}, bf16[216,128]{1,0:T(8,128)(2,1)S(1)}, u32[]{:S(2)}, u32[]{:S(2)}) %collective-permute-start.20) | collective-permute-done | bytes 55328 | tf_op jit(solution)/shard_map/ppermute | solution.py:502
  75.1 1.6 %collective-permute-start.21 = (bf16[864,128]{1,0:T(8,128)(2,1)S(1)}, bf16[864,128]{1,0:T(8,128)(2,1)S(1)}, u32[]{:S(2)}, u32[]{:S(2)}) collective-permute-start(bf16[864,128]{1,0:T(8,128)(2,1)S(1)} %bitcast.46), channel_id=1, source_target_pairs={{0,2},{2,0},{1,3},{3,1},{4,6},{6,4},{5,7},{7,5},{8,10},{10,8},{9,1... | collective-permute-start | bytes 663560 | tf_op jit(solution)/shard_map/ppermute | solution.py:502
  76.6 0.1 broadcast_in_dim.47
  76.7 0.1 broadcast_in_dim.57
  76.8 4.2 %collective-permute-done.21 = bf16[864,128]{1,0:T(8,128)(2,1)S(1)} collective-permute-done((bf16[864,128]{1,0:T(8,128)(2,1)S(1)}, bf16[864,128]{1,0:T(8,128)(2,1)S(1)}, u32[]{:S(2)}, u32[]{:S(2)}) %collective-permute-start.21) | collective-permute-done | bytes 221216 | tf_op jit(solution)/shard_map/ppermute | solution.py:502
  81.1 0.1 collective-permute-start.22
  81.2 0.1 broadcast_in_dim.46
  81.3 0.1 bitcast_dynamic-update-slice_fusion.3
  81.4 1.0 %shard_map.83 = (f32[64,3456]{1,0:T(8,128)}, f32[4,64]{1,0:T(4,128)}) custom-call(f32[1744,128]{1,0:T(8,128)S(1)} %bitcast.39), custom_call_target="tpu_custom_call" | custom-call | flops 2000000000 | tf_op jit(solution)/shard_map/pallas_call | solution.py:24
  82.4 0.6 collective-permute-done.22
  83.0 0.1 bitcast_dynamic-update-slice_fusion.2
  83.0 1.4 %bitcast_convert_fusion = f32[3456,128]{1,0:T(8,128)} fusion(bf16[2,1728,128]{2,1,0:T(8,128)(2,1)S(1)} %bitcast_dynamic-update-slice_fusion.2), kind=kLoop, calls=%fused_computation | loop fusion | flops 442368 | bytes 2654208 | tf_op jit(solution)/shard_map/convert_element_type | solution.py:728
  (39 shorter events, 0.4 us)
Async XLA Ops:
  1.6 13.7 %collective-permute-start = (bf16[1,24,24,128]{3,2,1,0:T(8,128)(2,1)S(1)}, bf16[1,24,24,128]{3,2,1,0:T(8,128)(2,1)S(1)}, u32[]{:S(2)}, u32[]{:S(2)}) collective-permute-start(bf16[1,24,24,128]{3,2,1,0:T(8,128)(2,1)S(1)} %get-tuple-element.70), channel_id=1, source_target_pairs={{0,4},{4,8},{8,12},{1,5},{5,9},{9,13},{2,6},{6,10},{10,14},{3,7},{... | collective-permute-start | bytes 442376 | tf_op jit(solution)/shard_map/ppermute | solution.py:680
  6.6 8.8 %collective-permute-start.1 = (bf16[1,24,24,128]{3,2,1,0:T(8,128)(2,1)S(1)}, bf16[1,24,24,128]{3,2,1,0:T(8,128)(2,1)S(1)}, u32[]{:S(2)}, u32[]{:S(2)}) collective-permute-start(bf16[1,24,24,128]{3,2,1,0:T(8,128)(2,1)S(1)} %get-tuple-element.69), channel_id=1, source_target_pairs={{4,0},{8,4},{12,8},{5,1},{9,5},{13,9},{6,2},{10,6},{14,10},{7,3},{... | collective-permute-start | bytes 442376 | tf_op jit(solution)/shard_map/ppermute | solution.py:681
  8.8 14.6 %collective-permute-start.2 = (bf16[16,3456]{1,0:T(8,128)(2,1)S(1)}, bf16[16,3456]{1,0:T(8,128)(2,1)S(1)}, u32[]{:S(2)}, u32[]{:S(2)}) collective-permute-start(bf16[16,3456]{1,0:T(8,128)(2,1)S(1)} %dynamic-slice_bitcast_fusion), channel_id=1, source_target_pairs={{0,4},{4,8},{8,12},{12,0},{1,5},{5,9},{9,13},{13,1},{2,6},{6,10},{... | collective-permute-start | bytes 331784 | tf_op jit(solution)/shard_map/ppermute | solution.py:502
  11.5 12.0 %collective-permute-start.3 = (bf16[16,3456]{1,0:T(8,128)(2,1)S(1)}, bf16[16,3456]{1,0:T(8,128)(2,1)S(1)}, u32[]{:S(2)}, u32[]{:S(2)}) collective-permute-start(bf16[16,3456]{1,0:T(8,128)(2,1)S(1)} %dynamic-slice_bitcast_fusion), channel_id=1, source_target_pairs={{0,8},{4,12},{8,0},{12,4},{1,9},{5,13},{9,1},{13,5},{2,10},{6,14},... | collective-permute-start | bytes 331784 | tf_op jit(solution)/shard_map/ppermute | solution.py:502
  14.0 9.4 %collective-permute-start.4 = (bf16[16,3456]{1,0:T(8,128)(2,1)S(1)}, bf16[16,3456]{1,0:T(8,128)(2,1)S(1)}, u32[]{:S(2)}, u32[]{:S(2)}) collective-permute-start(bf16[16,3456]{1,0:T(8,128)(2,1)S(1)} %dynamic-slice_bitcast_fusion), channel_id=1, source_target_pairs={{0,12},{4,0},{8,4},{12,8},{1,13},{5,1},{9,5},{13,9},{2,14},{6,2},{... | collective-permute-start | bytes 331784 | tf_op jit(solution)/shard_map/ppermute | solution.py:502
  15.4 1.1 %copy-start = (bf16[1,4,24,24,128]{4,3,2,1,0:T(8,128)(2,1)S(1)}, bf16[1,4,24,24,128]{4,3,2,1,0:T(8,128)(2,1)}, u32[]{:S(2)}) copy-start(bf16[1,4,24,24,128]{4,3,2,1,0:T(8,128)(2,1)} %param.5) | copy-start | bytes 1769476
  16.5 1.2 %copy-start.3 = (bf16[3456,128]{1,0:T(8,128)(2,1)S(1)}, bf16[3456,128]{1,0:T(8,128)(2,1)}, u32[]{:S(2)}) copy-start(bf16[3456,128]{1,0:T(8,128)(2,1)} %kernel.1) | copy-start | bytes 2654212
  17.6 17.3 %copy-start.2 = (bf16[3456,64]{0,1:T(8,128)(2,1)S(1)}, bf16[3456,64]{0,1:T(8,128)(2,1)}, u32[]{:S(2)}) copy-start(bf16[3456,64]{0,1:T(8,128)(2,1)} %param.8) | copy-start | bytes 1327108
  17.6 17.3 %copy-start.4 = (f32[256,4]{0,1:T(4,128)S(1)}, f32[256,4]{0,1:T(4,128)}, u32[]{:S(2)}) copy-start(f32[256,4]{0,1:T(4,128)} %param.9) | copy-start | bytes 12292
  17.6 17.3 %copy-start.5 = (f32[1,4]{1,0:T(1,128)S(1)}, f32[1,4]{1,0:T(1,128)}, u32[]{:S(2)}) copy-start(f32[1,4]{1,0:T(1,128)} %wanted.1) | copy-start | bytes 52
  23.5 9.8 %collective-permute-start.5 = (bf16[48,3456]{1,0:T(8,128)(2,1)S(1)}, bf16[48,3456]{1,0:T(8,128)(2,1)S(1)}, u32[]{:S(2)}, u32[]{:S(2)}) collective-permute-start(bf16[48,3456]{1,0:T(8,128)(2,1)S(1)} %shard_map.77.w1), channel_id=1, source_target_pairs={{0,2},{2,0},{1,3},{3,1},{4,6},{6,4},{5,7},{7,5},{8,10},{10,8},{9,1... | collective-permute-start | bytes 995336 | tf_op jit(solution)/shard_map/ppermute | solution.py:502
  25.1 6.4 %collective-permute-start.6 = (bf16[2,144,128]{2,1,0:T(8,128)(2,1)S(1)}, bf16[2,144,128]{2,1,0:T(8,128)(2,1)S(1)}, u32[]{:S(2)}, u32[]{:S(2)}) collective-permute-start(bf16[2,144,128]{2,1,0:T(8,128)(2,1)S(1)} %get-tuple-element.40.p0), channel_id=1, source_target_pairs={{0,4},{4,8},{8,12},{12,0},{1,5},{5,9},{9,13},{13,1},{2,6},{6,10},{... | collective-permute-start | bytes 221192 | tf_op jit(solution)/shard_map/ppermute | solution.py:502
  27.2 6.0 %collective-permute-start.7 = (bf16[2,144,128]{2,1,0:T(8,128)(2,1)S(1)}, bf16[2,144,128]{2,1,0:T(8,128)(2,1)S(1)}, u32[]{:S(2)}, u32[]{:S(2)}) collective-permute-start(bf16[2,144,128]{2,1,0:T(8,128)(2,1)S(1)} %get-tuple-element.40.p0), channel_id=1, source_target_pairs={{0,8},{4,12},{8,0},{12,4},{1,9},{5,13},{9,1},{13,5},{2,10},{6,14},... | collective-permute-start | bytes 221192 | tf_op jit(solution)/shard_map/ppermute | solution.py:502
  27.5 5.8 %collective-permute-start.8 = (bf16[2,144,128]{2,1,0:T(8,128)(2,1)S(1)}, bf16[2,144,128]{2,1,0:T(8,128)(2,1)S(1)}, u32[]{:S(2)}, u32[]{:S(2)}) collective-permute-start(bf16[2,144,128]{2,1,0:T(8,128)(2,1)S(1)} %get-tuple-element.40.p0), channel_id=1, source_target_pairs={{0,12},{4,0},{8,4},{12,8},{1,13},{5,1},{9,5},{13,9},{2,14},{6,2},{... | collective-permute-start | bytes 221192 | tf_op jit(solution)/shard_map/ppermute | solution.py:502
  30.4 2.9 %collective-permute-start.9 = (bf16[48,3456]{1,0:T(8,128)(2,1)S(1)}, bf16[48,3456]{1,0:T(8,128)(2,1)S(1)}, u32[]{:S(2)}, u32[]{:S(2)}) collective-permute-start(bf16[48,3456]{1,0:T(8,128)(2,1)S(1)} %shard_map.77.w1), channel_id=1, source_target_pairs={{0,1},{1,0},{2,3},{3,2},{4,5},{5,4},{6,7},{7,6},{8,9},{9,8},{10,11... | collective-permute-start | bytes 995336 | tf_op jit(solution)/shard_map/ppermute | solution.py:502
  33.3 1.6 %collective-permute-start.10 = (bf16[48,3456]{1,0:T(8,128)(2,1)S(1)}, bf16[48,3456]{1,0:T(8,128)(2,1)S(1)}, u32[]{:S(2)}, u32[]{:S(2)}) collective-permute-start(bf16[48,3456]{1,0:T(8,128)(2,1)S(1)} %collective-permute-done.5.w3), channel_id=1, source_target_pairs={{0,1},{1,0},{2,3},{3,2},{4,5},{5,4},{6,7},{7,6},{8,9},{9,8},{10,11... | collective-permute-start | bytes 995336 | tf_op jit(solution)/shard_map/ppermute | solution.py:502
  34.9 7.2 %copy-start.1 = (bf16[1,4,24,24,128]{4,3,2,1,0:T(8,128)(2,1)S(1)}, bf16[1,4,24,24,128]{4,3,2,1,0:T(8,128)(2,1)}, u32[]{:S(2)}) copy-start(bf16[1,4,24,24,128]{4,3,2,1,0:T(8,128)(2,1)} %param.5) | copy-start | bytes 1769476
  46.2 2.7 %collective-permute-start.11 = (f32[1728,128]{1,0:T(8,128)S(1)}, f32[1728,128]{1,0:T(8,128)S(1)}, u32[]{:S(2)}, u32[]{:S(2)}) collective-permute-start(f32[1728,128]{1,0:T(8,128)S(1)} %get-tuple-element.48), channel_id=1, source_target_pairs={{0,1},{1,0},{2,3},{3,2},{4,5},{5,4},{6,7},{7,6},{8,9},{9,8},{10,11... | collective-permute-start | bytes 2654216 | tf_op jit(solution)/shard_map/ppermute | solution.py:502
  48.4 1.9 %collective-permute-start.13 = (f32[872,128]{1,0:T(8,128)S(1)}, f32[872,128]{1,0:T(8,128)S(1)}, u32[]{:S(2)}, u32[]{:S(2)}) collective-permute-start(f32[872,128]{1,0:T(8,128)S(1)} %get-tuple-element.58), channel_id=1, source_target_pairs={{0,1},{1,0},{2,3},{3,2},{4,5},{5,4},{6,7},{7,6},{8,9},{9,8},{10,11... | collective-permute-start | bytes 1339400 | tf_op jit(solution)/shard_map/ppermute | solution.py:502
  49.0 7.5 %collective-permute-start.12 = (bf16[864,128]{1,0:T(8,128)(2,1)S(1)}, bf16[864,128]{1,0:T(8,128)(2,1)S(1)}, u32[]{:S(2)}, u32[]{:S(2)}) collective-permute-start(bf16[864,128]{1,0:T(8,128)(2,1)S(1)} %get-tuple-element.50), channel_id=1, source_target_pairs={{0,2},{2,0},{1,3},{3,1},{4,6},{6,4},{5,7},{7,5},{8,10},{10,8},{9,1... | collective-permute-start | bytes 663560 | tf_op jit(solution)/shard_map/ppermute | solution.py:502
  56.6 13.5 %collective-permute-start.18 = (f32[872,128]{1,0:T(8,128)S(1)}, f32[872,128]{1,0:T(8,128)S(1)}, u32[]{:S(2)}, u32[]{:S(2)}) collective-permute-start(f32[872,128]{1,0:T(8,128)S(1)} %add.85), channel_id=1, source_target_pairs={{0,2},{2,0},{1,3},{3,1},{4,6},{6,4},{5,7},{7,5},{8,10},{10,8},{9,1... | collective-permute-start | bytes 1339400 | tf_op jit(solution)/shard_map/ppermute | solution.py:502
  57.2 6.5 %collective-permute-start.14 = (bf16[216,128]{1,0:T(8,128)(2,1)S(1)}, bf16[216,128]{1,0:T(8,128)(2,1)S(1)}, u32[]{:S(2)}, u32[]{:S(2)}) collective-permute-start(bf16[216,128]{1,0:T(8,128)(2,1)S(1)} %get-tuple-element.59), channel_id=1, source_target_pairs={{0,4},{4,8},{8,12},{12,0},{1,5},{5,9},{9,13},{13,1},{2,6},{6,10},{... | collective-permute-start | bytes 165896 | tf_op jit(solution)/shard_map/ppermute | solution.py:502
  58.7 5.0 %collective-permute-start.15 = (bf16[216,128]{1,0:T(8,128)(2,1)S(1)}, bf16[216,128]{1,0:T(8,128)(2,1)S(1)}, u32[]{:S(2)}, u32[]{:S(2)}) collective-permute-start(bf16[216,128]{1,0:T(8,128)(2,1)S(1)} %get-tuple-element.60), channel_id=1, source_target_pairs={{0,12},{4,0},{8,4},{12,8},{1,13},{5,1},{9,5},{13,9},{2,14},{6,2},{... | collective-permute-start | bytes 165896 | tf_op jit(solution)/shard_map/ppermute | solution.py:502
  61.0 5.1 %collective-permute-start.16 = (bf16[216,128]{1,0:T(8,128)(2,1)S(1)}, bf16[216,128]{1,0:T(8,128)(2,1)S(1)}, u32[]{:S(2)}, u32[]{:S(2)}) collective-permute-start(bf16[216,128]{1,0:T(8,128)(2,1)S(1)} %get-tuple-element.61), channel_id=1, source_target_pairs={{0,8},{4,12},{8,0},{12,4},{1,9},{5,13},{9,1},{13,5},{2,10},{6,14},... | collective-permute-start | bytes 165896 | tf_op jit(solution)/shard_map/ppermute | solution.py:502
  66.1 6.0 %collective-permute-start.17 = (bf16[216,128]{1,0:T(8,128)(2,1)S(1)}, bf16[216,128]{1,0:T(8,128)(2,1)S(1)}, u32[]{:S(2)}, u32[]{:S(2)}) collective-permute-start(bf16[216,128]{1,0:T(8,128)(2,1)S(1)} %get-tuple-element.68), channel_id=1, source_target_pairs={{0,4},{4,8},{8,12},{12,0},{1,5},{5,9},{9,13},{13,1},{2,6},{6,10},{... | collective-permute-start | bytes 165896 | tf_op jit(solution)/shard_map/ppermute | solution.py:502
  66.3 5.8 %collective-permute-start.19 = (bf16[216,128]{1,0:T(8,128)(2,1)S(1)}, bf16[216,128]{1,0:T(8,128)(2,1)S(1)}, u32[]{:S(2)}, u32[]{:S(2)}) collective-permute-start(bf16[216,128]{1,0:T(8,128)(2,1)S(1)} %get-tuple-element.68), channel_id=1, source_target_pairs={{0,12},{4,0},{8,4},{12,8},{1,13},{5,1},{9,5},{13,9},{2,14},{6,2},{... | collective-permute-start | bytes 165896 | tf_op jit(solution)/shard_map/ppermute | solution.py:502
  70.0 5.1 %collective-permute-start.20 = (bf16[216,128]{1,0:T(8,128)(2,1)S(1)}, bf16[216,128]{1,0:T(8,128)(2,1)S(1)}, u32[]{:S(2)}, u32[]{:S(2)}) collective-permute-start(bf16[216,128]{1,0:T(8,128)(2,1)S(1)} %get-tuple-element.68), channel_id=1, source_target_pairs={{0,8},{4,12},{8,0},{12,4},{1,9},{5,13},{9,1},{13,5},{2,10},{6,14},... | collective-permute-start | bytes 165896 | tf_op jit(solution)/shard_map/ppermute | solution.py:502
  72.1 9.2 %collective-permute-start.23 = (f32[872,128]{1,0:T(8,128)S(1)}, f32[872,128]{1,0:T(8,128)S(1)}, u32[]{:S(2)}, u32[]{:S(2)}) collective-permute-start(f32[872,128]{1,0:T(8,128)S(1)} %add.91), channel_id=1, source_target_pairs={{0,1},{1,0},{2,3},{3,2},{4,5},{5,4},{6,7},{7,6},{8,9},{9,8},{10,11... | collective-permute-start | bytes 1339400 | tf_op jit(solution)/shard_map/ppermute | solution.py:502
  75.1 6.0 %collective-permute-start.21 = (bf16[864,128]{1,0:T(8,128)(2,1)S(1)}, bf16[864,128]{1,0:T(8,128)(2,1)S(1)}, u32[]{:S(2)}, u32[]{:S(2)}) collective-permute-start(bf16[864,128]{1,0:T(8,128)(2,1)S(1)} %bitcast.46), channel_id=1, source_target_pairs={{0,2},{2,0},{1,3},{3,1},{4,6},{6,4},{5,7},{7,5},{8,10},{10,8},{9,1... | collective-permute-start | bytes 663560 | tf_op jit(solution)/shard_map/ppermute | solution.py:502
  81.1 1.9 %collective-permute-start.22 = (bf16[1728,128]{1,0:T(8,128)(2,1)S(1)}, bf16[1728,128]{1,0:T(8,128)(2,1)S(1)}, u32[]{:S(2)}, u32[]{:S(2)}) collective-permute-start(bf16[1728,128]{1,0:T(8,128)(2,1)S(1)} %bitcast.44), channel_id=1, source_target_pairs={{0,1},{1,0},{2,3},{3,2},{4,5},{5,4},{6,7},{7,6},{8,9},{9,8},{10,11... | collective-permute-start | bytes 1327112 | tf_op jit(solution)/shard_map/ppermute | solution.py:502

commit v3 on v2

--- a/solution.py
+++ b/solution.py
@@ -325,13 +325,21 @@
         shift_ref[front : front + cells, :] = (slopes[where[0] * planes + k] * scale).astype(bf16).astype(f32)
         for e in range(3):
             g[e, k, wide : wide + cells, :] = shifted(shift_ref, cells, 1 - e).astype(bf16)
-    out = jnp.zeros((planes * cells, chans), f32)
+    out = None
     for a in range(3):
-        for b in range(3):
-            for e in range(3):
-                lhs = g[e, 2 - a : 2 - a + planes, (2 - b) * wide : (2 - b) * wide + cells, :].reshape(planes * cells, outs)
-                t = 9 * a + 3 * b + e
-                out = out + jnp.dot(lhs, w[:, t * chans : (t + 1) * chans], preferred_element_type=f32)
+        taps = [(b, e) for b in range(3) for e in range(3)]
+        lhs = jnp.concatenate(
+            [
+                g[e, 2 - a : 2 - a + planes, (2 - b) * wide : (2 - b) * wide + cells, :].reshape(planes * cells, outs)
+                for b, e in taps
+            ],
+            axis=1,
+        )
+        rhs = jnp.concatenate(
+            [w[:, (9 * a + 3 * b + e) * chans : (9 * a + 3 * b + e + 1) * chans] for b, e in taps], axis=0
+        )
+        part = jnp.dot(lhs, rhs, preferred_element_type=f32)
+        out = part if out is None else out + part
     keep = lax.broadcasted_iota(jnp.int32, (planes * cells, chans), 0) % wide < side
     pooled_grad[...] = jnp.where(keep, out, 0.0).reshape(planes, cells, chans)
 
@@ -421,18 +429,37 @@
     )
 
 
-def entry(vol, kernel, other, first, last, piece):
-    rows = piece.shape[0]
-    copy = 2 * lax.axis_index("dp") + lax.axis_index("rep")
-    piece[...] = kernel[pl.ds(pl.multiple_of(copy * rows, rows), rows), :]
+def entry(vol, first, last):
     first[0] = vol[0]
     last[0] = vol[vol.shape[0] - 1]
 
 
-def run_entry(vol, kernel, other):
+def run_entry(vol):
     plane = jax.ShapeDtypeStruct((1,) + vol.shape[1:], bf16)
-    piece = jax.ShapeDtypeStruct((kernel.shape[0] // 4, kernel.shape[1]), bf16)
-    return call(entry, (plane, plane, piece), [], vol, kernel, other)
+    return call(entry, (plane, plane), [], vol)
+
+
+def widen(x, across, near, far, out, room, done):
+    rows = x.shape[0]
+    own = 2 * lax.axis_index("rep") + lax.axis_index("dp")
+    copies = []
+    for k, part in enumerate((x, across, near, far)):
+        room[k] = part[...].astype(f32)
+        to = out.at[pl.ds(pl.multiple_of((own ^ k) * rows, 8), rows)]
+        copies.append(pltpu.make_async_copy(room.at[k], to, done.at[k]))
+        copies[-1].start()
+    for copy in copies:
+        copy.wait()
+
+
+def run_widen(x, across, near, far):
+    rows, cols = x.shape
+    return call(
+        widen,
+        jax.ShapeDtypeStruct((4 * rows, cols), f32),
+        [pltpu.VMEM((4, rows, cols), f32), pltpu.SemaphoreType.DMA((4,))],
+        x, across, near, far, far_outs=(0,),
+    )
 
 
 def join(r0, r1, r2, out):
@@ -723,9 +750,11 @@
     x = whole.reshape(-1, x.shape[1])
     second = gathered(second, "rep").reshape(-1, second.shape[1])
     second_total, head_total = run_spread_second(second, share, outs)
-    for axis in ("dp", "rep"):
-        x = gathered(x, axis).reshape(-1, x.shape[1])
-    first_total = x.astype(f32)
+    across_x = turn(x, "dp", 1)
+    near = turn(x, "rep", 1)
+    across_x, near, second_total, head_total = lax.optimization_barrier((across_x, near, second_total, head_total))
+    far = turn(across_x, "rep", 1)
+    first_total = run_widen(x, across_x, near, far)
     return (first_total, second_total.T, head_total.T)
 
 

time: 84.7 us -> 84.3 us (level)
  other arithmetic: 1.53 us -> 0.17 us
  Pallas kernels: 20.2 us -> 21.5 us
    convert_element_type x1 -> x0, other arithmetic: 1.38 us -> none  [shards(): first_total = x.astype(f32)]
    pallas_call x8 -> x9, Pallas kernels: 20.2 us -> 21.5 us  [call(): pl.pallas_call(body, out_shape=outs, in_specs=specs, out_specs=out_specs,...]
    ppermute x22 -> x23, starting transfers between devices: 24.6 us -> 24.6 us  [turn(): return lax.ppermute(x, axis, [(i, (i + step) % size) for i in range(size)])]
    ppermute x22 -> x23, waiting for transfers between devices: 26.1 us -> 26.1 us  [turn(): return lax.ppermute(x, axis, [(i, (i + step) % size) for i in range(size)])]
  transfers between devices with their start and end apart: 24 -> 25, of which waited for: 11 -> 11; matrix products, arithmetic and copies ran while one was open for 2% -> 2% of each run, Pallas kernels for 11% -> 11%
where the time goes in v3:
time: 84.3 us; the launch traced here: 84 us
  starting transfers between devices  30.8 us (37%)
  waiting for transfers between devices  26.1 us (31%)
  Pallas kernels  21.5 us (26%)
  local copies, waits for them, and re-layouts  4.37 us (5%)
  between operations  1.1 us (1%)
    ppermute x23, waiting for transfers between devices, turn(): return lax.ppermute(x, axis, [(i, (i + step) % size) for i in range(size)])  26.1 us
    ppermute x23, starting transfers between devices, turn(): return lax.ppermute(x, axis, [(i, (i + step) % size) for i in range(size)])  24.6 us
    pallas_call x9, Pallas kernels, call(): pl.pallas_call(body, out_shape=outs, in_specs=specs, out_specs=out_specs,...  21.5 us
    ppermute x1, starting transfers between devices, neighbours(): before = lax.ppermute(last, 'space', up)  4.94 us
    unnamed x12, local copies, waits for them, and re-layouts  2.25 us
  transfers between devices with their start and end apart: 25, of which 11 were waited for; matrix products, arithmetic and copies ran while one was open for 2% of the time, Pallas kernels for 11%

profile of v3, /device:TPU:0, one launch (start us, length us, event | category | flops | bytes accessed | tf_op | source)
XLA Modules:
  0.0 84.0 jit_solution(14163918811043365353)
XLA Ops:
  0.6 1.0 %slice_bitcast_fusion = (bf16[1,24,24,128]{3,2,1,0:T(8,128)(2,1)S(1)}, bf16[1,24,24,128]{3,2,1,0:T(8,128)(2,1)S(1)}) fusion(bf16[1,4,24,24,128]{4,3,2,1,0:T(8,128)(2,1)} %param.5), kind=kLoop, calls=%fused_computation.2 | loop fusion | bytes 589824 | tf_op jit(solution)/shard_map/slice | solution.py:721
  1.6 4.9 %collective-permute-start = (bf16[1,24,24,128]{3,2,1,0:T(8,128)(2,1)S(1)}, bf16[1,24,24,128]{3,2,1,0:T(8,128)(2,1)S(1)}, u32[]{:S(2)}, u32[]{:S(2)}) collective-permute-start(bf16[1,24,24,128]{3,2,1,0:T(8,128)(2,1)S(1)} %get-tuple-element.78), channel_id=1, source_target_pairs={{0,4},{4,8},{8,12},{1,5},{5,9},{9,13},{2,6},{6,10},{10,14},{3,7},{... | collective-permute-start | bytes 442376 | tf_op jit(solution)/shard_map/ppermute | solution.py:707
  6.6 1.3 %collective-permute-start.1 = (bf16[1,24,24,128]{3,2,1,0:T(8,128)(2,1)S(1)}, bf16[1,24,24,128]{3,2,1,0:T(8,128)(2,1)S(1)}, u32[]{:S(2)}, u32[]{:S(2)}) collective-permute-start(bf16[1,24,24,128]{3,2,1,0:T(8,128)(2,1)S(1)} %get-tuple-element.77), channel_id=1, source_target_pairs={{4,0},{8,4},{12,8},{5,1},{9,5},{13,9},{6,2},{10,6},{14,10},{7,3},{... | collective-permute-start | bytes 442376 | tf_op jit(solution)/shard_map/ppermute | solution.py:708
  7.9 0.9 %dynamic-slice_bitcast_fusion = bf16[16,3456]{1,0:T(8,128)(2,1)S(1)} fusion(bf16[3456,64]{0,1:T(8,128)(2,1)} %param.8, s32[]{:T(128)S(6)} %select_n.50), kind=kLoop, calls=%fused_computation.5 | loop fusion | bytes 221188 | tf_op jit(solution)/shard_map/dynamic_slice | solution.py:723
  8.8 2.6 %collective-permute-start.2 = (bf16[16,3456]{1,0:T(8,128)(2,1)S(1)}, bf16[16,3456]{1,0:T(8,128)(2,1)S(1)}, u32[]{:S(2)}, u32[]{:S(2)}) collective-permute-start(bf16[16,3456]{1,0:T(8,128)(2,1)S(1)} %dynamic-slice_bitcast_fusion), channel_id=1, source_target_pairs={{0,4},{4,8},{8,12},{12,0},{1,5},{5,9},{9,13},{13,1},{2,6},{6,10},{... | collective-permute-start | bytes 331784 | tf_op jit(solution)/shard_map/ppermute | solution.py:529
  11.5 2.6 %collective-permute-start.3 = (bf16[16,3456]{1,0:T(8,128)(2,1)S(1)}, bf16[16,3456]{1,0:T(8,128)(2,1)S(1)}, u32[]{:S(2)}, u32[]{:S(2)}) collective-permute-start(bf16[16,3456]{1,0:T(8,128)(2,1)S(1)} %dynamic-slice_bitcast_fusion), channel_id=1, source_target_pairs={{0,8},{4,12},{8,0},{12,4},{1,9},{5,13},{9,1},{13,5},{2,10},{6,14},... | collective-permute-start | bytes 331784 | tf_op jit(solution)/shard_map/ppermute | solution.py:529
  14.0 1.3 %collective-permute-start.4 = (bf16[16,3456]{1,0:T(8,128)(2,1)S(1)}, bf16[16,3456]{1,0:T(8,128)(2,1)S(1)}, u32[]{:S(2)}, u32[]{:S(2)}) collective-permute-start(bf16[16,3456]{1,0:T(8,128)(2,1)S(1)} %dynamic-slice_bitcast_fusion), channel_id=1, source_target_pairs={{0,12},{4,0},{8,4},{12,8},{1,13},{5,1},{9,5},{13,9},{2,14},{6,2},{... | collective-permute-start | bytes 331784 | tf_op jit(solution)/shard_map/ppermute | solution.py:529
  15.4 1.1 %copy-done = bf16[1,4,24,24,128]{4,3,2,1,0:T(8,128)(2,1)S(1)} copy-done((bf16[1,4,24,24,128]{4,3,2,1,0:T(8,128)(2,1)S(1)}, bf16[1,4,24,24,128]{4,3,2,1,0:T(8,128)(2,1)}, u32[]{:S(2)}) %copy-start) | copy-done | bytes 589848
  16.5 1.2 %copy-done.3 = bf16[3456,128]{1,0:T(8,128)(2,1)S(1)} copy-done((bf16[3456,128]{1,0:T(8,128)(2,1)S(1)}, bf16[3456,128]{1,0:T(8,128)(2,1)}, u32[]{:S(2)}) %copy-start.3) | copy-done | bytes 884760
  17.6 5.8 %shard_map.76 = (bf16[2,144,128]{2,1,0:T(8,128)(2,1)S(1)}, f32[4,768,128]{2,1,0:T(8,128)S(1)}) custom-call(bf16[4,24,24,128]{3,2,1,0:T(8,128)(2,1)S(1)} %bitcast.29, bf16[1,24,24,128]{3,2,1,0:T(8,128)(2,1)S(1)} %collective-permute-done.before, bf16[1,24,24,128]{3,2,1,0:T(8,128)(2,1)S(1)} %collective-permute-done.1.after, bf16[3456,128]{1,0:T(8,128)(2,1)S(1)} %copy-done.3), custom_call_target="tpu_custom_call" | custom-call | flops 8000000000 | tf_op jit(solution)/shard_map/pallas_call | solution.py:24
  23.4 0.0 collective-permute-done.2.r0
  23.5 0.0 collective-permute-done.4.r2
  23.5 1.6 %collective-permute-start.5 = (bf16[48,3456]{1,0:T(8,128)(2,1)S(1)}, bf16[48,3456]{1,0:T(8,128)(2,1)S(1)}, u32[]{:S(2)}, u32[]{:S(2)}) collective-permute-start(bf16[48,3456]{1,0:T(8,128)(2,1)S(1)} %shard_map.77.w1), channel_id=1, source_target_pairs={{0,2},{2,0},{1,3},{3,1},{4,6},{6,4},{5,7},{7,5},{8,10},{10,8},{9,1... | collective-permute-start | bytes 995336 | tf_op jit(solution)/shard_map/ppermute | solution.py:529
  25.1 2.2 %collective-permute-start.6 = (bf16[2,144,128]{2,1,0:T(8,128)(2,1)S(1)}, bf16[2,144,128]{2,1,0:T(8,128)(2,1)S(1)}, u32[]{:S(2)}, u32[]{:S(2)}) collective-permute-start(bf16[2,144,128]{2,1,0:T(8,128)(2,1)S(1)} %get-tuple-element.44.p0), channel_id=1, source_target_pairs={{0,4},{4,8},{8,12},{12,0},{1,5},{5,9},{9,13},{13,1},{2,6},{6,10},{... | collective-permute-start | bytes 221192 | tf_op jit(solution)/shard_map/ppermute | solution.py:529
  27.2 0.3 collective-permute-start.7
  27.5 2.9 %collective-permute-start.8 = (bf16[2,144,128]{2,1,0:T(8,128)(2,1)S(1)}, bf16[2,144,128]{2,1,0:T(8,128)(2,1)S(1)}, u32[]{:S(2)}, u32[]{:S(2)}) collective-permute-start(bf16[2,144,128]{2,1,0:T(8,128)(2,1)S(1)} %get-tuple-element.44.p0), channel_id=1, source_target_pairs={{0,12},{4,0},{8,4},{12,8},{1,13},{5,1},{9,5},{13,9},{2,14},{6,2},{... | collective-permute-start | bytes 221192 | tf_op jit(solution)/shard_map/ppermute | solution.py:529
  30.4 1.0 %collective-permute-done.6.p1 = bf16[2,144,128]{2,1,0:T(8,128)(2,1)S(1)} collective-permute-done((bf16[2,144,128]{2,1,0:T(8,128)(2,1)S(1)}, bf16[2,144,128]{2,1,0:T(8,128)(2,1)S(1)}, u32[]{:S(2)}, u32[]{:S(2)}) %collective-permute-start.6) | collective-permute-done | bytes 73760 | tf_op jit(solution)/shard_map/ppermute | solution.py:529
  31.4 1.9 %collective-permute-done.7.p2 = bf16[2,144,128]{2,1,0:T(8,128)(2,1)S(1)} collective-permute-done((bf16[2,144,128]{2,1,0:T(8,128)(2,1)S(1)}, bf16[2,144,128]{2,1,0:T(8,128)(2,1)S(1)}, u32[]{:S(2)}, u32[]{:S(2)}) %collective-permute-start.7) | collective-permute-done | bytes 73760 | tf_op jit(solution)/shard_map/ppermute | solution.py:529
  33.3 0.0 collective-permute-start.10
  33.3 1.6 %collective-permute-done.10.w4 = bf16[48,3456]{1,0:T(8,128)(2,1)S(1)} collective-permute-done((bf16[48,3456]{1,0:T(8,128)(2,1)S(1)}, bf16[48,3456]{1,0:T(8,128)(2,1)S(1)}, u32[]{:S(2)}, u32[]{:S(2)}) %collective-permute-start.10) | collective-permute-done | bytes 331808 | tf_op jit(solution)/shard_map/ppermute | solution.py:529
  34.9 0.0 copy-start.1
  34.9 7.2 %shard_map.78 = (f32[2,192,128]{2,1,0:T(8,128)S(1)}, bf16[8,192,64]{2,1,0:T(8,128)(2,1)S(1)}, f32[4,256]{1,0:T(4,128)S(1)}) custom-call(bf16[2,144,128]{2,1,0:T(8,128)(2,1)S(1)} %get-tuple-element.44.p0, bf16[2,144,128]{2,1,0:T(8,128)(2,1)S(1)} %collective-permute-done.6.p1, bf16[2,144,128]{2,1,0:T(8,128)(2,1)S(1)} %collective-permute-done.7.p2, ...), custom_call_target="tpu_custom_call" | custom-call | flops 8000000000 | tf_op jit(solution)/shard_map/pallas_call | solution.py:24
  42.1 4.1 %shard_map.79 = (f32[1728,128]{1,0:T(8,128)S(1)}, f32[1728,128]{1,0:T(8,128)S(1)}) custom-call(bf16[4,24,24,128]{3,2,1,0:T(8,128)(2,1)S(1)} %bitcast.30, bf16[1,24,24,128]{3,2,1,0:T(8,128)(2,1)S(1)} %collective-permute-done.before, bf16[1,24,24,128]{3,2,1,0:T(8,128)(2,1)S(1)} %collective-permute-done.1.after, f32[2,192,128]{2,1,0:T(8,128)S(1)} %get-tuple-element.49.spread, ...), custom_call_target="tpu_custom_call" | custom-call | flops 7000000000 | tf_op jit(solution)/shard_map/pallas_call | solution.py:24
  46.2 0.2 collective-permute-start.11
  46.4 2.1 %shard_map.82 = (f32[872,128]{1,0:T(8,128)S(1)}, f32[872,128]{1,0:T(8,128)S(1)}) custom-call(bf16[2,144,128]{2,1,0:T(8,128)(2,1)S(1)} %get-tuple-element.44.p0, bf16[2,144,128]{2,1,0:T(8,128)(2,1)S(1)} %collective-permute-done.6.p1, bf16[2,144,128]{2,1,0:T(8,128)(2,1)S(1)} %collective-permute-done.7.p2, bf16[2,144,128]{2,1,0:T(8,128)(2,1)S(1)} %collective-permute-done.8.p3, ...), custom_call_target="tpu_custom_call" | custom-call | flops 4000000000 | tf_op jit(solution)/shard_map/pallas_call | solution.py:24
  48.5 0.4 collective-permute-start.13
  48.9 0.1 shard_map.80
  49.0 0.6 collective-permute-start.12
  49.6 0.7 collective-permute-done.13
  50.4 6.1 %collective-permute-done.12.came = bf16[864,128]{1,0:T(8,128)(2,1)S(1)} collective-permute-done((bf16[864,128]{1,0:T(8,128)(2,1)S(1)}, bf16[864,128]{1,0:T(8,128)(2,1)S(1)}, u32[]{:S(2)}, u32[]{:S(2)}) %collective-permute-start.12) | collective-permute-done | bytes 221216 | tf_op jit(solution)/shard_map/ppermute | solution.py:529
  56.6 0.6 collective-permute-start.18
  57.2 1.6 %collective-permute-start.14 = (bf16[216,128]{1,0:T(8,128)(2,1)S(1)}, bf16[216,128]{1,0:T(8,128)(2,1)S(1)}, u32[]{:S(2)}, u32[]{:S(2)}) collective-permute-start(bf16[216,128]{1,0:T(8,128)(2,1)S(1)} %get-tuple-element.63), channel_id=1, source_target_pairs={{0,4},{4,8},{8,12},{12,0},{1,5},{5,9},{9,13},{13,1},{2,6},{6,10},{... | collective-permute-start | bytes 165896 | tf_op jit(solution)/shard_map/ppermute | solution.py:529
  58.7 2.3 %collective-permute-start.15 = (bf16[216,128]{1,0:T(8,128)(2,1)S(1)}, bf16[216,128]{1,0:T(8,128)(2,1)S(1)}, u32[]{:S(2)}, u32[]{:S(2)}) collective-permute-start(bf16[216,128]{1,0:T(8,128)(2,1)S(1)} %get-tuple-element.64), channel_id=1, source_target_pairs={{0,12},{4,0},{8,4},{12,8},{1,13},{5,1},{9,5},{13,9},{2,14},{6,2},{... | collective-permute-start | bytes 165896 | tf_op jit(solution)/shard_map/ppermute | solution.py:529
  61.0 0.1 collective-permute-start.16
  61.1 2.6 %collective-permute-done.14 = bf16[216,128]{1,0:T(8,128)(2,1)S(1)} collective-permute-done((bf16[216,128]{1,0:T(8,128)(2,1)S(1)}, bf16[216,128]{1,0:T(8,128)(2,1)S(1)}, u32[]{:S(2)}, u32[]{:S(2)}) %collective-permute-start.14) | collective-permute-done | bytes 55328 | tf_op jit(solution)/shard_map/ppermute | solution.py:529
  63.7 2.4 %collective-permute-done.16 = bf16[216,128]{1,0:T(8,128)(2,1)S(1)} collective-permute-done((bf16[216,128]{1,0:T(8,128)(2,1)S(1)}, bf16[216,128]{1,0:T(8,128)(2,1)S(1)}, u32[]{:S(2)}, u32[]{:S(2)}) %collective-permute-start.16) | collective-permute-done | bytes 55328 | tf_op jit(solution)/shard_map/ppermute | solution.py:529
  66.1 0.1 bitcast_dynamic-update-slice_fusion.5
  66.2 0.1 collective-permute-start.17
  66.3 3.7 %collective-permute-start.19 = (bf16[216,128]{1,0:T(8,128)(2,1)S(1)}, bf16[216,128]{1,0:T(8,128)(2,1)S(1)}, u32[]{:S(2)}, u32[]{:S(2)}) collective-permute-start(bf16[216,128]{1,0:T(8,128)(2,1)S(1)} %get-tuple-element.76), channel_id=1, source_target_pairs={{0,12},{4,0},{8,4},{12,8},{1,13},{5,1},{9,5},{13,9},{2,14},{6,2},{... | collective-permute-start | bytes 165896 | tf_op jit(solution)/shard_map/ppermute | solution.py:529
  70.0 0.1 add.72
  70.1 2.1 %collective-permute-done.17 = bf16[216,128]{1,0:T(8,128)(2,1)S(1)} collective-permute-done((bf16[216,128]{1,0:T(8,128)(2,1)S(1)}, bf16[216,128]{1,0:T(8,128)(2,1)S(1)}, u32[]{:S(2)}, u32[]{:S(2)}) %collective-permute-start.17) | collective-permute-done | bytes 55328 | tf_op jit(solution)/shard_map/ppermute | solution.py:529
  72.2 2.9 %collective-permute-done.20 = bf16[216,128]{1,0:T(8,128)(2,1)S(1)} collective-permute-done((bf16[216,128]{1,0:T(8,128)(2,1)S(1)}, bf16[216,128]{1,0:T(8,128)(2,1)S(1)}, u32[]{:S(2)}, u32[]{:S(2)}) %collective-permute-start.20) | collective-permute-done | bytes 55328 | tf_op jit(solution)/shard_map/ppermute | solution.py:529
  75.1 1.6 %collective-permute-start.21 = (bf16[864,128]{1,0:T(8,128)(2,1)S(1)}, bf16[864,128]{1,0:T(8,128)(2,1)S(1)}, u32[]{:S(2)}, u32[]{:S(2)}) collective-permute-start(bf16[864,128]{1,0:T(8,128)(2,1)S(1)} %bitcast.26), channel_id=1, source_target_pairs={{0,2},{2,0},{1,3},{3,1},{4,6},{6,4},{5,7},{7,5},{8,10},{10,8},{9,1... | collective-permute-start | bytes 663560 | tf_op jit(solution)/shard_map/ppermute | solution.py:529
  76.7 0.1 broadcast_in_dim.31
  76.8 1.0 %shard_map.83 = (f32[64,3456]{1,0:T(8,128)}, f32[4,64]{1,0:T(4,128)}) custom-call(f32[1744,128]{1,0:T(8,128)S(1)} %bitcast.25), custom_call_target="tpu_custom_call" | custom-call | flops 2000000000 | tf_op jit(solution)/shard_map/pallas_call | solution.py:24
  77.8 3.3 %collective-permute-done.21.across = bf16[864,128]{1,0:T(8,128)(2,1)S(1)} collective-permute-done((bf16[864,128]{1,0:T(8,128)(2,1)S(1)}, bf16[864,128]{1,0:T(8,128)(2,1)S(1)}, u32[]{:S(2)}, u32[]{:S(2)}) %collective-permute-start.21) | collective-permute-done | bytes 221216 | tf_op jit(solution)/shard_map/ppermute | solution.py:529
  81.1 1.5 %collective-permute-done.24.far = bf16[864,128]{1,0:T(8,128)(2,1)S(1)} collective-permute-done((bf16[864,128]{1,0:T(8,128)(2,1)S(1)}, bf16[864,128]{1,0:T(8,128)(2,1)S(1)}, u32[]{:S(2)}, u32[]{:S(2)}) %collective-permute-start.24) | collective-permute-done | bytes 221216 | tf_op jit(solution)/shard_map/ppermute | solution.py:529
  82.6 1.3 %shard_map.84 = f32[3456,128]{1,0:T(8,128)} custom-call(bf16[864,128]{1,0:T(8,128)(2,1)S(1)} %bitcast.28, bf16[864,128]{1,0:T(8,128)(2,1)S(1)} %collective-permute-done.21.across, bf16[864,128]{1,0:T(8,128)(2,1)S(1)} %collective-permute-done.22.near, bf16[864,128]{1,0:T(8,128)(2,1)S(1)} %collective-permute-done.24.far), custom_call_target="tpu_custom_call" | custom-call | tf_op jit(solution)/shard_map/pallas_call | solution.py:24
  (35 shorter events, 0.3 us)
Async XLA Ops:
  1.6 13.7 %collective-permute-start = (bf16[1,24,24,128]{3,2,1,0:T(8,128)(2,1)S(1)}, bf16[1,24,24,128]{3,2,1,0:T(8,128)(2,1)S(1)}, u32[]{:S(2)}, u32[]{:S(2)}) collective-permute-start(bf16[1,24,24,128]{3,2,1,0:T(8,128)(2,1)S(1)} %get-tuple-element.78), channel_id=1, source_target_pairs={{0,4},{4,8},{8,12},{1,5},{5,9},{9,13},{2,6},{6,10},{10,14},{3,7},{... | collective-permute-start | bytes 442376 | tf_op jit(solution)/shard_map/ppermute | solution.py:707
  6.6 8.8 %collective-permute-start.1 = (bf16[1,24,24,128]{3,2,1,0:T(8,128)(2,1)S(1)}, bf16[1,24,24,128]{3,2,1,0:T(8,128)(2,1)S(1)}, u32[]{:S(2)}, u32[]{:S(2)}) collective-permute-start(bf16[1,24,24,128]{3,2,1,0:T(8,128)(2,1)S(1)} %get-tuple-element.77), channel_id=1, source_target_pairs={{4,0},{8,4},{12,8},{5,1},{9,5},{13,9},{6,2},{10,6},{14,10},{7,3},{... | collective-permute-start | bytes 442376 | tf_op jit(solution)/shard_map/ppermute | solution.py:708
  8.8 14.6 %collective-permute-start.2 = (bf16[16,3456]{1,0:T(8,128)(2,1)S(1)}, bf16[16,3456]{1,0:T(8,128)(2,1)S(1)}, u32[]{:S(2)}, u32[]{:S(2)}) collective-permute-start(bf16[16,3456]{1,0:T(8,128)(2,1)S(1)} %dynamic-slice_bitcast_fusion), channel_id=1, source_target_pairs={{0,4},{4,8},{8,12},{12,0},{1,5},{5,9},{9,13},{13,1},{2,6},{6,10},{... | collective-permute-start | bytes 331784 | tf_op jit(solution)/shard_map/ppermute | solution.py:529
  11.5 12.0 %collective-permute-start.3 = (bf16[16,3456]{1,0:T(8,128)(2,1)S(1)}, bf16[16,3456]{1,0:T(8,128)(2,1)S(1)}, u32[]{:S(2)}, u32[]{:S(2)}) collective-permute-start(bf16[16,3456]{1,0:T(8,128)(2,1)S(1)} %dynamic-slice_bitcast_fusion), channel_id=1, source_target_pairs={{0,8},{4,12},{8,0},{12,4},{1,9},{5,13},{9,1},{13,5},{2,10},{6,14},... | collective-permute-start | bytes 331784 | tf_op jit(solution)/shard_map/ppermute | solution.py:529
  14.0 9.4 %collective-permute-start.4 = (bf16[16,3456]{1,0:T(8,128)(2,1)S(1)}, bf16[16,3456]{1,0:T(8,128)(2,1)S(1)}, u32[]{:S(2)}, u32[]{:S(2)}) collective-permute-start(bf16[16,3456]{1,0:T(8,128)(2,1)S(1)} %dynamic-slice_bitcast_fusion), channel_id=1, source_target_pairs={{0,12},{4,0},{8,4},{12,8},{1,13},{5,1},{9,5},{13,9},{2,14},{6,2},{... | collective-permute-start | bytes 331784 | tf_op jit(solution)/shard_map/ppermute | solution.py:529
  15.4 1.1 %copy-start = (bf16[1,4,24,24,128]{4,3,2,1,0:T(8,128)(2,1)S(1)}, bf16[1,4,24,24,128]{4,3,2,1,0:T(8,128)(2,1)}, u32[]{:S(2)}) copy-start(bf16[1,4,24,24,128]{4,3,2,1,0:T(8,128)(2,1)} %param.5) | copy-start | bytes 1769476
  16.5 1.2 %copy-start.3 = (bf16[3456,128]{1,0:T(8,128)(2,1)S(1)}, bf16[3456,128]{1,0:T(8,128)(2,1)}, u32[]{:S(2)}) copy-start(bf16[3456,128]{1,0:T(8,128)(2,1)} %kernel.1) | copy-start | bytes 2654212
  17.6 17.3 %copy-start.2 = (bf16[3456,64]{0,1:T(8,128)(2,1)S(1)}, bf16[3456,64]{0,1:T(8,128)(2,1)}, u32[]{:S(2)}) copy-start(bf16[3456,64]{0,1:T(8,128)(2,1)} %param.8) | copy-start | bytes 1327108
  17.6 17.3 %copy-start.4 = (f32[256,4]{0,1:T(4,128)S(1)}, f32[256,4]{0,1:T(4,128)}, u32[]{:S(2)}) copy-start(f32[256,4]{0,1:T(4,128)} %param.9) | copy-start | bytes 12292
  17.6 17.3 %copy-start.5 = (f32[1,4]{1,0:T(1,128)S(1)}, f32[1,4]{1,0:T(1,128)}, u32[]{:S(2)}) copy-start(f32[1,4]{1,0:T(1,128)} %wanted.1) | copy-start | bytes 52
  23.5 9.8 %collective-permute-start.5 = (bf16[48,3456]{1,0:T(8,128)(2,1)S(1)}, bf16[48,3456]{1,0:T(8,128)(2,1)S(1)}, u32[]{:S(2)}, u32[]{:S(2)}) collective-permute-start(bf16[48,3456]{1,0:T(8,128)(2,1)S(1)} %shard_map.77.w1), channel_id=1, source_target_pairs={{0,2},{2,0},{1,3},{3,1},{4,6},{6,4},{5,7},{7,5},{8,10},{10,8},{9,1... | collective-permute-start | bytes 995336 | tf_op jit(solution)/shard_map/ppermute | solution.py:529
  25.1 6.4 %collective-permute-start.6 = (bf16[2,144,128]{2,1,0:T(8,128)(2,1)S(1)}, bf16[2,144,128]{2,1,0:T(8,128)(2,1)S(1)}, u32[]{:S(2)}, u32[]{:S(2)}) collective-permute-start(bf16[2,144,128]{2,1,0:T(8,128)(2,1)S(1)} %get-tuple-element.44.p0), channel_id=1, source_target_pairs={{0,4},{4,8},{8,12},{12,0},{1,5},{5,9},{9,13},{13,1},{2,6},{6,10},{... | collective-permute-start | bytes 221192 | tf_op jit(solution)/shard_map/ppermute | solution.py:529
  27.2 6.0 %collective-permute-start.7 = (bf16[2,144,128]{2,1,0:T(8,128)(2,1)S(1)}, bf16[2,144,128]{2,1,0:T(8,128)(2,1)S(1)}, u32[]{:S(2)}, u32[]{:S(2)}) collective-permute-start(bf16[2,144,128]{2,1,0:T(8,128)(2,1)S(1)} %get-tuple-element.44.p0), channel_id=1, source_target_pairs={{0,8},{4,12},{8,0},{12,4},{1,9},{5,13},{9,1},{13,5},{2,10},{6,14},... | collective-permute-start | bytes 221192 | tf_op jit(solution)/shard_map/ppermute | solution.py:529
  27.5 5.8 %collective-permute-start.8 = (bf16[2,144,128]{2,1,0:T(8,128)(2,1)S(1)}, bf16[2,144,128]{2,1,0:T(8,128)(2,1)S(1)}, u32[]{:S(2)}, u32[]{:S(2)}) collective-permute-start(bf16[2,144,128]{2,1,0:T(8,128)(2,1)S(1)} %get-tuple-element.44.p0), channel_id=1, source_target_pairs={{0,12},{4,0},{8,4},{12,8},{1,13},{5,1},{9,5},{13,9},{2,14},{6,2},{... | collective-permute-start | bytes 221192 | tf_op jit(solution)/shard_map/ppermute | solution.py:529
  30.4 2.9 %collective-permute-start.9 = (bf16[48,3456]{1,0:T(8,128)(2,1)S(1)}, bf16[48,3456]{1,0:T(8,128)(2,1)S(1)}, u32[]{:S(2)}, u32[]{:S(2)}) collective-permute-start(bf16[48,3456]{1,0:T(8,128)(2,1)S(1)} %shard_map.77.w1), channel_id=1, source_target_pairs={{0,1},{1,0},{2,3},{3,2},{4,5},{5,4},{6,7},{7,6},{8,9},{9,8},{10,11... | collective-permute-start | bytes 995336 | tf_op jit(solution)/shard_map/ppermute | solution.py:529
  33.3 1.6 %collective-permute-start.10 = (bf16[48,3456]{1,0:T(8,128)(2,1)S(1)}, bf16[48,3456]{1,0:T(8,128)(2,1)S(1)}, u32[]{:S(2)}, u32[]{:S(2)}) collective-permute-start(bf16[48,3456]{1,0:T(8,128)(2,1)S(1)} %collective-permute-done.5.w3), channel_id=1, source_target_pairs={{0,1},{1,0},{2,3},{3,2},{4,5},{5,4},{6,7},{7,6},{8,9},{9,8},{10,11... | collective-permute-start | bytes 995336 | tf_op jit(solution)/shard_map/ppermute | solution.py:529
  34.9 7.2 %copy-start.1 = (bf16[1,4,24,24,128]{4,3,2,1,0:T(8,128)(2,1)S(1)}, bf16[1,4,24,24,128]{4,3,2,1,0:T(8,128)(2,1)}, u32[]{:S(2)}) copy-start(bf16[1,4,24,24,128]{4,3,2,1,0:T(8,128)(2,1)} %param.5) | copy-start | bytes 1769476
  46.2 2.7 %collective-permute-start.11 = (f32[1728,128]{1,0:T(8,128)S(1)}, f32[1728,128]{1,0:T(8,128)S(1)}, u32[]{:S(2)}, u32[]{:S(2)}) collective-permute-start(f32[1728,128]{1,0:T(8,128)S(1)} %get-tuple-element.52), channel_id=1, source_target_pairs={{0,1},{1,0},{2,3},{3,2},{4,5},{5,4},{6,7},{7,6},{8,9},{9,8},{10,11... | collective-permute-start | bytes 2654216 | tf_op jit(solution)/shard_map/ppermute | solution.py:529
  48.5 1.9 %collective-permute-start.13 = (f32[872,128]{1,0:T(8,128)S(1)}, f32[872,128]{1,0:T(8,128)S(1)}, u32[]{:S(2)}, u32[]{:S(2)}) collective-permute-start(f32[872,128]{1,0:T(8,128)S(1)} %get-tuple-element.62), channel_id=1, source_target_pairs={{0,1},{1,0},{2,3},{3,2},{4,5},{5,4},{6,7},{7,6},{8,9},{9,8},{10,11... | collective-permute-start | bytes 1339400 | tf_op jit(solution)/shard_map/ppermute | solution.py:529
  49.0 7.5 %collective-permute-start.12 = (bf16[864,128]{1,0:T(8,128)(2,1)S(1)}, bf16[864,128]{1,0:T(8,128)(2,1)S(1)}, u32[]{:S(2)}, u32[]{:S(2)}) collective-permute-start(bf16[864,128]{1,0:T(8,128)(2,1)S(1)} %get-tuple-element.54), channel_id=1, source_target_pairs={{0,2},{2,0},{1,3},{3,1},{4,6},{6,4},{5,7},{7,5},{8,10},{10,8},{9,1... | collective-permute-start | bytes 663560 | tf_op jit(solution)/shard_map/ppermute | solution.py:529
  56.6 13.4 %collective-permute-start.18 = (f32[872,128]{1,0:T(8,128)S(1)}, f32[872,128]{1,0:T(8,128)S(1)}, u32[]{:S(2)}, u32[]{:S(2)}) collective-permute-start(f32[872,128]{1,0:T(8,128)S(1)} %add.66), channel_id=1, source_target_pairs={{0,2},{2,0},{1,3},{3,1},{4,6},{6,4},{5,7},{7,5},{8,10},{10,8},{9,1... | collective-permute-start | bytes 1339400 | tf_op jit(solution)/shard_map/ppermute | solution.py:529
  57.2 6.5 %collective-permute-start.14 = (bf16[216,128]{1,0:T(8,128)(2,1)S(1)}, bf16[216,128]{1,0:T(8,128)(2,1)S(1)}, u32[]{:S(2)}, u32[]{:S(2)}) collective-permute-start(bf16[216,128]{1,0:T(8,128)(2,1)S(1)} %get-tuple-element.63), channel_id=1, source_target_pairs={{0,4},{4,8},{8,12},{12,0},{1,5},{5,9},{9,13},{13,1},{2,6},{6,10},{... | collective-permute-start | bytes 165896 | tf_op jit(solution)/shard_map/ppermute | solution.py:529
  58.7 5.0 %collective-permute-start.15 = (bf16[216,128]{1,0:T(8,128)(2,1)S(1)}, bf16[216,128]{1,0:T(8,128)(2,1)S(1)}, u32[]{:S(2)}, u32[]{:S(2)}) collective-permute-start(bf16[216,128]{1,0:T(8,128)(2,1)S(1)} %get-tuple-element.64), channel_id=1, source_target_pairs={{0,12},{4,0},{8,4},{12,8},{1,13},{5,1},{9,5},{13,9},{2,14},{6,2},{... | collective-permute-start | bytes 165896 | tf_op jit(solution)/shard_map/ppermute | solution.py:529
  61.0 5.1 %collective-permute-start.16 = (bf16[216,128]{1,0:T(8,128)(2,1)S(1)}, bf16[216,128]{1,0:T(8,128)(2,1)S(1)}, u32[]{:S(2)}, u32[]{:S(2)}) collective-permute-start(bf16[216,128]{1,0:T(8,128)(2,1)S(1)} %get-tuple-element.65), channel_id=1, source_target_pairs={{0,8},{4,12},{8,0},{12,4},{1,9},{5,13},{9,1},{13,5},{2,10},{6,14},... | collective-permute-start | bytes 165896 | tf_op jit(solution)/shard_map/ppermute | solution.py:529
  66.2 6.0 %collective-permute-start.17 = (bf16[216,128]{1,0:T(8,128)(2,1)S(1)}, bf16[216,128]{1,0:T(8,128)(2,1)S(1)}, u32[]{:S(2)}, u32[]{:S(2)}) collective-permute-start(bf16[216,128]{1,0:T(8,128)(2,1)S(1)} %get-tuple-element.76), channel_id=1, source_target_pairs={{0,4},{4,8},{8,12},{12,0},{1,5},{5,9},{9,13},{13,1},{2,6},{6,10},{... | collective-permute-start | bytes 165896 | tf_op jit(solution)/shard_map/ppermute | solution.py:529
  66.3 5.9 %collective-permute-start.19 = (bf16[216,128]{1,0:T(8,128)(2,1)S(1)}, bf16[216,128]{1,0:T(8,128)(2,1)S(1)}, u32[]{:S(2)}, u32[]{:S(2)}) collective-permute-start(bf16[216,128]{1,0:T(8,128)(2,1)S(1)} %get-tuple-element.76), channel_id=1, source_target_pairs={{0,12},{4,0},{8,4},{12,8},{1,13},{5,1},{9,5},{13,9},{2,14},{6,2},{... | collective-permute-start | bytes 165896 | tf_op jit(solution)/shard_map/ppermute | solution.py:529
  70.0 5.1 %collective-permute-start.20 = (bf16[216,128]{1,0:T(8,128)(2,1)S(1)}, bf16[216,128]{1,0:T(8,128)(2,1)S(1)}, u32[]{:S(2)}, u32[]{:S(2)}) collective-permute-start(bf16[216,128]{1,0:T(8,128)(2,1)S(1)} %get-tuple-element.76), channel_id=1, source_target_pairs={{0,8},{4,12},{8,0},{12,4},{1,9},{5,13},{9,1},{13,5},{2,10},{6,14},... | collective-permute-start | bytes 165896 | tf_op jit(solution)/shard_map/ppermute | solution.py:529
  72.2 4.6 %collective-permute-start.23 = (f32[872,128]{1,0:T(8,128)S(1)}, f32[872,128]{1,0:T(8,128)S(1)}, u32[]{:S(2)}, u32[]{:S(2)}) collective-permute-start(f32[872,128]{1,0:T(8,128)S(1)} %add.72), channel_id=1, source_target_pairs={{0,1},{1,0},{2,3},{3,2},{4,5},{5,4},{6,7},{7,6},{8,9},{9,8},{10,11... | collective-permute-start | bytes 1339400 | tf_op jit(solution)/shard_map/ppermute | solution.py:529
  75.1 6.0 %collective-permute-start.21 = (bf16[864,128]{1,0:T(8,128)(2,1)S(1)}, bf16[864,128]{1,0:T(8,128)(2,1)S(1)}, u32[]{:S(2)}, u32[]{:S(2)}) collective-permute-start(bf16[864,128]{1,0:T(8,128)(2,1)S(1)} %bitcast.26), channel_id=1, source_target_pairs={{0,2},{2,0},{1,3},{3,1},{4,6},{6,4},{5,7},{7,5},{8,10},{10,8},{9,1... | collective-permute-start | bytes 663560 | tf_op jit(solution)/shard_map/ppermute | solution.py:529
  76.7 4.4 %collective-permute-start.22 = (bf16[864,128]{1,0:T(8,128)(2,1)S(1)}, bf16[864,128]{1,0:T(8,128)(2,1)S(1)}, u32[]{:S(2)}, u32[]{:S(2)}) collective-permute-start(bf16[864,128]{1,0:T(8,128)(2,1)S(1)} %bitcast.27), channel_id=1, source_target_pairs={{0,1},{1,0},{2,3},{3,2},{4,5},{5,4},{6,7},{7,6},{8,9},{9,8},{10,11... | collective-permute-start | bytes 663560 | tf_op jit(solution)/shard_map/ppermute | solution.py:529
  81.1 1.5 %collective-permute-start.24 = (bf16[864,128]{1,0:T(8,128)(2,1)S(1)}, bf16[864,128]{1,0:T(8,128)(2,1)S(1)}, u32[]{:S(2)}, u32[]{:S(2)}) collective-permute-start(bf16[864,128]{1,0:T(8,128)(2,1)S(1)} %collective-permute-done.21.across), channel_id=1, source_target_pairs={{0,1},{1,0},{2,3},{3,2},{4,5},{5,4},{6,7},{7,6},{8,9},{9,8},{10,11... | collective-permute-start | bytes 663560 | tf_op jit(solution)/shard_map/ppermute | solution.py:529

commit v4 on v3

--- a/solution.py
+++ b/solution.py
@@ -59,7 +59,7 @@
         ).astype(bf16)
 
 
-def first_forward(vol, before, after, kernel, pooled, slope, u, rows_ref, pairs, acc, half, dense):
+def first_forward(vol, before, after, kernel, pooled, slope, u, rows_ref, pairs, accs, halves, dense):
     depth, rows, cols, chans = vol.shape
     wide = 32
     cells = rows * wide
@@ -89,7 +89,9 @@
     first_taps = jnp.concatenate([tap(0, b) for b in range(3)], axis=0)
     last_taps = jnp.concatenate([tap(2, b) for b in range(3)], axis=0)
 
-    def one_pair(t, carry):
+    def one_pair(t):
+        acc, half = accs.at[t], halves.at[t]
+
         def window(q, b):
             return u[2 * t + q, b * wide : b * wide + cells, :]
 
@@ -111,9 +113,9 @@
             even = half[pl.ds(h * wide, cols // 2, stride=2), :]
             odd = half[pl.ds(h * wide + 1, cols // 2, stride=2), :]
             dense[t, h * (cols // 2) : (h + 1) * (cols // 2), :] = (even + odd) * 0.125
-        return carry
-
-    lax.fori_loop(0, depth // 2, one_pair, 0)
+
+    for t in range(depth // 2):
+        one_pair(t)
     pooled[...] = dense[...].astype(bf16)
 
 
@@ -131,8 +133,8 @@
             pltpu.VMEM((depth + 2, cells + 2 * wide, 3 * chans), bf16),
             pltpu.VMEM((cells + 2 * front, chans), f32),
             pltpu.VMEM((3, 6 * chans, 2 * outs), bf16),
-            pltpu.VMEM((cells, 2 * outs), f32),
-            pltpu.VMEM((cells // 2, outs), f32),
+            pltpu.VMEM((depth // 2, cells, 2 * outs), f32),
+            pltpu.VMEM((depth // 2, cells // 2, outs), f32),
             pltpu.VMEM((depth // 2, rows * cols // 4, outs), f32),
         ],
         vol, before, after, kernel, work=heavy * 8,

time: 84.3 us -> 83.9 us (level)
  Pallas kernels: 21.5 us -> 20.6 us
    pallas_call x9, Pallas kernels: 21.5 us -> 20.6 us  [call(): pl.pallas_call(body, out_shape=outs, in_specs=specs, out_specs=out_specs,...]
  transfers between devices with their start and end apart: 25 -> 25, of which waited for: 11 -> 11; matrix products, arithmetic and copies ran while one was open for 2% -> 2% of each run, Pallas kernels for 11% -> 10%
where the time goes in v4:
time: 83.9 us; the launch traced here: 83.6 us
  starting transfers between devices  30.7 us (37%)
  waiting for transfers between devices  26.6 us (32%)
  Pallas kernels  20.6 us (25%)
  local copies, waits for them, and re-layouts  4.37 us (5%)
  between operations  1.07 us (1%)
    ppermute x23, waiting for transfers between devices, turn(): return lax.ppermute(x, axis, [(i, (i + step) % size) for i in range(size)])  26.6 us
    ppermute x23, starting transfers between devices, turn(): return lax.ppermute(x, axis, [(i, (i + step) % size) for i in range(size)])  24.5 us
    pallas_call x9, Pallas kernels, call(): pl.pallas_call(body, out_shape=outs, in_specs=specs, out_specs=out_specs,...  20.6 us
    ppermute x1, starting transfers between devices, neighbours(): before = lax.ppermute(last, 'space', up)  4.94 us
    unnamed x12, local copies, waits for them, and re-layouts  2.25 us
  transfers between devices with their start and end apart: 25, of which 11 were waited for; matrix products, arithmetic and copies ran while one was open for 2% of the time, Pallas kernels for 10%

profile of v4, /device:TPU:0, one launch (start us, length us, event | category | flops | bytes accessed | tf_op | source)
XLA Modules:
  0.0 83.6 jit_solution(13373285167862255610)
XLA Ops:
  0.6 1.0 %slice_bitcast_fusion = (bf16[1,24,24,128]{3,2,1,0:T(8,128)(2,1)S(1)}, bf16[1,24,24,128]{3,2,1,0:T(8,128)(2,1)S(1)}) fusion(bf16[1,4,24,24,128]{4,3,2,1,0:T(8,128)(2,1)} %param.5), kind=kLoop, calls=%fused_computation.2 | loop fusion | bytes 589824 | tf_op jit(solution)/shard_map/slice | solution.py:723
  1.6 4.9 %collective-permute-start = (bf16[1,24,24,128]{3,2,1,0:T(8,128)(2,1)S(1)}, bf16[1,24,24,128]{3,2,1,0:T(8,128)(2,1)S(1)}, u32[]{:S(2)}, u32[]{:S(2)}) collective-permute-start(bf16[1,24,24,128]{3,2,1,0:T(8,128)(2,1)S(1)} %get-tuple-element.78), channel_id=1, source_target_pairs={{0,4},{4,8},{8,12},{1,5},{5,9},{9,13},{2,6},{6,10},{10,14},{3,7},{... | collective-permute-start | bytes 442376 | tf_op jit(solution)/shard_map/ppermute | solution.py:709
  6.6 1.3 %collective-permute-start.1 = (bf16[1,24,24,128]{3,2,1,0:T(8,128)(2,1)S(1)}, bf16[1,24,24,128]{3,2,1,0:T(8,128)(2,1)S(1)}, u32[]{:S(2)}, u32[]{:S(2)}) collective-permute-start(bf16[1,24,24,128]{3,2,1,0:T(8,128)(2,1)S(1)} %get-tuple-element.77), channel_id=1, source_target_pairs={{4,0},{8,4},{12,8},{5,1},{9,5},{13,9},{6,2},{10,6},{14,10},{7,3},{... | collective-permute-start | bytes 442376 | tf_op jit(solution)/shard_map/ppermute | solution.py:710
  7.9 0.9 %dynamic-slice_bitcast_fusion = bf16[16,3456]{1,0:T(8,128)(2,1)S(1)} fusion(bf16[3456,64]{0,1:T(8,128)(2,1)} %param.8, s32[]{:T(128)S(6)} %select_n.50), kind=kLoop, calls=%fused_computation.5 | loop fusion | bytes 221188 | tf_op jit(solution)/shard_map/dynamic_slice | solution.py:725
  8.8 2.6 %collective-permute-start.2 = (bf16[16,3456]{1,0:T(8,128)(2,1)S(1)}, bf16[16,3456]{1,0:T(8,128)(2,1)S(1)}, u32[]{:S(2)}, u32[]{:S(2)}) collective-permute-start(bf16[16,3456]{1,0:T(8,128)(2,1)S(1)} %dynamic-slice_bitcast_fusion), channel_id=1, source_target_pairs={{0,4},{4,8},{8,12},{12,0},{1,5},{5,9},{9,13},{13,1},{2,6},{6,10},{... | collective-permute-start | bytes 331784 | tf_op jit(solution)/shard_map/ppermute | solution.py:531
  11.5 2.6 %collective-permute-start.3 = (bf16[16,3456]{1,0:T(8,128)(2,1)S(1)}, bf16[16,3456]{1,0:T(8,128)(2,1)S(1)}, u32[]{:S(2)}, u32[]{:S(2)}) collective-permute-start(bf16[16,3456]{1,0:T(8,128)(2,1)S(1)} %dynamic-slice_bitcast_fusion), channel_id=1, source_target_pairs={{0,8},{4,12},{8,0},{12,4},{1,9},{5,13},{9,1},{13,5},{2,10},{6,14},... | collective-permute-start | bytes 331784 | tf_op jit(solution)/shard_map/ppermute | solution.py:531
  14.0 1.3 %collective-permute-start.4 = (bf16[16,3456]{1,0:T(8,128)(2,1)S(1)}, bf16[16,3456]{1,0:T(8,128)(2,1)S(1)}, u32[]{:S(2)}, u32[]{:S(2)}) collective-permute-start(bf16[16,3456]{1,0:T(8,128)(2,1)S(1)} %dynamic-slice_bitcast_fusion), channel_id=1, source_target_pairs={{0,12},{4,0},{8,4},{12,8},{1,13},{5,1},{9,5},{13,9},{2,14},{6,2},{... | collective-permute-start | bytes 331784 | tf_op jit(solution)/shard_map/ppermute | solution.py:531
  15.4 0.0 collective-permute-done.before
  15.4 0.0 collective-permute-done.1.after
  15.4 1.1 %copy-done = bf16[1,4,24,24,128]{4,3,2,1,0:T(8,128)(2,1)S(1)} copy-done((bf16[1,4,24,24,128]{4,3,2,1,0:T(8,128)(2,1)S(1)}, bf16[1,4,24,24,128]{4,3,2,1,0:T(8,128)(2,1)}, u32[]{:S(2)}) %copy-start) | copy-done | bytes 589848
  16.5 1.2 %copy-done.3 = bf16[3456,128]{1,0:T(8,128)(2,1)S(1)} copy-done((bf16[3456,128]{1,0:T(8,128)(2,1)S(1)}, bf16[3456,128]{1,0:T(8,128)(2,1)}, u32[]{:S(2)}) %copy-start.3) | copy-done | bytes 884760
  17.6 5.1 %shard_map.76 = (bf16[2,144,128]{2,1,0:T(8,128)(2,1)S(1)}, f32[4,768,128]{2,1,0:T(8,128)S(1)}) custom-call(bf16[4,24,24,128]{3,2,1,0:T(8,128)(2,1)S(1)} %bitcast.29, bf16[1,24,24,128]{3,2,1,0:T(8,128)(2,1)S(1)} %collective-permute-done.before, bf16[1,24,24,128]{3,2,1,0:T(8,128)(2,1)S(1)} %collective-permute-done.1.after, bf16[3456,128]{1,0:T(8,128)(2,1)S(1)} %copy-done.3), custom_call_target="tpu_custom_call" | custom-call | flops 8000000000 | tf_op jit(solution)/shard_map/pallas_call | solution.py:24
  22.8 0.0 collective-permute-done.3.r1
  22.8 1.6 %collective-permute-start.5 = (bf16[48,3456]{1,0:T(8,128)(2,1)S(1)}, bf16[48,3456]{1,0:T(8,128)(2,1)S(1)}, u32[]{:S(2)}, u32[]{:S(2)}) collective-permute-start(bf16[48,3456]{1,0:T(8,128)(2,1)S(1)} %shard_map.77.w1), channel_id=1, source_target_pairs={{0,2},{2,0},{1,3},{3,1},{4,6},{6,4},{5,7},{7,5},{8,10},{10,8},{9,1... | collective-permute-start | bytes 995336 | tf_op jit(solution)/shard_map/ppermute | solution.py:531
  24.4 2.2 %collective-permute-start.6 = (bf16[2,144,128]{2,1,0:T(8,128)(2,1)S(1)}, bf16[2,144,128]{2,1,0:T(8,128)(2,1)S(1)}, u32[]{:S(2)}, u32[]{:S(2)}) collective-permute-start(bf16[2,144,128]{2,1,0:T(8,128)(2,1)S(1)} %get-tuple-element.44.p0), channel_id=1, source_target_pairs={{0,4},{4,8},{8,12},{12,0},{1,5},{5,9},{9,13},{13,1},{2,6},{6,10},{... | collective-permute-start | bytes 221192 | tf_op jit(solution)/shard_map/ppermute | solution.py:531
  26.5 0.3 collective-permute-start.7
  26.9 2.9 %collective-permute-start.8 = (bf16[2,144,128]{2,1,0:T(8,128)(2,1)S(1)}, bf16[2,144,128]{2,1,0:T(8,128)(2,1)S(1)}, u32[]{:S(2)}, u32[]{:S(2)}) collective-permute-start(bf16[2,144,128]{2,1,0:T(8,128)(2,1)S(1)} %get-tuple-element.44.p0), channel_id=1, source_target_pairs={{0,12},{4,0},{8,4},{12,8},{1,13},{5,1},{9,5},{13,9},{2,14},{6,2},{... | collective-permute-start | bytes 221192 | tf_op jit(solution)/shard_map/ppermute | solution.py:531
  29.7 0.0 collective-permute-start.9
  29.7 1.6 %collective-permute-done.6.p1 = bf16[2,144,128]{2,1,0:T(8,128)(2,1)S(1)} collective-permute-done((bf16[2,144,128]{2,1,0:T(8,128)(2,1)S(1)}, bf16[2,144,128]{2,1,0:T(8,128)(2,1)S(1)}, u32[]{:S(2)}, u32[]{:S(2)}) %collective-permute-start.6) | collective-permute-done | bytes 73760 | tf_op jit(solution)/shard_map/ppermute | solution.py:531
  31.3 1.7 %collective-permute-done.7.p2 = bf16[2,144,128]{2,1,0:T(8,128)(2,1)S(1)} collective-permute-done((bf16[2,144,128]{2,1,0:T(8,128)(2,1)S(1)}, bf16[2,144,128]{2,1,0:T(8,128)(2,1)S(1)}, u32[]{:S(2)}, u32[]{:S(2)}) %collective-permute-start.7) | collective-permute-done | bytes 73760 | tf_op jit(solution)/shard_map/ppermute | solution.py:531
  33.1 1.6 %collective-permute-done.10.w4 = bf16[48,3456]{1,0:T(8,128)(2,1)S(1)} collective-permute-done((bf16[48,3456]{1,0:T(8,128)(2,1)S(1)}, bf16[48,3456]{1,0:T(8,128)(2,1)S(1)}, u32[]{:S(2)}, u32[]{:S(2)}) %collective-permute-start.10) | collective-permute-done | bytes 331808 | tf_op jit(solution)/shard_map/ppermute | solution.py:531
  34.7 0.0 copy-start.1
  34.7 7.2 %shard_map.78 = (f32[2,192,128]{2,1,0:T(8,128)S(1)}, bf16[8,192,64]{2,1,0:T(8,128)(2,1)S(1)}, f32[4,256]{1,0:T(4,128)S(1)}) custom-call(bf16[2,144,128]{2,1,0:T(8,128)(2,1)S(1)} %get-tuple-element.44.p0, bf16[2,144,128]{2,1,0:T(8,128)(2,1)S(1)} %collective-permute-done.6.p1, bf16[2,144,128]{2,1,0:T(8,128)(2,1)S(1)} %collective-permute-done.7.p2, ...), custom_call_target="tpu_custom_call" | custom-call | flops 8000000000 | tf_op jit(solution)/shard_map/pallas_call | solution.py:24
  41.9 3.9 %shard_map.79 = (f32[1728,128]{1,0:T(8,128)S(1)}, f32[1728,128]{1,0:T(8,128)S(1)}) custom-call(bf16[4,24,24,128]{3,2,1,0:T(8,128)(2,1)S(1)} %bitcast.30, bf16[1,24,24,128]{3,2,1,0:T(8,128)(2,1)S(1)} %collective-permute-done.before, bf16[1,24,24,128]{3,2,1,0:T(8,128)(2,1)S(1)} %collective-permute-done.1.after, f32[2,192,128]{2,1,0:T(8,128)S(1)} %get-tuple-element.49.spread, ...), custom_call_target="tpu_custom_call" | custom-call | flops 7000000000 | tf_op jit(solution)/shard_map/pallas_call | solution.py:24
  45.8 0.2 collective-permute-start.11
  46.0 2.1 %shard_map.82 = (f32[872,128]{1,0:T(8,128)S(1)}, f32[872,128]{1,0:T(8,128)S(1)}) custom-call(bf16[2,144,128]{2,1,0:T(8,128)(2,1)S(1)} %get-tuple-element.44.p0, bf16[2,144,128]{2,1,0:T(8,128)(2,1)S(1)} %collective-permute-done.6.p1, bf16[2,144,128]{2,1,0:T(8,128)(2,1)S(1)} %collective-permute-done.7.p2, bf16[2,144,128]{2,1,0:T(8,128)(2,1)S(1)} %collective-permute-done.8.p3, ...), custom_call_target="tpu_custom_call" | custom-call | flops 4000000000 | tf_op jit(solution)/shard_map/pallas_call | solution.py:24
  48.1 0.4 collective-permute-start.13
  48.5 0.1 shard_map.80
  48.6 0.6 collective-permute-start.12
  49.2 0.7 collective-permute-done.13
  50.0 6.1 %collective-permute-done.12.came = bf16[864,128]{1,0:T(8,128)(2,1)S(1)} collective-permute-done((bf16[864,128]{1,0:T(8,128)(2,1)S(1)}, bf16[864,128]{1,0:T(8,128)(2,1)S(1)}, u32[]{:S(2)}, u32[]{:S(2)}) %collective-permute-start.12) | collective-permute-done | bytes 221216 | tf_op jit(solution)/shard_map/ppermute | solution.py:531
  56.2 0.6 collective-permute-start.18
  56.8 1.8 %collective-permute-start.14 = (bf16[216,128]{1,0:T(8,128)(2,1)S(1)}, bf16[216,128]{1,0:T(8,128)(2,1)S(1)}, u32[]{:S(2)}, u32[]{:S(2)}) collective-permute-start(bf16[216,128]{1,0:T(8,128)(2,1)S(1)} %get-tuple-element.63), channel_id=1, source_target_pairs={{0,4},{4,8},{8,12},{12,0},{1,5},{5,9},{9,13},{13,1},{2,6},{6,10},{... | collective-permute-start | bytes 165896 | tf_op jit(solution)/shard_map/ppermute | solution.py:531
  58.6 2.0 %collective-permute-start.15 = (bf16[216,128]{1,0:T(8,128)(2,1)S(1)}, bf16[216,128]{1,0:T(8,128)(2,1)S(1)}, u32[]{:S(2)}, u32[]{:S(2)}) collective-permute-start(bf16[216,128]{1,0:T(8,128)(2,1)S(1)} %get-tuple-element.64), channel_id=1, source_target_pairs={{0,12},{4,0},{8,4},{12,8},{1,13},{5,1},{9,5},{13,9},{2,14},{6,2},{... | collective-permute-start | bytes 165896 | tf_op jit(solution)/shard_map/ppermute | solution.py:531
  60.6 2.7 %collective-permute-done.14 = bf16[216,128]{1,0:T(8,128)(2,1)S(1)} collective-permute-done((bf16[216,128]{1,0:T(8,128)(2,1)S(1)}, bf16[216,128]{1,0:T(8,128)(2,1)S(1)}, u32[]{:S(2)}, u32[]{:S(2)}) %collective-permute-start.14) | collective-permute-done | bytes 55328 | tf_op jit(solution)/shard_map/ppermute | solution.py:531
  63.3 2.4 %collective-permute-done.16 = bf16[216,128]{1,0:T(8,128)(2,1)S(1)} collective-permute-done((bf16[216,128]{1,0:T(8,128)(2,1)S(1)}, bf16[216,128]{1,0:T(8,128)(2,1)S(1)}, u32[]{:S(2)}, u32[]{:S(2)}) %collective-permute-start.16) | collective-permute-done | bytes 55328 | tf_op jit(solution)/shard_map/ppermute | solution.py:531
  65.7 0.1 bitcast_dynamic-update-slice_fusion.5
  65.8 0.1 collective-permute-start.17
  65.9 3.7 %collective-permute-start.19 = (bf16[216,128]{1,0:T(8,128)(2,1)S(1)}, bf16[216,128]{1,0:T(8,128)(2,1)S(1)}, u32[]{:S(2)}, u32[]{:S(2)}) collective-permute-start(bf16[216,128]{1,0:T(8,128)(2,1)S(1)} %get-tuple-element.76), channel_id=1, source_target_pairs={{0,12},{4,0},{8,4},{12,8},{1,13},{5,1},{9,5},{13,9},{2,14},{6,2},{... | collective-permute-start | bytes 165896 | tf_op jit(solution)/shard_map/ppermute | solution.py:531
  69.7 0.1 add.72
  69.7 2.2 %collective-permute-done.17 = bf16[216,128]{1,0:T(8,128)(2,1)S(1)} collective-permute-done((bf16[216,128]{1,0:T(8,128)(2,1)S(1)}, bf16[216,128]{1,0:T(8,128)(2,1)S(1)}, u32[]{:S(2)}, u32[]{:S(2)}) %collective-permute-start.17) | collective-permute-done | bytes 55328 | tf_op jit(solution)/shard_map/ppermute | solution.py:531
  71.9 2.8 %collective-permute-done.20 = bf16[216,128]{1,0:T(8,128)(2,1)S(1)} collective-permute-done((bf16[216,128]{1,0:T(8,128)(2,1)S(1)}, bf16[216,128]{1,0:T(8,128)(2,1)S(1)}, u32[]{:S(2)}, u32[]{:S(2)}) %collective-permute-start.20) | collective-permute-done | bytes 55328 | tf_op jit(solution)/shard_map/ppermute | solution.py:531
  74.7 1.6 %collective-permute-start.21 = (bf16[864,128]{1,0:T(8,128)(2,1)S(1)}, bf16[864,128]{1,0:T(8,128)(2,1)S(1)}, u32[]{:S(2)}, u32[]{:S(2)}) collective-permute-start(bf16[864,128]{1,0:T(8,128)(2,1)S(1)} %bitcast.26), channel_id=1, source_target_pairs={{0,2},{2,0},{1,3},{3,1},{4,6},{6,4},{5,7},{7,5},{8,10},{10,8},{9,1... | collective-permute-start | bytes 663560 | tf_op jit(solution)/shard_map/ppermute | solution.py:531
  76.3 0.1 broadcast_in_dim.31
  76.4 1.0 %shard_map.83 = (f32[64,3456]{1,0:T(8,128)}, f32[4,64]{1,0:T(4,128)}) custom-call(f32[1744,128]{1,0:T(8,128)S(1)} %bitcast.25), custom_call_target="tpu_custom_call" | custom-call | flops 2000000000 | tf_op jit(solution)/shard_map/pallas_call | solution.py:24
  77.4 3.3 %collective-permute-done.21.across = bf16[864,128]{1,0:T(8,128)(2,1)S(1)} collective-permute-done((bf16[864,128]{1,0:T(8,128)(2,1)S(1)}, bf16[864,128]{1,0:T(8,128)(2,1)S(1)}, u32[]{:S(2)}, u32[]{:S(2)}) %collective-permute-start.21) | collective-permute-done | bytes 221216 | tf_op jit(solution)/shard_map/ppermute | solution.py:531
  80.7 1.5 %collective-permute-done.24.far = bf16[864,128]{1,0:T(8,128)(2,1)S(1)} collective-permute-done((bf16[864,128]{1,0:T(8,128)(2,1)S(1)}, bf16[864,128]{1,0:T(8,128)(2,1)S(1)}, u32[]{:S(2)}, u32[]{:S(2)}) %collective-permute-start.24) | collective-permute-done | bytes 221216 | tf_op jit(solution)/shard_map/ppermute | solution.py:531
  82.2 1.3 %shard_map.84 = f32[3456,128]{1,0:T(8,128)} custom-call(bf16[864,128]{1,0:T(8,128)(2,1)S(1)} %bitcast.28, bf16[864,128]{1,0:T(8,128)(2,1)S(1)} %collective-permute-done.21.across, bf16[864,128]{1,0:T(8,128)(2,1)S(1)} %collective-permute-done.22.near, bf16[864,128]{1,0:T(8,128)(2,1)S(1)} %collective-permute-done.24.far), custom_call_target="tpu_custom_call" | custom-call | tf_op jit(solution)/shard_map/pallas_call | solution.py:24
  (35 shorter events, 0.3 us)
Async XLA Ops:
  1.6 13.7 %collective-permute-start = (bf16[1,24,24,128]{3,2,1,0:T(8,128)(2,1)S(1)}, bf16[1,24,24,128]{3,2,1,0:T(8,128)(2,1)S(1)}, u32[]{:S(2)}, u32[]{:S(2)}) collective-permute-start(bf16[1,24,24,128]{3,2,1,0:T(8,128)(2,1)S(1)} %get-tuple-element.78), channel_id=1, source_target_pairs={{0,4},{4,8},{8,12},{1,5},{5,9},{9,13},{2,6},{6,10},{10,14},{3,7},{... | collective-permute-start | bytes 442376 | tf_op jit(solution)/shard_map/ppermute | solution.py:709
  6.6 8.8 %collective-permute-start.1 = (bf16[1,24,24,128]{3,2,1,0:T(8,128)(2,1)S(1)}, bf16[1,24,24,128]{3,2,1,0:T(8,128)(2,1)S(1)}, u32[]{:S(2)}, u32[]{:S(2)}) collective-permute-start(bf16[1,24,24,128]{3,2,1,0:T(8,128)(2,1)S(1)} %get-tuple-element.77), channel_id=1, source_target_pairs={{4,0},{8,4},{12,8},{5,1},{9,5},{13,9},{6,2},{10,6},{14,10},{7,3},{... | collective-permute-start | bytes 442376 | tf_op jit(solution)/shard_map/ppermute | solution.py:710
  8.8 13.9 %collective-permute-start.2 = (bf16[16,3456]{1,0:T(8,128)(2,1)S(1)}, bf16[16,3456]{1,0:T(8,128)(2,1)S(1)}, u32[]{:S(2)}, u32[]{:S(2)}) collective-permute-start(bf16[16,3456]{1,0:T(8,128)(2,1)S(1)} %dynamic-slice_bitcast_fusion), channel_id=1, source_target_pairs={{0,4},{4,8},{8,12},{12,0},{1,5},{5,9},{9,13},{13,1},{2,6},{6,10},{... | collective-permute-start | bytes 331784 | tf_op jit(solution)/shard_map/ppermute | solution.py:531
  11.5 11.3 %collective-permute-start.3 = (bf16[16,3456]{1,0:T(8,128)(2,1)S(1)}, bf16[16,3456]{1,0:T(8,128)(2,1)S(1)}, u32[]{:S(2)}, u32[]{:S(2)}) collective-permute-start(bf16[16,3456]{1,0:T(8,128)(2,1)S(1)} %dynamic-slice_bitcast_fusion), channel_id=1, source_target_pairs={{0,8},{4,12},{8,0},{12,4},{1,9},{5,13},{9,1},{13,5},{2,10},{6,14},... | collective-permute-start | bytes 331784 | tf_op jit(solution)/shard_map/ppermute | solution.py:531
  14.0 8.8 %collective-permute-start.4 = (bf16[16,3456]{1,0:T(8,128)(2,1)S(1)}, bf16[16,3456]{1,0:T(8,128)(2,1)S(1)}, u32[]{:S(2)}, u32[]{:S(2)}) collective-permute-start(bf16[16,3456]{1,0:T(8,128)(2,1)S(1)} %dynamic-slice_bitcast_fusion), channel_id=1, source_target_pairs={{0,12},{4,0},{8,4},{12,8},{1,13},{5,1},{9,5},{13,9},{2,14},{6,2},{... | collective-permute-start | bytes 331784 | tf_op jit(solution)/shard_map/ppermute | solution.py:531
  15.4 1.1 %copy-start = (bf16[1,4,24,24,128]{4,3,2,1,0:T(8,128)(2,1)S(1)}, bf16[1,4,24,24,128]{4,3,2,1,0:T(8,128)(2,1)}, u32[]{:S(2)}) copy-start(bf16[1,4,24,24,128]{4,3,2,1,0:T(8,128)(2,1)} %param.5) | copy-start | bytes 1769476
  16.5 1.2 %copy-start.3 = (bf16[3456,128]{1,0:T(8,128)(2,1)S(1)}, bf16[3456,128]{1,0:T(8,128)(2,1)}, u32[]{:S(2)}) copy-start(bf16[3456,128]{1,0:T(8,128)(2,1)} %kernel.1) | copy-start | bytes 2654212
  17.6 17.1 %copy-start.2 = (bf16[3456,64]{0,1:T(8,128)(2,1)S(1)}, bf16[3456,64]{0,1:T(8,128)(2,1)}, u32[]{:S(2)}) copy-start(bf16[3456,64]{0,1:T(8,128)(2,1)} %param.8) | copy-start | bytes 1327108
  17.6 17.1 %copy-start.4 = (f32[256,4]{0,1:T(4,128)S(1)}, f32[256,4]{0,1:T(4,128)}, u32[]{:S(2)}) copy-start(f32[256,4]{0,1:T(4,128)} %param.9) | copy-start | bytes 12292
  17.6 17.1 %copy-start.5 = (f32[1,4]{1,0:T(1,128)S(1)}, f32[1,4]{1,0:T(1,128)}, u32[]{:S(2)}) copy-start(f32[1,4]{1,0:T(1,128)} %wanted.1) | copy-start | bytes 52
  22.8 10.2 %collective-permute-start.5 = (bf16[48,3456]{1,0:T(8,128)(2,1)S(1)}, bf16[48,3456]{1,0:T(8,128)(2,1)S(1)}, u32[]{:S(2)}, u32[]{:S(2)}) collective-permute-start(bf16[48,3456]{1,0:T(8,128)(2,1)S(1)} %shard_map.77.w1), channel_id=1, source_target_pairs={{0,2},{2,0},{1,3},{3,1},{4,6},{6,4},{5,7},{7,5},{8,10},{10,8},{9,1... | collective-permute-start | bytes 995336 | tf_op jit(solution)/shard_map/ppermute | solution.py:531
  24.4 7.0 %collective-permute-start.6 = (bf16[2,144,128]{2,1,0:T(8,128)(2,1)S(1)}, bf16[2,144,128]{2,1,0:T(8,128)(2,1)S(1)}, u32[]{:S(2)}, u32[]{:S(2)}) collective-permute-start(bf16[2,144,128]{2,1,0:T(8,128)(2,1)S(1)} %get-tuple-element.44.p0), channel_id=1, source_target_pairs={{0,4},{4,8},{8,12},{12,0},{1,5},{5,9},{9,13},{13,1},{2,6},{6,10},{... | collective-permute-start | bytes 221192 | tf_op jit(solution)/shard_map/ppermute | solution.py:531
  26.5 6.5 %collective-permute-start.7 = (bf16[2,144,128]{2,1,0:T(8,128)(2,1)S(1)}, bf16[2,144,128]{2,1,0:T(8,128)(2,1)S(1)}, u32[]{:S(2)}, u32[]{:S(2)}) collective-permute-start(bf16[2,144,128]{2,1,0:T(8,128)(2,1)S(1)} %get-tuple-element.44.p0), channel_id=1, source_target_pairs={{0,8},{4,12},{8,0},{12,4},{1,9},{5,13},{9,1},{13,5},{2,10},{6,14},... | collective-permute-start | bytes 221192 | tf_op jit(solution)/shard_map/ppermute | solution.py:531
  26.9 6.2 %collective-permute-start.8 = (bf16[2,144,128]{2,1,0:T(8,128)(2,1)S(1)}, bf16[2,144,128]{2,1,0:T(8,128)(2,1)S(1)}, u32[]{:S(2)}, u32[]{:S(2)}) collective-permute-start(bf16[2,144,128]{2,1,0:T(8,128)(2,1)S(1)} %get-tuple-element.44.p0), channel_id=1, source_target_pairs={{0,12},{4,0},{8,4},{12,8},{1,13},{5,1},{9,5},{13,9},{2,14},{6,2},{... | collective-permute-start | bytes 221192 | tf_op jit(solution)/shard_map/ppermute | solution.py:531
  29.7 3.3 %collective-permute-start.9 = (bf16[48,3456]{1,0:T(8,128)(2,1)S(1)}, bf16[48,3456]{1,0:T(8,128)(2,1)S(1)}, u32[]{:S(2)}, u32[]{:S(2)}) collective-permute-start(bf16[48,3456]{1,0:T(8,128)(2,1)S(1)} %shard_map.77.w1), channel_id=1, source_target_pairs={{0,1},{1,0},{2,3},{3,2},{4,5},{5,4},{6,7},{7,6},{8,9},{9,8},{10,11... | collective-permute-start | bytes 995336 | tf_op jit(solution)/shard_map/ppermute | solution.py:531
  33.1 1.6 %collective-permute-start.10 = (bf16[48,3456]{1,0:T(8,128)(2,1)S(1)}, bf16[48,3456]{1,0:T(8,128)(2,1)S(1)}, u32[]{:S(2)}, u32[]{:S(2)}) collective-permute-start(bf16[48,3456]{1,0:T(8,128)(2,1)S(1)} %collective-permute-done.5.w3), channel_id=1, source_target_pairs={{0,1},{1,0},{2,3},{3,2},{4,5},{5,4},{6,7},{7,6},{8,9},{9,8},{10,11... | collective-permute-start | bytes 995336 | tf_op jit(solution)/shard_map/ppermute | solution.py:531
  34.7 7.2 %copy-start.1 = (bf16[1,4,24,24,128]{4,3,2,1,0:T(8,128)(2,1)S(1)}, bf16[1,4,24,24,128]{4,3,2,1,0:T(8,128)(2,1)}, u32[]{:S(2)}) copy-start(bf16[1,4,24,24,128]{4,3,2,1,0:T(8,128)(2,1)} %param.5) | copy-start | bytes 1769476
  45.8 2.7 %collective-permute-start.11 = (f32[1728,128]{1,0:T(8,128)S(1)}, f32[1728,128]{1,0:T(8,128)S(1)}, u32[]{:S(2)}, u32[]{:S(2)}) collective-permute-start(f32[1728,128]{1,0:T(8,128)S(1)} %get-tuple-element.52), channel_id=1, source_target_pairs={{0,1},{1,0},{2,3},{3,2},{4,5},{5,4},{6,7},{7,6},{8,9},{9,8},{10,11... | collective-permute-start | bytes 2654216 | tf_op jit(solution)/shard_map/ppermute | solution.py:531
  48.1 1.9 %collective-permute-start.13 = (f32[872,128]{1,0:T(8,128)S(1)}, f32[872,128]{1,0:T(8,128)S(1)}, u32[]{:S(2)}, u32[]{:S(2)}) collective-permute-start(f32[872,128]{1,0:T(8,128)S(1)} %get-tuple-element.62), channel_id=1, source_target_pairs={{0,1},{1,0},{2,3},{3,2},{4,5},{5,4},{6,7},{7,6},{8,9},{9,8},{10,11... | collective-permute-start | bytes 1339400 | tf_op jit(solution)/shard_map/ppermute | solution.py:531
  48.6 7.5 %collective-permute-start.12 = (bf16[864,128]{1,0:T(8,128)(2,1)S(1)}, bf16[864,128]{1,0:T(8,128)(2,1)S(1)}, u32[]{:S(2)}, u32[]{:S(2)}) collective-permute-start(bf16[864,128]{1,0:T(8,128)(2,1)S(1)} %get-tuple-element.54), channel_id=1, source_target_pairs={{0,2},{2,0},{1,3},{3,1},{4,6},{6,4},{5,7},{7,5},{8,10},{10,8},{9,1... | collective-permute-start | bytes 663560 | tf_op jit(solution)/shard_map/ppermute | solution.py:531
  56.2 13.5 %collective-permute-start.18 = (f32[872,128]{1,0:T(8,128)S(1)}, f32[872,128]{1,0:T(8,128)S(1)}, u32[]{:S(2)}, u32[]{:S(2)}) collective-permute-start(f32[872,128]{1,0:T(8,128)S(1)} %add.66), channel_id=1, source_target_pairs={{0,2},{2,0},{1,3},{3,1},{4,6},{6,4},{5,7},{7,5},{8,10},{10,8},{9,1... | collective-permute-start | bytes 1339400 | tf_op jit(solution)/shard_map/ppermute | solution.py:531
  56.8 6.5 %collective-permute-start.14 = (bf16[216,128]{1,0:T(8,128)(2,1)S(1)}, bf16[216,128]{1,0:T(8,128)(2,1)S(1)}, u32[]{:S(2)}, u32[]{:S(2)}) collective-permute-start(bf16[216,128]{1,0:T(8,128)(2,1)S(1)} %get-tuple-element.63), channel_id=1, source_target_pairs={{0,4},{4,8},{8,12},{12,0},{1,5},{5,9},{9,13},{13,1},{2,6},{6,10},{... | collective-permute-start | bytes 165896 | tf_op jit(solution)/shard_map/ppermute | solution.py:531
  58.6 4.8 %collective-permute-start.15 = (bf16[216,128]{1,0:T(8,128)(2,1)S(1)}, bf16[216,128]{1,0:T(8,128)(2,1)S(1)}, u32[]{:S(2)}, u32[]{:S(2)}) collective-permute-start(bf16[216,128]{1,0:T(8,128)(2,1)S(1)} %get-tuple-element.64), channel_id=1, source_target_pairs={{0,12},{4,0},{8,4},{12,8},{1,13},{5,1},{9,5},{13,9},{2,14},{6,2},{... | collective-permute-start | bytes 165896 | tf_op jit(solution)/shard_map/ppermute | solution.py:531
  60.6 5.1 %collective-permute-start.16 = (bf16[216,128]{1,0:T(8,128)(2,1)S(1)}, bf16[216,128]{1,0:T(8,128)(2,1)S(1)}, u32[]{:S(2)}, u32[]{:S(2)}) collective-permute-start(bf16[216,128]{1,0:T(8,128)(2,1)S(1)} %get-tuple-element.65), channel_id=1, source_target_pairs={{0,8},{4,12},{8,0},{12,4},{1,9},{5,13},{9,1},{13,5},{2,10},{6,14},... | collective-permute-start | bytes 165896 | tf_op jit(solution)/shard_map/ppermute | solution.py:531
  65.8 6.1 %collective-permute-start.17 = (bf16[216,128]{1,0:T(8,128)(2,1)S(1)}, bf16[216,128]{1,0:T(8,128)(2,1)S(1)}, u32[]{:S(2)}, u32[]{:S(2)}) collective-permute-start(bf16[216,128]{1,0:T(8,128)(2,1)S(1)} %get-tuple-element.76), channel_id=1, source_target_pairs={{0,4},{4,8},{8,12},{12,0},{1,5},{5,9},{9,13},{13,1},{2,6},{6,10},{... | collective-permute-start | bytes 165896 | tf_op jit(solution)/shard_map/ppermute | solution.py:531
  65.9 6.0 %collective-permute-start.19 = (bf16[216,128]{1,0:T(8,128)(2,1)S(1)}, bf16[216,128]{1,0:T(8,128)(2,1)S(1)}, u32[]{:S(2)}, u32[]{:S(2)}) collective-permute-start(bf16[216,128]{1,0:T(8,128)(2,1)S(1)} %get-tuple-element.76), channel_id=1, source_target_pairs={{0,12},{4,0},{8,4},{12,8},{1,13},{5,1},{9,5},{13,9},{2,14},{6,2},{... | collective-permute-start | bytes 165896 | tf_op jit(solution)/shard_map/ppermute | solution.py:531
  69.6 5.1 %collective-permute-start.20 = (bf16[216,128]{1,0:T(8,128)(2,1)S(1)}, bf16[216,128]{1,0:T(8,128)(2,1)S(1)}, u32[]{:S(2)}, u32[]{:S(2)}) collective-permute-start(bf16[216,128]{1,0:T(8,128)(2,1)S(1)} %get-tuple-element.76), channel_id=1, source_target_pairs={{0,8},{4,12},{8,0},{12,4},{1,9},{5,13},{9,1},{13,5},{2,10},{6,14},... | collective-permute-start | bytes 165896 | tf_op jit(solution)/shard_map/ppermute | solution.py:531
  71.9 4.5 %collective-permute-start.23 = (f32[872,128]{1,0:T(8,128)S(1)}, f32[872,128]{1,0:T(8,128)S(1)}, u32[]{:S(2)}, u32[]{:S(2)}) collective-permute-start(f32[872,128]{1,0:T(8,128)S(1)} %add.72), channel_id=1, source_target_pairs={{0,1},{1,0},{2,3},{3,2},{4,5},{5,4},{6,7},{7,6},{8,9},{9,8},{10,11... | collective-permute-start | bytes 1339400 | tf_op jit(solution)/shard_map/ppermute | solution.py:531
  74.7 6.0 %collective-permute-start.21 = (bf16[864,128]{1,0:T(8,128)(2,1)S(1)}, bf16[864,128]{1,0:T(8,128)(2,1)S(1)}, u32[]{:S(2)}, u32[]{:S(2)}) collective-permute-start(bf16[864,128]{1,0:T(8,128)(2,1)S(1)} %bitcast.26), channel_id=1, source_target_pairs={{0,2},{2,0},{1,3},{3,1},{4,6},{6,4},{5,7},{7,5},{8,10},{10,8},{9,1... | collective-permute-start | bytes 663560 | tf_op jit(solution)/shard_map/ppermute | solution.py:531
  76.3 4.4 %collective-permute-start.22 = (bf16[864,128]{1,0:T(8,128)(2,1)S(1)}, bf16[864,128]{1,0:T(8,128)(2,1)S(1)}, u32[]{:S(2)}, u32[]{:S(2)}) collective-permute-start(bf16[864,128]{1,0:T(8,128)(2,1)S(1)} %bitcast.27), channel_id=1, source_target_pairs={{0,1},{1,0},{2,3},{3,2},{4,5},{5,4},{6,7},{7,6},{8,9},{9,8},{10,11... | collective-permute-start | bytes 663560 | tf_op jit(solution)/shard_map/ppermute | solution.py:531
  80.7 1.5 %collective-permute-start.24 = (bf16[864,128]{1,0:T(8,128)(2,1)S(1)}, bf16[864,128]{1,0:T(8,128)(2,1)S(1)}, u32[]{:S(2)}, u32[]{:S(2)}) collective-permute-start(bf16[864,128]{1,0:T(8,128)(2,1)S(1)} %collective-permute-done.21.across), channel_id=1, source_target_pairs={{0,1},{1,0},{2,3},{3,2},{4,5},{5,4},{6,7},{7,6},{8,9},{9,8},{10,11... | collective-permute-start | bytes 663560 | tf_op jit(solution)/shard_map/ppermute | solution.py:531

commit v5 on v4

--- a/solution.py
+++ b/solution.py
@@ -99,9 +99,8 @@
         acc[:, 0:outs] = jnp.dot(left, first_taps, preferred_element_type=f32)
         right = jnp.concatenate([window(3, b) for b in range(3)], axis=1)
         acc[:, outs:] = jnp.dot(right, last_taps, preferred_element_type=f32)
-        for b in range(3):
-            both = jnp.concatenate([window(1, b), window(2, b)], axis=1)
-            acc[...] += jnp.dot(both, pairs[b], preferred_element_type=f32)
+        both = jnp.concatenate([window(q, b) for b in range(3) for q in (1, 2)], axis=1)
+        acc[...] += jnp.dot(both, pairs[...].reshape(18 * chans, 2 * outs), preferred_element_type=f32)
         for h in range(rows // 2):
             part = acc[h * 2 * wide : (h + 1) * 2 * wide, :]
             slopes, values = slope_and_activation(part)
@@ -316,8 +315,6 @@
     error = predicted - target
     result[...] = error * feature
     scale = jnp.sum(head * error, axis=0, keepdims=True)
-    for d in range(depth):
-        own[d] = (slopes[d + 1, :, 0:share] * scale[:, 0:share]).astype(bf16)
     shift_ref[...] = jnp.zeros_like(shift_ref)
     rim = jnp.zeros((planes + 2, wide, outs), bf16)
     for e in range(3):
@@ -344,6 +341,8 @@
         out = part if out is None else out + part
     keep = lax.broadcasted_iota(jnp.int32, (planes * cells, chans), 0) % wide < side
     pooled_grad[...] = jnp.where(keep, out, 0.0).reshape(planes, cells, chans)
+    for d in range(depth):
+        own[d] = (slopes[d + 1, :, 0:share] * scale[:, 0:share]).astype(bf16)
 
 
 def run_second_layer(parts, part_kernel, pieces, head, wanted):

time: 83.9 us -> 84 us (level)
  transfers between devices with their start and end apart: 25 -> 25, of which waited for: 11 -> 12; matrix products, arithmetic and copies ran while one was open for 2% -> 2% of each run, Pallas kernels for 10% -> 10%
where the time goes in v5:
time: 84 us; the launch traced here: 83.7 us
  starting transfers between devices  30.7 us (37%)
  waiting for transfers between devices  26.7 us (32%)
  Pallas kernels  20.7 us (25%)
  local copies, waits for them, and re-layouts  4.37 us (5%)
  between operations  1.07 us (1%)
    ppermute x23, waiting for transfers between devices, turn(): return lax.ppermute(x, axis, [(i, (i + step) % size) for i in range(size)])  26.7 us
    ppermute x23, starting transfers between devices, turn(): return lax.ppermute(x, axis, [(i, (i + step) % size) for i in range(size)])  24.4 us
    pallas_call x9, Pallas kernels, call(): pl.pallas_call(body, out_shape=outs, in_specs=specs, out_specs=out_specs,...  20.7 us
    ppermute x1, starting transfers between devices, neighbours(): before = lax.ppermute(last, 'space', up)  4.94 us
    unnamed x12, local copies, waits for them, and re-layouts  2.25 us
  transfers between devices with their start and end apart: 25, of which 12 were waited for; matrix products, arithmetic and copies ran while one was open for 2% of the time, Pallas kernels for 10%

profile of v5, /device:TPU:0, one launch (start us, length us, event | category | flops | bytes accessed | tf_op | source)
XLA Modules:
  0.0 83.7 jit_solution(17553892785953970119)
XLA Ops:
  0.6 1.0 %slice_bitcast_fusion = (bf16[1,24,24,128]{3,2,1,0:T(8,128)(2,1)S(1)}, bf16[1,24,24,128]{3,2,1,0:T(8,128)(2,1)S(1)}) fusion(bf16[1,4,24,24,128]{4,3,2,1,0:T(8,128)(2,1)} %param.5), kind=kLoop, calls=%fused_computation.2 | loop fusion | bytes 589824 | tf_op jit(solution)/shard_map/slice | solution.py:722
  1.6 4.9 %collective-permute-start = (bf16[1,24,24,128]{3,2,1,0:T(8,128)(2,1)S(1)}, bf16[1,24,24,128]{3,2,1,0:T(8,128)(2,1)S(1)}, u32[]{:S(2)}, u32[]{:S(2)}) collective-permute-start(bf16[1,24,24,128]{3,2,1,0:T(8,128)(2,1)S(1)} %get-tuple-element.78), channel_id=1, source_target_pairs={{0,4},{4,8},{8,12},{1,5},{5,9},{9,13},{2,6},{6,10},{10,14},{3,7},{... | collective-permute-start | bytes 442376 | tf_op jit(solution)/shard_map/ppermute | solution.py:708
  6.6 1.3 %collective-permute-start.1 = (bf16[1,24,24,128]{3,2,1,0:T(8,128)(2,1)S(1)}, bf16[1,24,24,128]{3,2,1,0:T(8,128)(2,1)S(1)}, u32[]{:S(2)}, u32[]{:S(2)}) collective-permute-start(bf16[1,24,24,128]{3,2,1,0:T(8,128)(2,1)S(1)} %get-tuple-element.77), channel_id=1, source_target_pairs={{4,0},{8,4},{12,8},{5,1},{9,5},{13,9},{6,2},{10,6},{14,10},{7,3},{... | collective-permute-start | bytes 442376 | tf_op jit(solution)/shard_map/ppermute | solution.py:709
  7.9 0.9 %dynamic-slice_bitcast_fusion = bf16[16,3456]{1,0:T(8,128)(2,1)S(1)} fusion(bf16[3456,64]{0,1:T(8,128)(2,1)} %param.8, s32[]{:T(128)S(6)} %select_n.50), kind=kLoop, calls=%fused_computation.5 | loop fusion | bytes 221188 | tf_op jit(solution)/shard_map/dynamic_slice | solution.py:724
  8.8 2.6 %collective-permute-start.2 = (bf16[16,3456]{1,0:T(8,128)(2,1)S(1)}, bf16[16,3456]{1,0:T(8,128)(2,1)S(1)}, u32[]{:S(2)}, u32[]{:S(2)}) collective-permute-start(bf16[16,3456]{1,0:T(8,128)(2,1)S(1)} %dynamic-slice_bitcast_fusion), channel_id=1, source_target_pairs={{0,4},{4,8},{8,12},{12,0},{1,5},{5,9},{9,13},{13,1},{2,6},{6,10},{... | collective-permute-start | bytes 331784 | tf_op jit(solution)/shard_map/ppermute | solution.py:530
  11.5 2.6 %collective-permute-start.3 = (bf16[16,3456]{1,0:T(8,128)(2,1)S(1)}, bf16[16,3456]{1,0:T(8,128)(2,1)S(1)}, u32[]{:S(2)}, u32[]{:S(2)}) collective-permute-start(bf16[16,3456]{1,0:T(8,128)(2,1)S(1)} %dynamic-slice_bitcast_fusion), channel_id=1, source_target_pairs={{0,8},{4,12},{8,0},{12,4},{1,9},{5,13},{9,1},{13,5},{2,10},{6,14},... | collective-permute-start | bytes 331784 | tf_op jit(solution)/shard_map/ppermute | solution.py:530
  14.0 1.3 %collective-permute-start.4 = (bf16[16,3456]{1,0:T(8,128)(2,1)S(1)}, bf16[16,3456]{1,0:T(8,128)(2,1)S(1)}, u32[]{:S(2)}, u32[]{:S(2)}) collective-permute-start(bf16[16,3456]{1,0:T(8,128)(2,1)S(1)} %dynamic-slice_bitcast_fusion), channel_id=1, source_target_pairs={{0,12},{4,0},{8,4},{12,8},{1,13},{5,1},{9,5},{13,9},{2,14},{6,2},{... | collective-permute-start | bytes 331784 | tf_op jit(solution)/shard_map/ppermute | solution.py:530
  15.4 0.0 collective-permute-done.before
  15.4 0.0 collective-permute-done.1.after
  15.4 1.1 %copy-done = bf16[1,4,24,24,128]{4,3,2,1,0:T(8,128)(2,1)S(1)} copy-done((bf16[1,4,24,24,128]{4,3,2,1,0:T(8,128)(2,1)S(1)}, bf16[1,4,24,24,128]{4,3,2,1,0:T(8,128)(2,1)}, u32[]{:S(2)}) %copy-start) | copy-done | bytes 589848
  16.5 1.2 %copy-done.3 = bf16[3456,128]{1,0:T(8,128)(2,1)S(1)} copy-done((bf16[3456,128]{1,0:T(8,128)(2,1)S(1)}, bf16[3456,128]{1,0:T(8,128)(2,1)}, u32[]{:S(2)}) %copy-start.3) | copy-done | bytes 884760
  17.6 5.1 %shard_map.76 = (bf16[2,144,128]{2,1,0:T(8,128)(2,1)S(1)}, f32[4,768,128]{2,1,0:T(8,128)S(1)}) custom-call(bf16[4,24,24,128]{3,2,1,0:T(8,128)(2,1)S(1)} %bitcast.29, bf16[1,24,24,128]{3,2,1,0:T(8,128)(2,1)S(1)} %collective-permute-done.before, bf16[1,24,24,128]{3,2,1,0:T(8,128)(2,1)S(1)} %collective-permute-done.1.after, bf16[3456,128]{1,0:T(8,128)(2,1)S(1)} %copy-done.3), custom_call_target="tpu_custom_call" | custom-call | flops 8000000000 | tf_op jit(solution)/shard_map/pallas_call | solution.py:24
  22.7 0.0 collective-permute-done.2.r0
  22.7 0.1 collective-permute-done.3.r1
  22.8 1.6 %collective-permute-start.5 = (bf16[48,3456]{1,0:T(8,128)(2,1)S(1)}, bf16[48,3456]{1,0:T(8,128)(2,1)S(1)}, u32[]{:S(2)}, u32[]{:S(2)}) collective-permute-start(bf16[48,3456]{1,0:T(8,128)(2,1)S(1)} %shard_map.77.w1), channel_id=1, source_target_pairs={{0,2},{2,0},{1,3},{3,1},{4,6},{6,4},{5,7},{7,5},{8,10},{10,8},{9,1... | collective-permute-start | bytes 995336 | tf_op jit(solution)/shard_map/ppermute | solution.py:530
  24.4 2.1 %collective-permute-start.6 = (bf16[2,144,128]{2,1,0:T(8,128)(2,1)S(1)}, bf16[2,144,128]{2,1,0:T(8,128)(2,1)S(1)}, u32[]{:S(2)}, u32[]{:S(2)}) collective-permute-start(bf16[2,144,128]{2,1,0:T(8,128)(2,1)S(1)} %get-tuple-element.44.p0), channel_id=1, source_target_pairs={{0,4},{4,8},{8,12},{12,0},{1,5},{5,9},{9,13},{13,1},{2,6},{6,10},{... | collective-permute-start | bytes 221192 | tf_op jit(solution)/shard_map/ppermute | solution.py:530
  26.5 0.4 collective-permute-start.7
  26.9 2.8 %collective-permute-start.8 = (bf16[2,144,128]{2,1,0:T(8,128)(2,1)S(1)}, bf16[2,144,128]{2,1,0:T(8,128)(2,1)S(1)}, u32[]{:S(2)}, u32[]{:S(2)}) collective-permute-start(bf16[2,144,128]{2,1,0:T(8,128)(2,1)S(1)} %get-tuple-element.44.p0), channel_id=1, source_target_pairs={{0,12},{4,0},{8,4},{12,8},{1,13},{5,1},{9,5},{13,9},{2,14},{6,2},{... | collective-permute-start | bytes 221192 | tf_op jit(solution)/shard_map/ppermute | solution.py:530
  29.7 1.6 %collective-permute-done.6.p1 = bf16[2,144,128]{2,1,0:T(8,128)(2,1)S(1)} collective-permute-done((bf16[2,144,128]{2,1,0:T(8,128)(2,1)S(1)}, bf16[2,144,128]{2,1,0:T(8,128)(2,1)S(1)}, u32[]{:S(2)}, u32[]{:S(2)}) %collective-permute-start.6) | collective-permute-done | bytes 73760 | tf_op jit(solution)/shard_map/ppermute | solution.py:530
  31.3 1.7 %collective-permute-done.7.p2 = bf16[2,144,128]{2,1,0:T(8,128)(2,1)S(1)} collective-permute-done((bf16[2,144,128]{2,1,0:T(8,128)(2,1)S(1)}, bf16[2,144,128]{2,1,0:T(8,128)(2,1)S(1)}, u32[]{:S(2)}, u32[]{:S(2)}) %collective-permute-start.7) | collective-permute-done | bytes 73760 | tf_op jit(solution)/shard_map/ppermute | solution.py:530
  33.1 1.6 %collective-permute-done.10.w4 = bf16[48,3456]{1,0:T(8,128)(2,1)S(1)} collective-permute-done((bf16[48,3456]{1,0:T(8,128)(2,1)S(1)}, bf16[48,3456]{1,0:T(8,128)(2,1)S(1)}, u32[]{:S(2)}, u32[]{:S(2)}) %collective-permute-start.10) | collective-permute-done | bytes 331808 | tf_op jit(solution)/shard_map/ppermute | solution.py:530
  34.7 0.0 copy-start.1
  34.7 7.1 %shard_map.78 = (f32[2,192,128]{2,1,0:T(8,128)S(1)}, bf16[8,192,64]{2,1,0:T(8,128)(2,1)S(1)}, f32[4,256]{1,0:T(4,128)S(1)}) custom-call(bf16[2,144,128]{2,1,0:T(8,128)(2,1)S(1)} %get-tuple-element.44.p0, bf16[2,144,128]{2,1,0:T(8,128)(2,1)S(1)} %collective-permute-done.6.p1, bf16[2,144,128]{2,1,0:T(8,128)(2,1)S(1)} %collective-permute-done.7.p2, ...), custom_call_target="tpu_custom_call" | custom-call | flops 8000000000 | tf_op jit(solution)/shard_map/pallas_call | solution.py:24
  41.8 4.1 %shard_map.79 = (f32[1728,128]{1,0:T(8,128)S(1)}, f32[1728,128]{1,0:T(8,128)S(1)}) custom-call(bf16[4,24,24,128]{3,2,1,0:T(8,128)(2,1)S(1)} %bitcast.30, bf16[1,24,24,128]{3,2,1,0:T(8,128)(2,1)S(1)} %collective-permute-done.before, bf16[1,24,24,128]{3,2,1,0:T(8,128)(2,1)S(1)} %collective-permute-done.1.after, f32[2,192,128]{2,1,0:T(8,128)S(1)} %get-tuple-element.49.spread, ...), custom_call_target="tpu_custom_call" | custom-call | flops 7000000000 | tf_op jit(solution)/shard_map/pallas_call | solution.py:24
  45.9 0.2 collective-permute-start.11
  46.1 2.1 %shard_map.82 = (f32[872,128]{1,0:T(8,128)S(1)}, f32[872,128]{1,0:T(8,128)S(1)}) custom-call(bf16[2,144,128]{2,1,0:T(8,128)(2,1)S(1)} %get-tuple-element.44.p0, bf16[2,144,128]{2,1,0:T(8,128)(2,1)S(1)} %collective-permute-done.6.p1, bf16[2,144,128]{2,1,0:T(8,128)(2,1)S(1)} %collective-permute-done.7.p2, bf16[2,144,128]{2,1,0:T(8,128)(2,1)S(1)} %collective-permute-done.8.p3, ...), custom_call_target="tpu_custom_call" | custom-call | flops 4000000000 | tf_op jit(solution)/shard_map/pallas_call | solution.py:24
  48.2 0.4 collective-permute-start.13
  48.6 0.1 shard_map.80
  48.7 0.6 collective-permute-start.12
  49.3 0.7 collective-permute-done.13
  50.1 6.1 %collective-permute-done.12.came = bf16[864,128]{1,0:T(8,128)(2,1)S(1)} collective-permute-done((bf16[864,128]{1,0:T(8,128)(2,1)S(1)}, bf16[864,128]{1,0:T(8,128)(2,1)S(1)}, u32[]{:S(2)}, u32[]{:S(2)}) %collective-permute-start.12) | collective-permute-done | bytes 221216 | tf_op jit(solution)/shard_map/ppermute | solution.py:530
  56.3 0.6 collective-permute-start.18
  56.9 1.8 %collective-permute-start.14 = (bf16[216,128]{1,0:T(8,128)(2,1)S(1)}, bf16[216,128]{1,0:T(8,128)(2,1)S(1)}, u32[]{:S(2)}, u32[]{:S(2)}) collective-permute-start(bf16[216,128]{1,0:T(8,128)(2,1)S(1)} %get-tuple-element.63), channel_id=1, source_target_pairs={{0,4},{4,8},{8,12},{12,0},{1,5},{5,9},{9,13},{13,1},{2,6},{6,10},{... | collective-permute-start | bytes 165896 | tf_op jit(solution)/shard_map/ppermute | solution.py:530
  58.7 2.0 %collective-permute-start.15 = (bf16[216,128]{1,0:T(8,128)(2,1)S(1)}, bf16[216,128]{1,0:T(8,128)(2,1)S(1)}, u32[]{:S(2)}, u32[]{:S(2)}) collective-permute-start(bf16[216,128]{1,0:T(8,128)(2,1)S(1)} %get-tuple-element.64), channel_id=1, source_target_pairs={{0,12},{4,0},{8,4},{12,8},{1,13},{5,1},{9,5},{13,9},{2,14},{6,2},{... | collective-permute-start | bytes 165896 | tf_op jit(solution)/shard_map/ppermute | solution.py:530
  60.7 2.7 %collective-permute-done.14 = bf16[216,128]{1,0:T(8,128)(2,1)S(1)} collective-permute-done((bf16[216,128]{1,0:T(8,128)(2,1)S(1)}, bf16[216,128]{1,0:T(8,128)(2,1)S(1)}, u32[]{:S(2)}, u32[]{:S(2)}) %collective-permute-start.14) | collective-permute-done | bytes 55328 | tf_op jit(solution)/shard_map/ppermute | solution.py:530
  63.4 2.4 %collective-permute-done.16 = bf16[216,128]{1,0:T(8,128)(2,1)S(1)} collective-permute-done((bf16[216,128]{1,0:T(8,128)(2,1)S(1)}, bf16[216,128]{1,0:T(8,128)(2,1)S(1)}, u32[]{:S(2)}, u32[]{:S(2)}) %collective-permute-start.16) | collective-permute-done | bytes 55328 | tf_op jit(solution)/shard_map/ppermute | solution.py:530
  65.8 0.1 bitcast_dynamic-update-slice_fusion.5
  65.9 0.1 collective-permute-start.17
  66.0 3.7 %collective-permute-start.19 = (bf16[216,128]{1,0:T(8,128)(2,1)S(1)}, bf16[216,128]{1,0:T(8,128)(2,1)S(1)}, u32[]{:S(2)}, u32[]{:S(2)}) collective-permute-start(bf16[216,128]{1,0:T(8,128)(2,1)S(1)} %get-tuple-element.76), channel_id=1, source_target_pairs={{0,12},{4,0},{8,4},{12,8},{1,13},{5,1},{9,5},{13,9},{2,14},{6,2},{... | collective-permute-start | bytes 165896 | tf_op jit(solution)/shard_map/ppermute | solution.py:530
  69.7 0.1 add.72
  69.8 2.2 %collective-permute-done.17 = bf16[216,128]{1,0:T(8,128)(2,1)S(1)} collective-permute-done((bf16[216,128]{1,0:T(8,128)(2,1)S(1)}, bf16[216,128]{1,0:T(8,128)(2,1)S(1)}, u32[]{:S(2)}, u32[]{:S(2)}) %collective-permute-start.17) | collective-permute-done | bytes 55328 | tf_op jit(solution)/shard_map/ppermute | solution.py:530
  72.0 2.8 %collective-permute-done.20 = bf16[216,128]{1,0:T(8,128)(2,1)S(1)} collective-permute-done((bf16[216,128]{1,0:T(8,128)(2,1)S(1)}, bf16[216,128]{1,0:T(8,128)(2,1)S(1)}, u32[]{:S(2)}, u32[]{:S(2)}) %collective-permute-start.20) | collective-permute-done | bytes 55328 | tf_op jit(solution)/shard_map/ppermute | solution.py:530
  74.8 1.6 %collective-permute-start.21 = (bf16[864,128]{1,0:T(8,128)(2,1)S(1)}, bf16[864,128]{1,0:T(8,128)(2,1)S(1)}, u32[]{:S(2)}, u32[]{:S(2)}) collective-permute-start(bf16[864,128]{1,0:T(8,128)(2,1)S(1)} %bitcast.26), channel_id=1, source_target_pairs={{0,2},{2,0},{1,3},{3,1},{4,6},{6,4},{5,7},{7,5},{8,10},{10,8},{9,1... | collective-permute-start | bytes 663560 | tf_op jit(solution)/shard_map/ppermute | solution.py:530
  76.4 0.1 broadcast_in_dim.31
  76.5 1.0 %shard_map.83 = (f32[64,3456]{1,0:T(8,128)}, f32[4,64]{1,0:T(4,128)}) custom-call(f32[1744,128]{1,0:T(8,128)S(1)} %bitcast.25), custom_call_target="tpu_custom_call" | custom-call | flops 2000000000 | tf_op jit(solution)/shard_map/pallas_call | solution.py:24
  77.5 3.3 %collective-permute-done.21.across = bf16[864,128]{1,0:T(8,128)(2,1)S(1)} collective-permute-done((bf16[864,128]{1,0:T(8,128)(2,1)S(1)}, bf16[864,128]{1,0:T(8,128)(2,1)S(1)}, u32[]{:S(2)}, u32[]{:S(2)}) %collective-permute-start.21) | collective-permute-done | bytes 221216 | tf_op jit(solution)/shard_map/ppermute | solution.py:530
  80.8 1.5 %collective-permute-done.24.far = bf16[864,128]{1,0:T(8,128)(2,1)S(1)} collective-permute-done((bf16[864,128]{1,0:T(8,128)(2,1)S(1)}, bf16[864,128]{1,0:T(8,128)(2,1)S(1)}, u32[]{:S(2)}, u32[]{:S(2)}) %collective-permute-start.24) | collective-permute-done | bytes 221216 | tf_op jit(solution)/shard_map/ppermute | solution.py:530
  82.3 1.3 %shard_map.84 = f32[3456,128]{1,0:T(8,128)} custom-call(bf16[864,128]{1,0:T(8,128)(2,1)S(1)} %bitcast.28, bf16[864,128]{1,0:T(8,128)(2,1)S(1)} %collective-permute-done.21.across, bf16[864,128]{1,0:T(8,128)(2,1)S(1)} %collective-permute-done.22.near, bf16[864,128]{1,0:T(8,128)(2,1)S(1)} %collective-permute-done.24.far), custom_call_target="tpu_custom_call" | custom-call | tf_op jit(solution)/shard_map/pallas_call | solution.py:24
  (35 shorter events, 0.3 us)
Async XLA Ops:
  1.6 13.7 %collective-permute-start = (bf16[1,24,24,128]{3,2,1,0:T(8,128)(2,1)S(1)}, bf16[1,24,24,128]{3,2,1,0:T(8,128)(2,1)S(1)}, u32[]{:S(2)}, u32[]{:S(2)}) collective-permute-start(bf16[1,24,24,128]{3,2,1,0:T(8,128)(2,1)S(1)} %get-tuple-element.78), channel_id=1, source_target_pairs={{0,4},{4,8},{8,12},{1,5},{5,9},{9,13},{2,6},{6,10},{10,14},{3,7},{... | collective-permute-start | bytes 442376 | tf_op jit(solution)/shard_map/ppermute | solution.py:708
  6.6 8.8 %collective-permute-start.1 = (bf16[1,24,24,128]{3,2,1,0:T(8,128)(2,1)S(1)}, bf16[1,24,24,128]{3,2,1,0:T(8,128)(2,1)S(1)}, u32[]{:S(2)}, u32[]{:S(2)}) collective-permute-start(bf16[1,24,24,128]{3,2,1,0:T(8,128)(2,1)S(1)} %get-tuple-element.77), channel_id=1, source_target_pairs={{4,0},{8,4},{12,8},{5,1},{9,5},{13,9},{6,2},{10,6},{14,10},{7,3},{... | collective-permute-start | bytes 442376 | tf_op jit(solution)/shard_map/ppermute | solution.py:709
  8.8 13.9 %collective-permute-start.2 = (bf16[16,3456]{1,0:T(8,128)(2,1)S(1)}, bf16[16,3456]{1,0:T(8,128)(2,1)S(1)}, u32[]{:S(2)}, u32[]{:S(2)}) collective-permute-start(bf16[16,3456]{1,0:T(8,128)(2,1)S(1)} %dynamic-slice_bitcast_fusion), channel_id=1, source_target_pairs={{0,4},{4,8},{8,12},{12,0},{1,5},{5,9},{9,13},{13,1},{2,6},{6,10},{... | collective-permute-start | bytes 331784 | tf_op jit(solution)/shard_map/ppermute | solution.py:530
  11.5 11.3 %collective-permute-start.3 = (bf16[16,3456]{1,0:T(8,128)(2,1)S(1)}, bf16[16,3456]{1,0:T(8,128)(2,1)S(1)}, u32[]{:S(2)}, u32[]{:S(2)}) collective-permute-start(bf16[16,3456]{1,0:T(8,128)(2,1)S(1)} %dynamic-slice_bitcast_fusion), channel_id=1, source_target_pairs={{0,8},{4,12},{8,0},{12,4},{1,9},{5,13},{9,1},{13,5},{2,10},{6,14},... | collective-permute-start | bytes 331784 | tf_op jit(solution)/shard_map/ppermute | solution.py:530
  14.0 8.8 %collective-permute-start.4 = (bf16[16,3456]{1,0:T(8,128)(2,1)S(1)}, bf16[16,3456]{1,0:T(8,128)(2,1)S(1)}, u32[]{:S(2)}, u32[]{:S(2)}) collective-permute-start(bf16[16,3456]{1,0:T(8,128)(2,1)S(1)} %dynamic-slice_bitcast_fusion), channel_id=1, source_target_pairs={{0,12},{4,0},{8,4},{12,8},{1,13},{5,1},{9,5},{13,9},{2,14},{6,2},{... | collective-permute-start | bytes 331784 | tf_op jit(solution)/shard_map/ppermute | solution.py:530
  15.4 1.1 %copy-start = (bf16[1,4,24,24,128]{4,3,2,1,0:T(8,128)(2,1)S(1)}, bf16[1,4,24,24,128]{4,3,2,1,0:T(8,128)(2,1)}, u32[]{:S(2)}) copy-start(bf16[1,4,24,24,128]{4,3,2,1,0:T(8,128)(2,1)} %param.5) | copy-start | bytes 1769476
  16.5 1.2 %copy-start.3 = (bf16[3456,128]{1,0:T(8,128)(2,1)S(1)}, bf16[3456,128]{1,0:T(8,128)(2,1)}, u32[]{:S(2)}) copy-start(bf16[3456,128]{1,0:T(8,128)(2,1)} %kernel.1) | copy-start | bytes 2654212
  17.6 17.1 %copy-start.2 = (bf16[3456,64]{0,1:T(8,128)(2,1)S(1)}, bf16[3456,64]{0,1:T(8,128)(2,1)}, u32[]{:S(2)}) copy-start(bf16[3456,64]{0,1:T(8,128)(2,1)} %param.8) | copy-start | bytes 1327108
  17.6 17.1 %copy-start.4 = (f32[256,4]{0,1:T(4,128)S(1)}, f32[256,4]{0,1:T(4,128)}, u32[]{:S(2)}) copy-start(f32[256,4]{0,1:T(4,128)} %param.9) | copy-start | bytes 12292
  17.6 17.1 %copy-start.5 = (f32[1,4]{1,0:T(1,128)S(1)}, f32[1,4]{1,0:T(1,128)}, u32[]{:S(2)}) copy-start(f32[1,4]{1,0:T(1,128)} %wanted.1) | copy-start | bytes 52
  22.8 10.2 %collective-permute-start.5 = (bf16[48,3456]{1,0:T(8,128)(2,1)S(1)}, bf16[48,3456]{1,0:T(8,128)(2,1)S(1)}, u32[]{:S(2)}, u32[]{:S(2)}) collective-permute-start(bf16[48,3456]{1,0:T(8,128)(2,1)S(1)} %shard_map.77.w1), channel_id=1, source_target_pairs={{0,2},{2,0},{1,3},{3,1},{4,6},{6,4},{5,7},{7,5},{8,10},{10,8},{9,1... | collective-permute-start | bytes 995336 | tf_op jit(solution)/shard_map/ppermute | solution.py:530
  24.4 7.0 %collective-permute-start.6 = (bf16[2,144,128]{2,1,0:T(8,128)(2,1)S(1)}, bf16[2,144,128]{2,1,0:T(8,128)(2,1)S(1)}, u32[]{:S(2)}, u32[]{:S(2)}) collective-permute-start(bf16[2,144,128]{2,1,0:T(8,128)(2,1)S(1)} %get-tuple-element.44.p0), channel_id=1, source_target_pairs={{0,4},{4,8},{8,12},{12,0},{1,5},{5,9},{9,13},{13,1},{2,6},{6,10},{... | collective-permute-start | bytes 221192 | tf_op jit(solution)/shard_map/ppermute | solution.py:530
  26.5 6.6 %collective-permute-start.7 = (bf16[2,144,128]{2,1,0:T(8,128)(2,1)S(1)}, bf16[2,144,128]{2,1,0:T(8,128)(2,1)S(1)}, u32[]{:S(2)}, u32[]{:S(2)}) collective-permute-start(bf16[2,144,128]{2,1,0:T(8,128)(2,1)S(1)} %get-tuple-element.44.p0), channel_id=1, source_target_pairs={{0,8},{4,12},{8,0},{12,4},{1,9},{5,13},{9,1},{13,5},{2,10},{6,14},... | collective-permute-start | bytes 221192 | tf_op jit(solution)/shard_map/ppermute | solution.py:530
  26.9 6.2 %collective-permute-start.8 = (bf16[2,144,128]{2,1,0:T(8,128)(2,1)S(1)}, bf16[2,144,128]{2,1,0:T(8,128)(2,1)S(1)}, u32[]{:S(2)}, u32[]{:S(2)}) collective-permute-start(bf16[2,144,128]{2,1,0:T(8,128)(2,1)S(1)} %get-tuple-element.44.p0), channel_id=1, source_target_pairs={{0,12},{4,0},{8,4},{12,8},{1,13},{5,1},{9,5},{13,9},{2,14},{6,2},{... | collective-permute-start | bytes 221192 | tf_op jit(solution)/shard_map/ppermute | solution.py:530
  29.7 3.4 %collective-permute-start.9 = (bf16[48,3456]{1,0:T(8,128)(2,1)S(1)}, bf16[48,3456]{1,0:T(8,128)(2,1)S(1)}, u32[]{:S(2)}, u32[]{:S(2)}) collective-permute-start(bf16[48,3456]{1,0:T(8,128)(2,1)S(1)} %shard_map.77.w1), channel_id=1, source_target_pairs={{0,1},{1,0},{2,3},{3,2},{4,5},{5,4},{6,7},{7,6},{8,9},{9,8},{10,11... | collective-permute-start | bytes 995336 | tf_op jit(solution)/shard_map/ppermute | solution.py:530
  33.1 1.6 %collective-permute-start.10 = (bf16[48,3456]{1,0:T(8,128)(2,1)S(1)}, bf16[48,3456]{1,0:T(8,128)(2,1)S(1)}, u32[]{:S(2)}, u32[]{:S(2)}) collective-permute-start(bf16[48,3456]{1,0:T(8,128)(2,1)S(1)} %collective-permute-done.5.w3), channel_id=1, source_target_pairs={{0,1},{1,0},{2,3},{3,2},{4,5},{5,4},{6,7},{7,6},{8,9},{9,8},{10,11... | collective-permute-start | bytes 995336 | tf_op jit(solution)/shard_map/ppermute | solution.py:530
  34.7 7.1 %copy-start.1 = (bf16[1,4,24,24,128]{4,3,2,1,0:T(8,128)(2,1)S(1)}, bf16[1,4,24,24,128]{4,3,2,1,0:T(8,128)(2,1)}, u32[]{:S(2)}) copy-start(bf16[1,4,24,24,128]{4,3,2,1,0:T(8,128)(2,1)} %param.5) | copy-start | bytes 1769476
  45.9 2.7 %collective-permute-start.11 = (f32[1728,128]{1,0:T(8,128)S(1)}, f32[1728,128]{1,0:T(8,128)S(1)}, u32[]{:S(2)}, u32[]{:S(2)}) collective-permute-start(f32[1728,128]{1,0:T(8,128)S(1)} %get-tuple-element.52), channel_id=1, source_target_pairs={{0,1},{1,0},{2,3},{3,2},{4,5},{5,4},{6,7},{7,6},{8,9},{9,8},{10,11... | collective-permute-start | bytes 2654216 | tf_op jit(solution)/shard_map/ppermute | solution.py:530
  48.2 1.9 %collective-permute-start.13 = (f32[872,128]{1,0:T(8,128)S(1)}, f32[872,128]{1,0:T(8,128)S(1)}, u32[]{:S(2)}, u32[]{:S(2)}) collective-permute-start(f32[872,128]{1,0:T(8,128)S(1)} %get-tuple-element.62), channel_id=1, source_target_pairs={{0,1},{1,0},{2,3},{3,2},{4,5},{5,4},{6,7},{7,6},{8,9},{9,8},{10,11... | collective-permute-start | bytes 1339400 | tf_op jit(solution)/shard_map/ppermute | solution.py:530
  48.7 7.5 %collective-permute-start.12 = (bf16[864,128]{1,0:T(8,128)(2,1)S(1)}, bf16[864,128]{1,0:T(8,128)(2,1)S(1)}, u32[]{:S(2)}, u32[]{:S(2)}) collective-permute-start(bf16[864,128]{1,0:T(8,128)(2,1)S(1)} %get-tuple-element.54), channel_id=1, source_target_pairs={{0,2},{2,0},{1,3},{3,1},{4,6},{6,4},{5,7},{7,5},{8,10},{10,8},{9,1... | collective-permute-start | bytes 663560 | tf_op jit(solution)/shard_map/ppermute | solution.py:530
  56.3 13.5 %collective-permute-start.18 = (f32[872,128]{1,0:T(8,128)S(1)}, f32[872,128]{1,0:T(8,128)S(1)}, u32[]{:S(2)}, u32[]{:S(2)}) collective-permute-start(f32[872,128]{1,0:T(8,128)S(1)} %add.66), channel_id=1, source_target_pairs={{0,2},{2,0},{1,3},{3,1},{4,6},{6,4},{5,7},{7,5},{8,10},{10,8},{9,1... | collective-permute-start | bytes 1339400 | tf_op jit(solution)/shard_map/ppermute | solution.py:530
  56.9 6.5 %collective-permute-start.14 = (bf16[216,128]{1,0:T(8,128)(2,1)S(1)}, bf16[216,128]{1,0:T(8,128)(2,1)S(1)}, u32[]{:S(2)}, u32[]{:S(2)}) collective-permute-start(bf16[216,128]{1,0:T(8,128)(2,1)S(1)} %get-tuple-element.63), channel_id=1, source_target_pairs={{0,4},{4,8},{8,12},{12,0},{1,5},{5,9},{9,13},{13,1},{2,6},{6,10},{... | collective-permute-start | bytes 165896 | tf_op jit(solution)/shard_map/ppermute | solution.py:530
  58.7 4.8 %collective-permute-start.15 = (bf16[216,128]{1,0:T(8,128)(2,1)S(1)}, bf16[216,128]{1,0:T(8,128)(2,1)S(1)}, u32[]{:S(2)}, u32[]{:S(2)}) collective-permute-start(bf16[216,128]{1,0:T(8,128)(2,1)S(1)} %get-tuple-element.64), channel_id=1, source_target_pairs={{0,12},{4,0},{8,4},{12,8},{1,13},{5,1},{9,5},{13,9},{2,14},{6,2},{... | collective-permute-start | bytes 165896 | tf_op jit(solution)/shard_map/ppermute | solution.py:530
  60.7 5.1 %collective-permute-start.16 = (bf16[216,128]{1,0:T(8,128)(2,1)S(1)}, bf16[216,128]{1,0:T(8,128)(2,1)S(1)}, u32[]{:S(2)}, u32[]{:S(2)}) collective-permute-start(bf16[216,128]{1,0:T(8,128)(2,1)S(1)} %get-tuple-element.65), channel_id=1, source_target_pairs={{0,8},{4,12},{8,0},{12,4},{1,9},{5,13},{9,1},{13,5},{2,10},{6,14},... | collective-permute-start | bytes 165896 | tf_op jit(solution)/shard_map/ppermute | solution.py:530
  65.9 6.1 %collective-permute-start.17 = (bf16[216,128]{1,0:T(8,128)(2,1)S(1)}, bf16[216,128]{1,0:T(8,128)(2,1)S(1)}, u32[]{:S(2)}, u32[]{:S(2)}) collective-permute-start(bf16[216,128]{1,0:T(8,128)(2,1)S(1)} %get-tuple-element.76), channel_id=1, source_target_pairs={{0,4},{4,8},{8,12},{12,0},{1,5},{5,9},{9,13},{13,1},{2,6},{6,10},{... | collective-permute-start | bytes 165896 | tf_op jit(solution)/shard_map/ppermute | solution.py:530
  66.0 6.0 %collective-permute-start.19 = (bf16[216,128]{1,0:T(8,128)(2,1)S(1)}, bf16[216,128]{1,0:T(8,128)(2,1)S(1)}, u32[]{:S(2)}, u32[]{:S(2)}) collective-permute-start(bf16[216,128]{1,0:T(8,128)(2,1)S(1)} %get-tuple-element.76), channel_id=1, source_target_pairs={{0,12},{4,0},{8,4},{12,8},{1,13},{5,1},{9,5},{13,9},{2,14},{6,2},{... | collective-permute-start | bytes 165896 | tf_op jit(solution)/shard_map/ppermute | solution.py:530
  69.7 5.1 %collective-permute-start.20 = (bf16[216,128]{1,0:T(8,128)(2,1)S(1)}, bf16[216,128]{1,0:T(8,128)(2,1)S(1)}, u32[]{:S(2)}, u32[]{:S(2)}) collective-permute-start(bf16[216,128]{1,0:T(8,128)(2,1)S(1)} %get-tuple-element.76), channel_id=1, source_target_pairs={{0,8},{4,12},{8,0},{12,4},{1,9},{5,13},{9,1},{13,5},{2,10},{6,14},... | collective-permute-start | bytes 165896 | tf_op jit(solution)/shard_map/ppermute | solution.py:530
  72.0 4.5 %collective-permute-start.23 = (f32[872,128]{1,0:T(8,128)S(1)}, f32[872,128]{1,0:T(8,128)S(1)}, u32[]{:S(2)}, u32[]{:S(2)}) collective-permute-start(f32[872,128]{1,0:T(8,128)S(1)} %add.72), channel_id=1, source_target_pairs={{0,1},{1,0},{2,3},{3,2},{4,5},{5,4},{6,7},{7,6},{8,9},{9,8},{10,11... | collective-permute-start | bytes 1339400 | tf_op jit(solution)/shard_map/ppermute | solution.py:530
  74.8 6.0 %collective-permute-start.21 = (bf16[864,128]{1,0:T(8,128)(2,1)S(1)}, bf16[864,128]{1,0:T(8,128)(2,1)S(1)}, u32[]{:S(2)}, u32[]{:S(2)}) collective-permute-start(bf16[864,128]{1,0:T(8,128)(2,1)S(1)} %bitcast.26), channel_id=1, source_target_pairs={{0,2},{2,0},{1,3},{3,1},{4,6},{6,4},{5,7},{7,5},{8,10},{10,8},{9,1... | collective-permute-start | bytes 663560 | tf_op jit(solution)/shard_map/ppermute | solution.py:530
  76.4 4.4 %collective-permute-start.22 = (bf16[864,128]{1,0:T(8,128)(2,1)S(1)}, bf16[864,128]{1,0:T(8,128)(2,1)S(1)}, u32[]{:S(2)}, u32[]{:S(2)}) collective-permute-start(bf16[864,128]{1,0:T(8,128)(2,1)S(1)} %bitcast.27), channel_id=1, source_target_pairs={{0,1},{1,0},{2,3},{3,2},{4,5},{5,4},{6,7},{7,6},{8,9},{9,8},{10,11... | collective-permute-start | bytes 663560 | tf_op jit(solution)/shard_map/ppermute | solution.py:530
  80.8 1.5 %collective-permute-start.24 = (bf16[864,128]{1,0:T(8,128)(2,1)S(1)}, bf16[864,128]{1,0:T(8,128)(2,1)S(1)}, u32[]{:S(2)}, u32[]{:S(2)}) collective-permute-start(bf16[864,128]{1,0:T(8,128)(2,1)S(1)} %collective-permute-done.21.across), channel_id=1, source_target_pairs={{0,1},{1,0},{2,3},{3,2},{4,5},{5,4},{6,7},{7,6},{8,9},{9,8},{10,11... | collective-permute-start | bytes 663560 | tf_op jit(solution)/shard_map/ppermute | solution.py:530
